TPU v7x, 32 devices: a whole 2x2x4 slice. The times are simulated.
32 devices in a mesh: ens: 2 (over y), lat: 4 (over z), lon: 4 (over x, core).
Axes of the slice: x: 2, y: 2, z: 4, core: 2. Of those that a mesh axis runs over, the one named last changes fastest.
Arguments:
- sample_quantities: bfloat16 [2, 24, 256, 512], P('ens', None, 'lat', 'lon'), may hold values from -6 to 6
- conv_weight: bfloat16 [216, 256], replicated, may hold values from -0.4375 to 0.4375
- conv_bias: float32 [256], replicated, may hold values from -3 to 3
- out_weight: bfloat16 [256, 24], replicated, may hold values from -0.375 to 0.375
- obs_index: int32 [4, 4, 256], P('lat', 'lon'), may hold values from 0 to 196607
- obs_count: int32 [4, 4], P('lat', 'lon'), may hold values from 85 to 256, as said below
- obs_value: float32 [4, 4, 256], P('lat', 'lon'), may hold values from -8 to 8
- obs_weight: float32 [4, 4, 256], P('lat', 'lon'), may hold values from 0.002 to 0.03
Outputs:
- updated_estimates: bfloat16 [2, 24, 256, 512], P('ens', None, 'lat', 'lon')
Inputs may be any that keep to these rules, and one draw needn't show every extreme that they name: `obs_index`: flat index v * 64 * 128 + r * 128 + c into the own shard's block; slots at or past the shard's count are unused. `obs_count`: some shard has exactly 256 live slots.
All inputs are finite; a program needn't handle non-finite values.
Results may differ from a plain program's by a relative error of at most 0.0075.
Values may be sent and summed in bfloat16 or wider, within the bound.
No kernel may reach another device: no remote copies, remote signals or barrier semaphores. Data moves between devices by JAX's collectives and lax.ppermute only.
A program may use at most 64 MiB of HBM per device.

v0:
```python
import math

import jax
import jax.numpy as jnp
from jax import lax
from jax.sharding import PartitionSpec as P

NS_ITERS = 20


def extended(shard, sides, width, wrap):
    for axis, dim in sides:
        size, length = (lax.axis_size(axis), shard.shape[dim])
        up = [(i, (i + 1) % size) for i in range(size if wrap else size - 1)]
        down = [(j, i) for i, j in up]
        last = lax.slice_in_dim(shard, length - width, length, axis=dim)
        leading = lax.slice_in_dim(shard, 0, width, axis=dim)
        before = lax.ppermute(last, axis, up)
        after = lax.ppermute(leading, axis, down)
        shard = jnp.concatenate([before, shard, after], axis=dim)
    return shard


def substep(padded, conv_weight, conv_bias, out_weight):
    nvar = padded.shape[0]
    rows = padded.shape[1] - 2
    cols = padded.shape[2] - 2
    patches = jnp.concatenate(
        [padded[:, a : a + rows, b : b + cols] for a in range(3) for b in range(3)], axis=0
    )
    patches = patches.reshape(9 * nvar, rows * cols)
    pre = lax.dot_general(
        conv_weight, patches, (((0,), (0,)), ((), ())), preferred_element_type=jnp.float32
    )
    hidden = jax.nn.gelu(pre + conv_bias[:, None]).astype(jnp.bfloat16)
    change = lax.dot_general(
        out_weight, hidden, (((0,), (0,)), ((), ())), preferred_element_type=jnp.float32
    )
    centre = padded[:, 1:-1, 1:-1].astype(jnp.float32)
    return (centre + change.reshape(nvar, rows, cols)).astype(jnp.bfloat16)


def blend_weights(gram, proj):
    entries_number = gram.shape[0]
    eye = jnp.eye(entries_number, dtype=gram.dtype)
    system = (entries_number - 1) * eye + gram
    scale = jnp.sqrt(jnp.sum(system * system))
    current = system / scale
    inverse = eye
    for turn in range(NS_ITERS):
        factor = 1.5 * eye - 0.5 * jnp.dot(inverse, current, precision=lax.Precision.HIGHEST)
        current = jnp.dot(current, factor, precision=lax.Precision.HIGHEST)
        inverse = jnp.dot(factor, inverse, precision=lax.Precision.HIGHEST)
    root_inv = inverse / jnp.sqrt(scale)
    half = jnp.dot(root_inv, proj, precision=lax.Precision.HIGHEST)
    mean_w = jnp.dot(root_inv, half, precision=lax.Precision.HIGHEST)
    full = mean_w[:, None] + math.sqrt(entries_number - 1.0) * root_inv
    return 1.0 / entries_number + full - jnp.mean(full, axis=0, keepdims=True)


def per_device(
    sample_quantities,
    conv_weight,
    conv_bias,
    out_weight,
    obs_index,
    obs_count,
    obs_value,
    obs_weight,
):
    gridded_quantity = sample_quantities[0]
    nvar, rows, cols = gridded_quantity.shape
    banded = extended(gridded_quantity, (("lat", 1),), 2, False)
    padded = extended(banded, (("lon", 2),), 2, True)
    middle = substep(padded, conv_weight, conv_bias, out_weight)
    total_rows = rows * lax.axis_size("lat")
    global_row = lax.axis_index("lat") * rows - 1 + jnp.arange(rows + 2, dtype=jnp.int32)
    inside = (global_row >= 0) & (global_row < total_rows)
    middle = jnp.where(inside[None, :, None], middle, jnp.zeros_like(middle))
    gridded_quantity = substep(middle, conv_weight, conv_bias, out_weight)
    flat = gridded_quantity.reshape(-1)
    slots = obs_index.reshape(-1)
    picked = jnp.take(flat, slots).astype(jnp.float32)
    members = lax.all_gather(picked[None, :], "ens", axis=0, tiled=True)
    live = (jnp.arange(slots.shape[0], dtype=jnp.int32) < obs_count.reshape(())).astype(jnp.float32)
    weight = obs_weight.reshape(-1) * live
    mean = jnp.mean(members, axis=0)
    spread = members - mean[None, :]
    innov = obs_value.reshape(-1) - mean
    weighted = spread * weight[None, :]
    gram_part = jnp.dot(weighted, spread.T, precision=lax.Precision.HIGHEST)
    proj_part = jnp.dot(weighted, innov, precision=lax.Precision.HIGHEST)
    gram, proj = lax.psum((gram_part, proj_part), ("lat", "lon"))
    transform_weights_square = blend_weights(gram, proj)
    column = lax.dynamic_slice_in_dim(transform_weights_square, lax.axis_index("ens"), 1, 1)[:, 0]
    blended = jnp.tensordot(
        column,
        lax.all_gather(gridded_quantity[None], "ens", axis=0, tiled=True).astype(jnp.float32),
        axes=1,
        precision=lax.Precision.HIGHEST,
    )
    return blended.astype(jnp.bfloat16)[None]


def solution(mesh):
    return jax.shard_map(
        per_device,
        mesh=mesh,
        in_specs=(
            P("ens", None, "lat", "lon"),
            P(),
            P(),
            P(),
            P("lat", "lon", None),
            P("lat", "lon"),
            P("lat", "lon", None),
            P("lat", "lon", None),
        ),
        out_specs=P("ens", None, "lat", "lon"),
        check_vma=False,
    )
```

profile of v0, /device:TPU:0, one launch (start us, length us, event | category | flops | bytes accessed | tf_op | source)
XLA Modules:
  0.0 137.1 jit_solution(16326370746522004776)
XLA Ops:
  0.9 5.1 %collective-permute-start = (bf16[24,2,128]{2,1,0:T(2,128)(2,1)S(1)}, bf16[24,2,128]{2,1,0:T(2,128)(2,1)S(1)}, u32[]{:S(2)}, u32[]{:S(2)}) collective-permute-start(bf16[24,2,128]{2,1,0:T(2,128)(2,1)S(1)} %get-tuple-element.11), channel_id=1, source_target_pairs={{0,4},{4,8},{8,12},{1,5},{5,9},{9,13},{2,6},{6,10},{10,14},{3,7},{... | collective-permute-start | bytes 36872 | tf_op jit(solution)/shard_map/ppermute | solution.py:18
  6.0 1.3 collective-permute-start.1
  9.3 2.3 %collective-permute-done.1 = bf16[24,2,128]{2,1,0:T(2,128)(2,1)S(1)} collective-permute-done((bf16[24,2,128]{2,1,0:T(2,128)(2,1)S(1)}, bf16[24,2,128]{2,1,0:T(2,128)(2,1)S(1)}, u32[]{:S(2)}, u32[]{:S(2)}) %collective-permute-start.1) | collective-permute-done | bytes 12320 | tf_op jit(solution)/shard_map/ppermute | solution.py:19
  13.0 1.7 %collective-permute-start.3 = (bf16[24,68,2]{2,1,0:T(8,128)(2,1)S(1)}, bf16[24,68,2]{2,1,0:T(8,128)(2,1)S(1)}, u32[]{:S(2)}, u32[]{:S(2)}) collective-permute-start(bf16[24,68,2]{2,1,0:T(8,128)(2,1)S(1)} %get-tuple-element.7), channel_id=1, source_target_pairs={{1,0},{2,1},{3,2},{0,3},{5,4},{6,5},{7,6},{4,7},{9,8},{10,9},{11,1... | collective-permute-start | bytes 19592 | tf_op jit(solution)/shard_map/ppermute | solution.py:19
  14.8 8.9 %collective-permute-done.2 = bf16[24,68,2]{2,1,0:T(8,128)(2,1)S(1)} collective-permute-done((bf16[24,68,2]{2,1,0:T(8,128)(2,1)S(1)}, bf16[24,68,2]{2,1,0:T(8,128)(2,1)S(1)}, u32[]{:S(2)}, u32[]{:S(2)}) %collective-permute-start.2) | collective-permute-done | bytes 6560 | tf_op jit(solution)/shard_map/ppermute | solution.py:18
  24.5 2.2 %pad_maximum_fusion.1 = (bf16[24,68,130]{2,1,0:T(8,128)(2,1)S(1)}, bf16[24,68,130]{2,1,0:T(8,128)(2,1)S(1)}) fusion(bf16[24,68,2]{2,1,0:T(8,128)(2,1)S(1)} %collective-permute-done.3, bf16[24,2,128]{2,1,0:T(2,128)(2,1)S(1)} %collective-permute-done.1, bf16[24,64,128]{2,1,0:T(8,128)(2,1)} %bitcast.208, bf16[24,2,128]{2,1,0:T(2,128)(2,1)S(1)} %collective-permute-done, ...), kind=kLoop, calls=%fused_computation.84 | loop fusion | flops 3394560 | bytes 1279488 | tf_op jit(solution)/shard_map/concatenate | solution.py:20
  28.5 1.3 slice_dynamic-update-slice_fusion.6
  30.8 1.3 slice_dynamic-update-slice_fusion.4
  32.1 1.6 %slice_dynamic-update-slice_fusion.8 = bf16[216,66,130]{2,1,0:T(8,128)(2,1)} fusion(bf16[216,66,130]{2,1,0:T(8,128)(2,1)} %slice_dynamic-update-slice_fusion.4, bf16[24,68,132]{2,1,0:T(8,128)(2,1)S(1)} %pad_maximum_fusion), kind=kLoop, calls=%fused_computation.89 | loop fusion | bytes 1296576
  33.7 1.3 slice_dynamic-update-slice_fusion.3
  35.0 1.3 slice_dynamic-update-slice_fusion.2
  36.3 1.6 %slice_dynamic-update-slice_fusion.1 = bf16[216,66,130]{2,1,0:T(8,128)(2,1)} fusion(bf16[216,66,130]{2,1,0:T(8,128)(2,1)} %slice_dynamic-update-slice_fusion.2, bf16[24,68,132]{2,1,0:T(8,128)(2,1)S(1)} %pad_maximum_fusion), kind=kLoop, calls=%fused_computation.75 | loop fusion | bytes 1296576
  37.9 1.3 slice_dynamic-update-slice_fusion
  39.2 11.0 %reshape.164 = bf16[216,8580]{1,0:T(8,128)(2,1)} reshape(bf16[216,66,130]{2,1,0:T(8,128)(2,1)} %slice_dynamic-update-slice_fusion) | data formatting | bytes 7413120 | tf_op jit(solution)/shard_map/reshape | solution.py:31
  50.2 5.6 %convolution_bitcast_fusion = f32[24,8580]{1,0:T(8,128)S(1)} fusion(bf16[256,24]{0,1:T(8,128)(2,1)S(1)} %copy-done.5, bf16[216,8580]{1,0:T(8,128)(2,1)} %reshape.164, bf16[216,256]{1,0:T(8,128)(2,1)S(1)} %copy-done, f32[256]{0:T(256)S(1)} %copy-done.6), kind=kOutput, calls=%fused_computation.7 | convolution fusion | flops 1076275200 | bytes 4654144 | tf_op jit(solution)/shard_map/dot_general | solution.py:36
  55.9 2.2 %reshape.137 = f32[24,66,130]{2,1,0:T(8,128)} reshape(f32[24,8580]{1,0:T(8,128)S(1)} %convolution_bitcast_fusion) | data formatting | bytes 1647360 | tf_op jit(solution)/shard_map/reshape | solution.py:40
  58.1 2.2 %fusion.46 = bf16[24,66,130]{2,1,0:T(8,128)(2,1)S(1)} fusion(f32[24,66,130]{2,1,0:T(8,128)} %reshape.137, pred[66]{0:T(512)(128)(4,1)S(1)} %compare_and_fusion, bf16[24,68,132]{2,1,0:T(8,128)(2,1)S(1)} %pad_maximum_fusion), kind=kLoop, calls=%fused_computation.73 | loop fusion | flops 823680 | bytes 1647426 | tf_op jit(solution)/shard_map/jit(_where)/select_n | solution.py:79
  63.1 1.7 %copy-done.2 = bf16[216,64,128]{2,1,0:T(8,128)(2,1)} copy-done((bf16[216,64,128]{2,1,0:T(8,128)(2,1)}, bf16[216,64,128]{2,1,0:T(8,128)(2,1)S(1)}, u32[]{:S(2)}) %copy-start.2) | copy-done | bytes 3538968
  64.9 10.4 %fusion.23 = f32[3,8,64,128]{3,1,2,0:T(8,128)S(1)} fusion(bf16[256,24]{0,1:T(8,128)(2,1)S(1)} %copy-done.5, bf16[216,256]{1,0:T(8,128)(2,1)S(1)} %copy-done, f32[256]{0:T(256)S(1)} %copy-done.6, bf16[27,8,64,128]{3,2,1,0:T(8,128)(2,1)} %bitcast.212), kind=kOutput, calls=%fused_computation.28 | convolution fusion | flops 1027604480 | bytes 4449280 | tf_op jit(solution)/shard_map/dot_general | solution.py:36
  75.8 1.9 %gather_fusion = bf16[256]{0:T(256)(128)(2,1)S(1)} fusion(bf16[196608]{0:T(1024)(128)(2,1)S(1)} %bitcast.205, s32[1024]{0:T(1024)S(1)} %pad_clamp_fusion), kind=kCustom, calls=%fused_computation | custom fusion | bytes 2048 | tf_op jit(solution)/shard_map/jit(_take)/gather | solution.py:83
  77.8 4.2 %all-gather.1 = f32[2,1,256]{2,1,0:T(1,128)S(1)} all-gather(f32[1,1,256]{2,1,0:T(1,128)S(1)} %bitcast_convert_fusion), channel_id=1, replica_groups=mesh['ens'=2,'lat'=4,'lon'=4] {'ens'}, dimensions={0}, use_global_device_ids=true | all-gather | bytes 3072 | tf_op jit(solution)/shard_map/all_gather | solution.py:84
  82.3 32.1 %all-reduce = (f32[2,2]{1,0:T(2,128)S(1)}, f32[2]{0:T(128)S(1)}) all-reduce(f32[2,2]{1,0:T(2,128)S(1)} %fusion.51, f32[2]{0:T(128)S(1)} %convolution_bitcast_fusion.3), channel_id=1, replica_groups=mesh['ens'=2,'lat'=4,'lon'=4] {'lat','lon'}, use_global_device_ids=true, to_apply=%region_1.2 | all-reduce | flops 6 | bytes 48 | tf_op jit(solution)/shard_map/psum | solution.py:93
  123.6 8.9 %all-gather = bf16[48,64,128]{2,1,0:T(8,128)(2,1)S(1)} all-gather(bf16[24,64,128]{2,1,0:T(8,128)(2,1)S(1)} %fusion.47), channel_id=2, replica_groups=mesh['ens'=2,'lat'=4,'lon'=4] {'ens'}, dimensions={0}, use_global_device_ids=true | all-gather | bytes 1179648 | tf_op jit(solution)/shard_map/all_gather | solution.py:98
  133.5 2.8 %fusion.48 = f32[1,24,64,128]{3,0,2,1:T(1,128)S(1)} fusion(bf16[2,24,64,128]{3,2,1,0:T(8,128)(2,1)S(1)} %bitcast.210, f32[2]{0:T(128)S(1)} %dynamic-slice_reduce_fusion), kind=kOutput, calls=%fused_computation.87 | convolution fusion | flops 4718592 | bytes 1572872 | tf_op jit(solution)/shard_map/dot_general | solution.py:96
  (110 shorter events, 20.9 us)
Async XLA Ops:
  0.0 50.2 %copy-start = (bf16[216,256]{1,0:T(8,128)(2,1)S(1)}, bf16[216,256]{1,0:T(8,128)(2,1)}, u32[]{:S(2)}) copy-start(bf16[216,256]{1,0:T(8,128)(2,1)} %param.9) | copy-start | bytes 331780
  0.9 26.8 %copy-start.1 = (bf16[1,24,64,128]{3,2,1,0:T(8,128)(2,1)S(1)}, bf16[1,24,64,128]{3,2,1,0:T(8,128)(2,1)}, u32[]{:S(2)}) copy-start(bf16[1,24,64,128]{3,2,1,0:T(8,128)(2,1)} %param.8) | copy-start | bytes 1179652
  0.9 8.4 %collective-permute-start = (bf16[24,2,128]{2,1,0:T(2,128)(2,1)S(1)}, bf16[24,2,128]{2,1,0:T(2,128)(2,1)S(1)}, u32[]{:S(2)}, u32[]{:S(2)}) collective-permute-start(bf16[24,2,128]{2,1,0:T(2,128)(2,1)S(1)} %get-tuple-element.11), channel_id=1, source_target_pairs={{0,4},{4,8},{8,12},{1,5},{5,9},{9,13},{2,6},{6,10},{10,14},{3,7},{... | collective-permute-start | bytes 36872 | tf_op jit(solution)/shard_map/ppermute | solution.py:18
  6.0 5.6 %collective-permute-start.1 = (bf16[24,2,128]{2,1,0:T(2,128)(2,1)S(1)}, bf16[24,2,128]{2,1,0:T(2,128)(2,1)S(1)}, u32[]{:S(2)}, u32[]{:S(2)}) collective-permute-start(bf16[24,2,128]{2,1,0:T(2,128)(2,1)S(1)} %get-tuple-element.12), channel_id=1, source_target_pairs={{4,0},{8,4},{12,8},{5,1},{9,5},{13,9},{6,2},{10,6},{14,10},{7,3},{... | collective-permute-start | bytes 36872 | tf_op jit(solution)/shard_map/ppermute | solution.py:19
  13.0 10.7 %collective-permute-start.2 = (bf16[24,68,2]{2,1,0:T(8,128)(2,1)S(1)}, bf16[24,68,2]{2,1,0:T(8,128)(2,1)S(1)}, u32[]{:S(2)}, u32[]{:S(2)}) collective-permute-start(bf16[24,68,2]{2,1,0:T(8,128)(2,1)S(1)} %get-tuple-element.8), channel_id=1, source_target_pairs={{0,1},{1,2},{2,3},{3,0},{4,5},{5,6},{6,7},{7,4},{8,9},{9,10},{10,1... | collective-permute-start | bytes 19592 | tf_op jit(solution)/shard_map/ppermute | solution.py:18
  13.0 11.5 %collective-permute-start.3 = (bf16[24,68,2]{2,1,0:T(8,128)(2,1)S(1)}, bf16[24,68,2]{2,1,0:T(8,128)(2,1)S(1)}, u32[]{:S(2)}, u32[]{:S(2)}) collective-permute-start(bf16[24,68,2]{2,1,0:T(8,128)(2,1)S(1)} %get-tuple-element.7), channel_id=1, source_target_pairs={{1,0},{2,1},{3,2},{0,3},{5,4},{6,5},{7,6},{4,7},{9,8},{10,9},{11,1... | collective-permute-start | bytes 19592 | tf_op jit(solution)/shard_map/ppermute | solution.py:19
  39.2 11.0 %copy-start.5 = (bf16[256,24]{0,1:T(8,128)(2,1)S(1)}, bf16[256,24]{0,1:T(8,128)(2,1)}, u32[]{:S(2)}) copy-start(bf16[256,24]{0,1:T(8,128)(2,1)} %param.11) | copy-start | bytes 36868
  39.2 11.0 %copy-start.6 = (f32[256]{0:T(256)S(1)}, f32[256]{0:T(256)}, u32[]{:S(2)}) copy-start(f32[256]{0:T(256)} %param.10) | copy-start | bytes 3076
  63.1 1.8 %copy-start.2 = (bf16[216,64,128]{2,1,0:T(8,128)(2,1)}, bf16[216,64,128]{2,1,0:T(8,128)(2,1)S(1)}, u32[]{:S(2)}) copy-start(bf16[216,64,128]{2,1,0:T(8,128)(2,1)S(1)} %slice_dynamic-update-slice_fusion.9) | copy-start | bytes 10616836
  64.9 12.9 %copy-start.3 = (s32[1,1,256]{2,1,0:T(1,128)S(1)}, s32[1,1,256]{2,1,0:T(1,128)}, u32[]{:S(2)}) copy-start(s32[1,1,256]{2,1,0:T(1,128)} %param.12) | copy-start | bytes 3076
  64.9 17.2 %copy-start.4 = (f32[1,1,256]{2,1,0:T(1,128)S(1)}, f32[1,1,256]{2,1,0:T(1,128)}, u32[]{:S(2)}) copy-start(f32[1,1,256]{2,1,0:T(1,128)} %param.14) | copy-start | bytes 3076
where the time goes:
time: 138 us; the launch traced here: 137 us
  blocking collectives  45.3 us (33%)
  local copies, waits for them, and re-layouts  32.8 us (24%)
  matrix products  27.4 us (20%)
  waiting for transfers between devices  12 us (9%)
  other arithmetic  9.8 us (7%)
  starting transfers between devices  8.17 us (6%)
  between operations  1.67 us (1%)
    psum x1, blocking collectives, per_device(): gram, proj = lax.psum((gram_part, proj_part), ('lat', 'lon'))  32.1 us
    dot_general x2, matrix products, substep(): lax.dot_general(out_weight, hidden, (((0,), (0,)), ((), ())), preferred_e...  16 us
    unnamed x31, local copies, waits for them, and re-layouts  14.6 us
    reshape x1, local copies, waits for them, and re-layouts, substep(): patches = patches.reshape(9 * nvar, rows * cols)  11 us
    all_gather x1, blocking collectives, per_device(): lax.all_gather(gridded_quantity[None], 'ens', axis=0, tiled=True)  8.94 us
    ppermute x2, waiting for transfers between devices, extended(): before = lax.ppermute(last, axis, up)  8.93 us
    ppermute x2, starting transfers between devices, extended(): before = lax.ppermute(last, axis, up)  5.15 us
    all_gather x1, blocking collectives, per_device(): members = lax.all_gather(picked[None, :], 'ens', axis=0, tiled=True)  4.24 us
  transfers between devices with their start and end apart: 4, of which 3 were waited for; matrix products, arithmetic and copies ran while one was open for 1% of the time, Pallas kernels for 0%

commit v1 on v0

v1 whole, which is shorter than its diff:
```python
import functools
import math

import jax
import jax.numpy as jnp
from jax import lax
from jax.experimental import pallas as pl
from jax.experimental.pallas import tpu as pltpu
from jax.sharding import PartitionSpec as P

NS_ITERS = 20
GELU_A = math.sqrt(2.0 / math.pi)
GELU_B = GELU_A * 0.044715
F32 = jnp.float32
BF16 = jnp.bfloat16
PAD = 8


def lanes_of(shape):
    return lax.broadcasted_iota(jnp.int32, shape, len(shape) - 1)


def rows_kernel(top_ref, bottom_ref, up_ref, down_ref, stage):
    nvar, tile, cols = top_ref.shape
    for ref, out, first in ((top_ref, up_ref, 0), (bottom_ref, down_ref, tile - 2)):
        stage[...] = ref[...].reshape(nvar * tile, cols).astype(F32)
        both = [stage[pl.ds(first + i, nvar, stride=tile), :] for i in range(2)]
        out[...] = jnp.concatenate(both, axis=0).astype(BF16)


def edge_rows(x):
    nvar, rows, cols = x.shape
    tile = 16
    last = rows // tile - 1
    out = jax.ShapeDtypeStruct((2 * nvar, cols), BF16)
    return pl.pallas_call(
        rows_kernel,
        out_shape=(out, out),
        grid=(1,),
        in_specs=[
            pl.BlockSpec((nvar, tile, cols), lambda i: (0, 0, 0)),
            pl.BlockSpec((nvar, tile, cols), lambda i: (0, last, 0)),
        ],
        out_specs=[pl.BlockSpec((2 * nvar, cols), lambda i: (0, 0))] * 2,
        scratch_shapes=[pltpu.VMEM((nvar * tile, cols), F32)],
        name="edge_rows",
    )(x, x)


def columns_kernel(x_ref, north_ref, south_ref, left_ref, right_ref, stage):
    nvar, rows, cols = x_ref.shape
    wanted = (0, 1, cols - 2, cols - 1)
    k = lax.broadcasted_iota(jnp.int32, (8, cols), 0)
    lane = lanes_of((8, cols))
    pick = jnp.zeros((8, cols), F32)
    for i, c in enumerate(wanted):
        pick = jnp.where((k == i) & (lane == c), 1.0, pick)
    pick = pick.astype(BF16)
    per = cols // rows
    flat = x_ref[...].reshape(nvar * rows, cols)
    taken = lax.dot_general(pick, flat, (((1,), (1,)), ((), ())), preferred_element_type=F32)
    for v in range(nvar):
        block = taken[:, (v // per) * cols : (v // per + 1) * cols]
        shift = (2 - (v % per) * rows) % cols
        stage[8 * v : 8 * v + 8, :] = pltpu.roll(block, shift, 1)
    lane = lanes_of((nvar, cols))
    halo = []
    for ref, first in ((north_ref, 0), (south_ref, rows + 2)):
        for i in range(2):
            halo.append((first + i, ref[i * nvar : (i + 1) * nvar, :].astype(F32)))
    outs = []
    for i, c in enumerate(wanted):
        column = stage[pl.ds(i, nvar, stride=8), :]
        column = jnp.where(lane < rows + 2, column, 0.0)
        for at, row in halo:
            column = jnp.where(lane == at, pltpu.roll(row, (at - c) % cols, 1), column)
        outs.append(column)
    left_ref[...] = jnp.concatenate(outs[:2], axis=0).astype(BF16)
    right_ref[...] = jnp.concatenate(outs[2:], axis=0).astype(BF16)


def edge_columns(x, north, south):
    nvar, rows, cols = x.shape
    out = jax.ShapeDtypeStruct((2 * nvar, cols), BF16)
    return pl.pallas_call(
        columns_kernel,
        out_shape=(out, out),
        scratch_shapes=[pltpu.VMEM((8 * nvar, cols), F32)],
        name="edge_columns",
    )(x, north, south)


def gelu2(pre):
    inner = pre * (GELU_A + GELU_B * (pre * pre))
    return pre + pre * jnp.tanh(inner)


def forecast_kernel(
    spot_ref,
    north_in_ref,
    inside_ref,
    x_ref,
    north_ref,
    south_ref,
    own_left_ref,
    own_right_ref,
    from_left_ref,
    from_right_ref,
    conv_ref,
    out_w_ref,
    lane_ref,
    forecast_ref,
    picked_ref,
    xf,
    first,
    second,
    final,
    seen,
):
    nvar, rows, cols = x_ref.shape
    block = 3 * nvar + PAD
    deep = 3 * block
    lane = lanes_of((nvar, cols))
    ones = jnp.ones((PAD, cols), F32)

    def tap_rows(row, west, east, at):
        left = jnp.where(lane == 0, pltpu.roll(west, (cols - at) % cols, 1), pltpu.roll(row, 1, 1))
        right = jnp.where(
            lane == cols - 1, pltpu.roll(east, (2 * cols - 1 - at) % cols, 1), pltpu.roll(row, cols - 1, 1)
        )
        return jnp.concatenate([row, left, right, ones], axis=0).astype(BF16)

    def advance(patches, centre):
        pre = jnp.dot(conv_ref[...], patches, preferred_element_type=F32)
        hidden = gelu2(pre).astype(BF16)
        change = jnp.dot(out_w_ref[...], hidden, preferred_element_type=F32)
        return (centre + change[:nvar]).astype(BF16).astype(F32)

    xf[...] = x_ref[...].reshape(nvar * rows, cols).astype(F32)
    from_left = from_left_ref[...].astype(F32)
    from_right = from_right_ref[...].astype(F32)
    own_left = own_left_ref[...].astype(F32)
    own_right = own_right_ref[...].astype(F32)
    far_west, west = from_left[:nvar], from_left[nvar:]
    east, far_east = from_right[:nvar], from_right[nvar:]
    inner_west, inner_east = own_left[:nvar], own_right[nvar:]

    for ref, start in ((north_ref, 0), (south_ref, rows + 2)):
        for i in range(2):
            row = ref[i * nvar : (i + 1) * nvar, :].astype(F32)
            first[(start + i) * block : (start + i + 1) * block, :] = tap_rows(row, west, east, start + i)

    def fill(r, carry):
        row = xf[pl.ds(r, nvar, stride=rows), :]
        at = pl.multiple_of((r + 2) * block, 16)
        first[pl.ds(at, block), :] = tap_rows(row, west, east, r + 2)
        return carry

    lax.fori_loop(0, rows, fill, 0, unroll=4)

    sides = []
    for mid, low, high in ((west, far_west, inner_west), (east, inner_east, far_east)):
        stack = []
        for a in range(3):
            for entry in (mid, low, high):
                stack.append(pltpu.roll(entry, (1 - a) % cols, 1) if a != 1 else entry)
            stack.append(ones)
        sides.append(jnp.concatenate(stack, axis=0).astype(BF16))
    patches = jnp.concatenate(sides, axis=1)
    beside = advance(patches, jnp.concatenate([west, east], axis=1))
    keep = jnp.where(lane == 1, north_in_ref[0], jnp.where(lane == rows + 2, north_in_ref[1], 1)) > 0
    mid_west = jnp.where(keep, beside[:, :cols], 0.0)
    mid_east = jnp.where(keep, beside[:, cols:], 0.0)

    def pair(source, at):
        at = pl.multiple_of(at * block, 16)
        patches = jnp.concatenate(
            [source[pl.ds(at, deep), :], source[pl.ds(at + block, deep), :]], axis=1
        )
        centre = jnp.concatenate(
            [source[pl.ds(at + block, nvar), :], source[pl.ds(at + 2 * block, nvar), :]], axis=1
        ).astype(F32)
        return advance(patches, centre)

    def first_step(i, carry):
        both = pair(first, 2 * i)
        for half in range(2):
            m = 2 * i + half
            good = (jnp.where(m == 0, north_in_ref[0], 1) * jnp.where(m == rows + 1, north_in_ref[1], 1)) > 0
            row = both[:, half * cols : (half + 1) * cols]
            row = jnp.where(good, row, 0.0)
            at = pl.multiple_of(m * block, 16)
            second[pl.ds(at, block), :] = tap_rows(row, mid_west, mid_east, m + 1)
        return carry

    lax.fori_loop(0, rows // 2 + 1, first_step, 0, unroll=3)

    def second_step(j, carry):
        both = pair(second, 2 * j)
        both = jnp.concatenate([both[:, :cols], both[:, cols:]], axis=0)
        at = pl.multiple_of(j * 2 * nvar, 16)
        final[pl.ds(at, 2 * nvar), :] = both
        forecast_ref[pl.ds(at, 2 * nvar), :] = both.astype(BF16)
        return carry

    lax.fori_loop(0, rows // 2, second_step, 0, unroll=4)

    def look(o, carry):
        seen[pl.ds(o, 1), :] = final[pl.ds(spot_ref[o], 1), :]
        return carry

    slots = seen.shape[0]
    lax.fori_loop(0, slots, look, 0, unroll=8)
    masked = jnp.where(lane_ref[...] == lanes_of((slots, cols)), seen[...], 0.0).astype(BF16)
    values = lax.dot_general(
        jnp.ones((8, cols), BF16), masked, (((1,), (1,)), ((), ())), preferred_element_type=F32
    )
    picked_ref[...] = values
    del inside_ref


def run_forecast(spot, inside, x, north, south, own_left, own_right, from_left, from_right, conv, out_w, lane):
    nvar, rows, cols = x.shape
    slots = spot.shape[0]
    block = 3 * nvar + PAD
    smem = pl.BlockSpec(memory_space=pltpu.SMEM)
    vmem = pl.BlockSpec(memory_space=pltpu.VMEM)
    return pl.pallas_call(
        forecast_kernel,
        out_shape=(
            jax.ShapeDtypeStruct((rows * nvar, cols), BF16),
            jax.ShapeDtypeStruct((8, slots), F32),
        ),
        in_specs=[smem, smem, smem] + [vmem] * 10,
        out_specs=(vmem, vmem),
        scratch_shapes=[
            pltpu.VMEM((nvar * rows, cols), F32),
            pltpu.VMEM(((rows + 4) * block, cols), BF16),
            pltpu.VMEM(((rows + 2) * block, cols), BF16),
            pltpu.VMEM((rows * nvar, cols), F32),
            pltpu.VMEM((slots, cols), F32),
        ],
        name="forecast",
    )(spot, inside, inside, x, north, south, own_left, own_right, from_left, from_right, conv, out_w, lane)


def pair_weights(gram, proj):
    count = len(proj)
    system = [[gram[k][m] + (float(count - 1) if k == m else 0.0) for m in range(count)] for k in range(count)]
    total = sum(entry * entry for line in system for entry in line)
    scale = jnp.sqrt(total)
    one = jnp.ones_like(scale)
    eye = [[one if k == m else 0.0 * one for m in range(count)] for k in range(count)]

    def times(left, right):
        return [
            [sum(left[k][j] * right[j][m] for j in range(count)) for m in range(count)] for k in range(count)
        ]

    current = [[entry / scale for entry in line] for line in system]
    inverse = eye
    for turn in range(NS_ITERS):
        both = times(inverse, current)
        factor = [[1.5 * eye[k][m] - 0.5 * both[k][m] for m in range(count)] for k in range(count)]
        current = times(current, factor)
        inverse = times(factor, inverse)
    root = jnp.sqrt(scale)
    root_inv = [[entry / root for entry in line] for line in inverse]
    half = [sum(root_inv[k][j] * proj[j] for j in range(count)) for k in range(count)]
    mean_w = [sum(root_inv[k][j] * half[j] for j in range(count)) for k in range(count)]
    span = math.sqrt(count - 1.0)
    full = [[mean_w[k] + span * root_inv[k][m] for m in range(count)] for k in range(count)]
    centre = [sum(full[k][m] for k in range(count)) / count for m in range(count)]
    return [[1.0 / count + full[k][m] - centre[m] for m in range(count)] for k in range(count)]


def analysis_kernel(me_ref, told_ref, mine_ref, other_ref, out_ref, blended):
    count, shards = told_ref.shape[0], told_ref.shape[1]
    nvar, rows, cols = out_ref.shape
    pairs = [(k, m) for k in range(count) for m in range(k, count)]
    sums = {key: 0.0 for key in pairs}
    for k in range(count):
        sums[k] = 0.0
    for s in range(shards):
        hx = [told_ref[k, s, 0:2, :] for k in range(count)]
        value = told_ref[0, s, 2:4, :]
        weight = told_ref[0, s, 4:6, :]
        mean = sum(hx) / count
        spread = [h - mean for h in hx]
        innov = value - mean
        for k in range(count):
            scaled = spread[k] * weight
            sums[k] = sums[k] + scaled * innov
            for m in range(k, count):
                sums[k, m] = sums[k, m] + scaled * spread[m]
    tile = (8, cols)
    whole = {key: jnp.broadcast_to(jnp.sum(term, keepdims=True), tile) for key, term in sums.items()}
    gram = [[whole[min(k, m), max(k, m)] for m in range(count)] for k in range(count)]
    weights = pair_weights(gram, [whole[k] for k in range(count)])
    me = me_ref[0]
    mine = jnp.where(me == 0, weights[0][0], weights[1][1])[0:1, :]
    other = jnp.where(me == 0, weights[1][0], weights[0][1])[0:1, :]
    blended[...] = mine * mine_ref[...].astype(F32) + other * other_ref[...].astype(F32)
    for v in range(nvar):
        for r in range(0, rows, 16):
            halves = [
                blended[pl.ds((r + 8 * i) * nvar + v, 8, stride=nvar), :] for i in range(2)
            ]
            out_ref[v, r : r + 16, :] = jnp.concatenate(halves, axis=0).astype(BF16)


def run_analysis(me, told, mine, other, shape):
    nvar, rows, cols = shape
    vmem = pl.BlockSpec(memory_space=pltpu.VMEM)
    return pl.pallas_call(
        analysis_kernel,
        out_shape=jax.ShapeDtypeStruct(shape, BF16),
        in_specs=[pl.BlockSpec(memory_space=pltpu.SMEM), vmem, vmem, vmem],
        out_specs=vmem,
        scratch_shapes=[pltpu.VMEM((nvar * rows, cols), F32)],
        name="analysis",
    )(me, told, mine, other)


def blend_weights(gram, proj):
    entries_number = gram.shape[0]
    eye = jnp.eye(entries_number, dtype=gram.dtype)
    system = (entries_number - 1) * eye + gram
    scale = jnp.sqrt(jnp.sum(system * system))
    current = system / scale
    inverse = eye
    for turn in range(NS_ITERS):
        factor = 1.5 * eye - 0.5 * jnp.dot(inverse, current, precision=lax.Precision.HIGHEST)
        current = jnp.dot(current, factor, precision=lax.Precision.HIGHEST)
        inverse = jnp.dot(factor, inverse, precision=lax.Precision.HIGHEST)
    root_inv = inverse / jnp.sqrt(scale)
    half = jnp.dot(root_inv, proj, precision=lax.Precision.HIGHEST)
    mean_w = jnp.dot(root_inv, half, precision=lax.Precision.HIGHEST)
    full = mean_w[:, None] + math.sqrt(entries_number - 1.0) * root_inv
    return 1.0 / entries_number + full - jnp.mean(full, axis=0, keepdims=True)


def many_members(told, forecast, shape):
    nvar, rows, cols = shape
    members = told[:, :, 0:2, :].reshape(told.shape[0], -1)
    value = told[0, :, 2:4, :].reshape(-1)
    weight = told[0, :, 4:6, :].reshape(-1)
    mean = jnp.mean(members, axis=0)
    spread = members - mean[None, :]
    innov = value - mean
    weighted = spread * weight[None, :]
    gram = jnp.dot(weighted, spread.T, precision=lax.Precision.HIGHEST)
    proj = jnp.dot(weighted, innov, precision=lax.Precision.HIGHEST)
    transform = blend_weights(gram, proj)
    column = lax.dynamic_slice_in_dim(transform, lax.axis_index("ens"), 1, 1)[:, 0]
    everyone = lax.all_gather(forecast[None], "ens", axis=0, tiled=True)
    blended = jnp.tensordot(column, everyone.astype(F32), axes=1, precision=lax.Precision.HIGHEST)
    return blended.astype(BF16).reshape(rows, nvar, cols).transpose(1, 0, 2)


def packed_weights(conv_weight, conv_bias, out_weight, nvar):
    hid = conv_bias.shape[0]
    taps = conv_weight.reshape(3, 3, nvar, hid)
    taps = jnp.stack([taps[:, 1], taps[:, 0], taps[:, 2]], axis=1).reshape(3, 3 * nvar, hid)
    high = conv_bias.astype(BF16)
    rest = conv_bias - high.astype(F32)
    middle = rest.astype(BF16)
    low = (rest - middle.astype(F32)).astype(BF16)
    bias = jnp.zeros((3, PAD, hid), BF16)
    bias = bias.at[1, 0].set(high).at[1, 1].set(middle).at[1, 2].set(low)
    conv = jnp.concatenate([taps, bias], axis=1).reshape(-1, hid).T
    half = (out_weight.astype(F32) * 0.5).astype(BF16).T
    return conv, half


def per_device(
    sample_quantities,
    conv_weight,
    conv_bias,
    out_weight,
    obs_index,
    obs_count,
    obs_value,
    obs_weight,
):
    x = sample_quantities[0]
    nvar, rows, cols = x.shape
    n_ens, n_lat, n_lon = (lax.axis_size(axis) for axis in ("ens", "lat", "lon"))
    down_lat = [(i, i + 1) for i in range(n_lat - 1)]
    up_lat = [(j, i) for i, j in down_lat]
    right_lon = [(i, (i + 1) % n_lon) for i in range(n_lon)]
    left_lon = [(j, i) for i, j in right_lon]

    first_rows, last_rows = edge_rows(x)
    north = lax.ppermute(last_rows, "lat", down_lat)
    south = lax.ppermute(first_rows, "lat", up_lat)
    own_left, own_right = edge_columns(x, north, south)
    from_left = lax.ppermute(own_right, "lon", right_lon)
    from_right = lax.ppermute(own_left, "lon", left_lon)

    conv, out_w = packed_weights(conv_weight, conv_bias, out_weight, nvar)
    slots = obs_index.reshape(-1)
    var, row, lane = slots // (rows * cols), slots // cols % rows, slots % cols
    spot = jnp.clip(row * nvar + var, 0, rows * nvar - 1)
    here = lax.axis_index("lat")
    inside = jnp.stack([here > 0, here < n_lat - 1]).astype(jnp.int32)
    forecast, picked = run_forecast(
        spot,
        inside,
        x,
        north,
        south,
        own_left,
        own_right,
        from_left,
        from_right,
        conv,
        out_w,
        lane[:, None],
    )

    count = slots.shape[0]
    live = (jnp.arange(count, dtype=jnp.int32) < obs_count.reshape(())).astype(F32)
    weight = obs_weight.reshape(-1) * live
    fold = (count // cols, cols)
    note = jnp.concatenate(
        [picked[0].reshape(fold), obs_value.reshape(fold), weight.reshape(fold), jnp.zeros(fold, F32)], axis=0
    )
    devices = n_ens * n_lat * n_lon
    notes = jnp.broadcast_to(note[None], (devices,) + note.shape)
    told = lax.all_to_all(notes, ("ens", "lat", "lon"), 0, 0, tiled=True)
    told = told.reshape(n_ens, n_lat * n_lon, *note.shape)
    if n_ens == 2:
        other = lax.ppermute(forecast, "ens", [(0, 1), (1, 0)])
        me = lax.axis_index("ens").reshape(1)
        return run_analysis(me, told, forecast, other, x.shape)[None]
    return many_members(told, forecast, x.shape)[None]


def solution(mesh):
    return jax.shard_map(
        per_device,
        mesh=mesh,
        in_specs=(
            P("ens", None, "lat", "lon"),
            P(),
            P(),
            P(),
            P("lat", "lon", None),
            P("lat", "lon"),
            P("lat", "lon", None),
            P("lat", "lon", None),
        ),
        out_specs=P("ens", None, "lat", "lon"),
        check_vma=False,
    )
```

time: 138 us -> 62.4 us (0.45)
  blocking collectives: 45.3 us -> 0 us
  Pallas kernels: 0 us -> 29 us
  matrix products: 27.4 us -> 0 us
  local copies, waits for them, and re-layouts: 32.8 us -> 5.7 us
  other arithmetic: 9.8 us -> 2.57 us
  starting transfers between devices: 8.17 us -> 12.6 us
    psum x1 -> x0, blocking collectives: 32.1 us -> none  [per_device(): gram, proj = lax.psum((gram_part, proj_part), ('lat', 'lon'))]
    pallas_call x0 -> x4, Pallas kernels: none -> 29 us  [the longest x1 22.9 us: run_forecast(): pl.pallas_call(forecast_kernel, out_shape=(jax.ShapeDtypeStruct((rows * n...]
    dot_general x66 -> x0, matrix products: 27.4 us -> none  [the longest x2 16 us: substep(): lax.dot_general(out_weight, hidden, (((0,), (0,)), ((), ())), preferred_e...]
    all_gather x2 -> x0, blocking collectives: 13.2 us -> none  [the longest x1 8.94 us: per_device(): lax.all_gather(gridded_quantity[None], 'ens', axis=0, tiled=True)]
    reshape x2, local copies, waits for them, and re-layouts: 13.2 us -> 0.89 us  [the longest x1 0.76 us: packed_weights(): conv = jnp.concatenate([taps, bias], axis=1).reshape(-1, hid).T]
    unnamed x31 -> x24, local copies, waits for them, and re-layouts: 14.6 us -> 3.34 us
    ppermute x4 -> x5, waiting for transfers between devices: 12 us -> 3.12 us  [the longest x1 2.23 us: per_device(): south = lax.ppermute(first_rows, 'lat', up_lat)]
    all_to_all x0 -> x1, waiting for transfers between devices: none -> 8.2 us  [per_device(): told = lax.all_to_all(notes, ('ens', 'lat', 'lon'), 0, 0, tiled=True)]
  transfers between devices with their start and end apart: 4 -> 6, of which waited for: 3 -> 3; matrix products, arithmetic and copies ran while one was open for 1% -> 8% of each run, Pallas kernels for 0% -> 0%
where the time goes in v1:
time: 62.4 us; the launch traced here: 62 us
  Pallas kernels  29 us (46%)
  starting transfers between devices  12.6 us (20%)
  waiting for transfers between devices  11.3 us (18%)
  local copies, waits for them, and re-layouts  5.7 us (9%)
  other arithmetic  2.57 us (4%)
  between operations  0.78 us (1%)
    pallas_call x1, Pallas kernels, run_forecast(): pl.pallas_call(forecast_kernel, out_shape=(jax.ShapeDtypeStruct((rows * n...  22.9 us
    all_to_all x1, waiting for transfers between devices, per_device(): told = lax.all_to_all(notes, ('ens', 'lat', 'lon'), 0, 0, tiled=True)  8.2 us
    ppermute x1, starting transfers between devices, per_device(): north = lax.ppermute(last_rows, 'lat', down_lat)  5.1 us
    all_to_all x1, starting transfers between devices, per_device(): told = lax.all_to_all(notes, ('ens', 'lat', 'lon'), 0, 0, tiled=True)  4.22 us
    unnamed x24, local copies, waits for them, and re-layouts  3.34 us
    pallas_call x1, Pallas kernels, run_analysis(): pl.pallas_call(analysis_kernel, out_shape=jax.ShapeDtypeStruct(shape, BF1...  2.59 us
    ppermute x1, waiting for transfers between devices, per_device(): south = lax.ppermute(first_rows, 'lat', up_lat)  2.23 us
    pallas_call x1, Pallas kernels, edge_columns(): pl.pallas_call(columns_kernel, out_shape=(out, out), scratch_shapes=[pltp...  1.92 us
  transfers between devices with their start and end apart: 6, of which 3 were waited for; matrix products, arithmetic and copies ran while one was open for 8% of the time, Pallas kernels for 0%

profile of v1, /device:TPU:0, one launch (start us, length us, event | category | flops | bytes accessed | tf_op | source)
XLA Modules:
  0.0 62.0 jit_solution(7154982780314566016)
XLA Ops:
  0.0 1.6 %edge_rows.1 = (bf16[48,128]{1,0:T(8,128)(2,1)}, bf16[48,128]{1,0:T(8,128)(2,1)}) custom-call(bf16[24,64,128]{2,1,0:T(8,128)(2,1)} %bitcast.19, bf16[24,64,128]{2,1,0:T(8,128)(2,1)} %bitcast.20), custom_call_target="tpu_custom_call" | custom-call | tf_op jit(solution)/shard_map/edge_rows/pallas_call | solution.py:36
  1.6 5.1 %collective-permute-start = (bf16[48,128]{1,0:T(8,128)(2,1)}, bf16[48,128]{1,0:T(8,128)(2,1)S(1)}, u32[]{:S(2)}, u32[]{:S(2)}) collective-permute-start(bf16[48,128]{1,0:T(8,128)(2,1)} %get-tuple-element.47), channel_id=1, source_target_pairs={{0,4},{4,8},{8,12},{1,5},{5,9},{9,13},{2,6},{6,10},{10,14},{3,7},{... | collective-permute-start | bytes 36872 | tf_op jit(solution)/shard_map/ppermute | solution.py:395
  6.7 1.3 %collective-permute-start.1 = (bf16[48,128]{1,0:T(8,128)(2,1)}, bf16[48,128]{1,0:T(8,128)(2,1)S(1)}, u32[]{:S(2)}, u32[]{:S(2)}) collective-permute-start(bf16[48,128]{1,0:T(8,128)(2,1)} %get-tuple-element.48), channel_id=1, source_target_pairs={{4,0},{8,4},{12,8},{5,1},{9,5},{13,9},{6,2},{10,6},{14,10},{7,3},{... | collective-permute-start | bytes 36872 | tf_op jit(solution)/shard_map/ppermute | solution.py:396
  8.0 0.6 fusion.5.spot_ref
  8.7 0.6 fusion.1.out_w_ref
  9.5 0.7 %add_select_fusion.lane_ref = s32[256,1]{1,0:T(8,128)} fusion(s32[256,1]{1,0:T(8,128)S(1)} %copy.11), kind=kLoop, calls=%fused_computation | loop fusion | flops 2816 | bytes 2048 | tf_op jit(solution)/shard_map/jit(remainder)/select_n | solution.py:403
  10.3 2.2 %collective-permute-done.1.south_ref = bf16[48,128]{1,0:T(8,128)(2,1)S(1)} collective-permute-done((bf16[48,128]{1,0:T(8,128)(2,1)}, bf16[48,128]{1,0:T(8,128)(2,1)S(1)}, u32[]{:S(2)}, u32[]{:S(2)}) %collective-permute-start.1) | collective-permute-done | bytes 12320 | tf_op jit(solution)/shard_map/ppermute | solution.py:396
  12.5 0.6 copy-done.4
  13.1 1.9 %edge_columns.1 = (bf16[48,128]{1,0:T(8,128)(2,1)}, bf16[48,128]{1,0:T(8,128)(2,1)}) custom-call(bf16[24,64,128]{2,1,0:T(8,128)(2,1)} %bitcast.21, bf16[48,128]{1,0:T(8,128)(2,1)} %copy-done.3, bf16[48,128]{1,0:T(8,128)(2,1)} %copy-done.4), custom_call_target="tpu_custom_call" | custom-call | tf_op jit(solution)/shard_map/edge_columns/pallas_call | solution.py:85
  15.1 0.5 collective-permute-start.2
  15.6 0.6 add_convert_fusion.north_in_ref.inside_ref
  16.8 0.8 %copy.10 = bf16[240,256]{0,1:T(8,128)(2,1)} copy(bf16[240,256]{1,0:T(8,128)(2,1)S(1)} %bitcast.25) | data formatting | bytes 245760 | tf_op jit(solution)/shard_map/reshape | solution.py:371
  17.6 0.9 %collective-permute-done.2.from_left_ref = bf16[48,128]{1,0:T(8,128)(2,1)S(1)} collective-permute-done((bf16[48,128]{1,0:T(8,128)(2,1)}, bf16[48,128]{1,0:T(8,128)(2,1)S(1)}, u32[]{:S(2)}, u32[]{:S(2)}) %collective-permute-start.2) | collective-permute-done | bytes 12320 | tf_op jit(solution)/shard_map/ppermute | solution.py:398
  18.5 0.6 copy-done.7
  19.1 22.9 %forecast.1 = (bf16[1536,128]{1,0:T(8,128)(2,1)}, f32[8,256]{1,0:T(8,128)}) custom-call(s32[256]{0:T(256)} %fusion.5.spot_ref, s32[2]{0:T(128)} %add_convert_fusion.north_in_ref.inside_ref, s32[2]{0:T(128)} %add_convert_fusion.north_in_ref.inside_ref, bf16[24,64,128]{2,1,0:T(8,128)(2,1)} %bitcast.22, bf16[48,128]{1,0:T(8,128)(2,1)} %copy-done.3, ...), custom_call_target="tpu_custom_call" | custom-call | tf_op jit(solution)/shard_map/forecast/pallas_call | solution.py:228
  42.0 1.5 %collective-permute-start.4 = (bf16[1536,128]{1,0:T(8,128)(2,1)}, bf16[1536,128]{1,0:T(8,128)(2,1)S(1)}, u32[]{:S(2)}, u32[]{:S(2)}) collective-permute-start(bf16[1536,128]{1,0:T(8,128)(2,1)} %get-tuple-element.52.mine_ref), channel_id=1, source_target_pairs={{0,16},{16,0},{1,17},{17,1},{2,18},{18,2},{3,19},{19,3},{4,20},{20... | collective-permute-start | bytes 1179656 | tf_op jit(solution)/shard_map/ppermute | solution.py:434
  43.5 0.7 %copy-done.10 = f32[1,1,256]{2,1,0:T(1,128)S(1)} copy-done((f32[1,1,256]{2,1,0:T(1,128)S(1)}, f32[1,1,256]{2,1,0:T(1,128)}, u32[]{:S(2)}) %copy-start.10) | copy-done | bytes 1048
  44.2 0.7 %slice.78 = f32[1,256]{1,0:T(1,128)S(1)} slice(f32[8,256]{1,0:T(8,128)} %get-tuple-element.51), slice={[0:1], [0:256]} | slice | bytes 2048 | tf_op jit(solution)/shard_map/slice | solution.py:427
  44.9 0.7 %copy-done.11 = f32[1,1,256]{2,1,0:T(1,128)S(1)} copy-done((f32[1,1,256]{2,1,0:T(1,128)S(1)}, f32[1,1,256]{2,1,0:T(1,128)}, u32[]{:S(2)}) %copy-start.11) | copy-done | bytes 1048
  45.6 0.7 %broadcast_in_dim.4 = f32[32,8,128]{2,1,0:T(8,128)} broadcast(f32[8,128]{1,0:T(8,128)S(1)} %pad_maximum_fusion.2), dimensions={1,2} | broadcast | bytes 135168 | tf_op jit(solution)/shard_map/broadcast_in_dim | solution.py:430
  46.2 4.2 %all-to-all-start = ((f32[32,8,128]{2,1,0:T(8,128)}), f32[32,8,128]{2,1,0:T(8,128)S(1)}, u32[]{:S(2)}, u32[]{:S(2)}) async-start(f32[32,8,128]{2,1,0:T(8,128)} %broadcast_in_dim.4), calls=%async_computation | async-start | bytes 262144 | tf_op jit(solution)/shard_map/all_to_all | solution.py:431
  50.5 8.2 %all-to-all-done = f32[32,8,128]{2,1,0:T(8,128)S(1)} async-done(((f32[32,8,128]{2,1,0:T(8,128)}), f32[32,8,128]{2,1,0:T(8,128)S(1)}, u32[]{:S(2)}, u32[]{:S(2)}) %all-to-all-start) | async-done | bytes 131104 | tf_op jit(solution)/shard_map/all_to_all | solution.py:431
  58.7 0.6 %copy-done = f32[32,8,128]{2,1,0:T(8,128)} copy-done((f32[32,8,128]{2,1,0:T(8,128)}, f32[32,8,128]{2,1,0:T(8,128)S(1)}, u32[]{:S(2)}) %copy-start) | copy-done | bytes 131096
  59.4 2.6 %analysis.1 = bf16[24,64,128]{2,1,0:T(8,128)(2,1)} custom-call(s32[1]{0:T(128)} %bitcast.me_ref, f32[2,16,8,128]{3,2,1,0:T(8,128)} %bitcast.23, bf16[1536,128]{1,0:T(8,128)(2,1)} %get-tuple-element.52.mine_ref, bf16[1536,128]{1,0:T(8,128)(2,1)} %copy-done.1), custom_call_target="tpu_custom_call" | custom-call | tf_op jit(solution)/shard_map/analysis/pallas_call | solution.py:315
  (37 shorter events, 0.4 us)
Async XLA Ops:
  0.0 8.0 %copy-start.8 = (s32[1,1,256]{2,1,0:T(1,128)S(1)}, s32[1,1,256]{2,1,0:T(1,128)}, u32[]{:S(2)}) copy-start(s32[1,1,256]{2,1,0:T(1,128)} %param.18) | copy-start | bytes 3076
  0.0 8.7 %copy-start.9 = (f32[256]{0:T(256)S(1)}, f32[256]{0:T(256)}, u32[]{:S(2)}) copy-start(f32[256]{0:T(256)} %param.16) | copy-start | bytes 3076
  0.0 9.3 %copy-start.2 = (bf16[216,256]{1,0:T(8,128)(2,1)S(1)}, bf16[216,256]{1,0:T(8,128)(2,1)}, u32[]{:S(2)}) copy-start(bf16[216,256]{1,0:T(8,128)(2,1)} %param.15) | copy-start | bytes 331780
  1.6 7.1 %copy-start.5 = (bf16[256,24]{0,1:T(8,128)(2,1)S(1)}, bf16[256,24]{0,1:T(8,128)(2,1)}, u32[]{:S(2)}) copy-start(bf16[256,24]{0,1:T(8,128)(2,1)} %param.17) | copy-start | bytes 36868
  1.6 8.7 %collective-permute-start = (bf16[48,128]{1,0:T(8,128)(2,1)}, bf16[48,128]{1,0:T(8,128)(2,1)S(1)}, u32[]{:S(2)}, u32[]{:S(2)}) collective-permute-start(bf16[48,128]{1,0:T(8,128)(2,1)} %get-tuple-element.47), channel_id=1, source_target_pairs={{0,4},{4,8},{8,12},{1,5},{5,9},{9,13},{2,6},{6,10},{10,14},{3,7},{... | collective-permute-start | bytes 36872 | tf_op jit(solution)/shard_map/ppermute | solution.py:395
  6.7 5.8 %collective-permute-start.1 = (bf16[48,128]{1,0:T(8,128)(2,1)}, bf16[48,128]{1,0:T(8,128)(2,1)S(1)}, u32[]{:S(2)}, u32[]{:S(2)}) collective-permute-start(bf16[48,128]{1,0:T(8,128)(2,1)} %get-tuple-element.48), channel_id=1, source_target_pairs={{4,0},{8,4},{12,8},{5,1},{9,5},{13,9},{6,2},{10,6},{14,10},{7,3},{... | collective-permute-start | bytes 36872 | tf_op jit(solution)/shard_map/ppermute | solution.py:396
  10.3 2.2 %copy-start.3 = (bf16[48,128]{1,0:T(8,128)(2,1)}, bf16[48,128]{1,0:T(8,128)(2,1)S(1)}, u32[]{:S(2)}) copy-start(bf16[48,128]{1,0:T(8,128)(2,1)S(1)} %collective-permute-done.north_ref) | copy-start | bytes 36868
  12.5 0.6 copy-start.4
  15.1 2.5 %collective-permute-start.3 = (bf16[48,128]{1,0:T(8,128)(2,1)}, bf16[48,128]{1,0:T(8,128)(2,1)S(1)}, u32[]{:S(2)}, u32[]{:S(2)}) collective-permute-start(bf16[48,128]{1,0:T(8,128)(2,1)} %get-tuple-element.49.own_left_ref), channel_id=1, source_target_pairs={{1,0},{2,1},{3,2},{0,3},{5,4},{6,5},{7,6},{4,7},{9,8},{10,9},{11,1... | collective-permute-start | bytes 36872 | tf_op jit(solution)/shard_map/ppermute | solution.py:399
  15.1 3.4 %collective-permute-start.2 = (bf16[48,128]{1,0:T(8,128)(2,1)}, bf16[48,128]{1,0:T(8,128)(2,1)S(1)}, u32[]{:S(2)}, u32[]{:S(2)}) collective-permute-start(bf16[48,128]{1,0:T(8,128)(2,1)} %get-tuple-element.50.own_right_ref), channel_id=1, source_target_pairs={{0,1},{1,2},{2,3},{3,0},{4,5},{5,6},{6,7},{7,4},{8,9},{9,10},{10,1... | collective-permute-start | bytes 36872 | tf_op jit(solution)/shard_map/ppermute | solution.py:398
  17.6 0.9 %copy-start.6 = (bf16[48,128]{1,0:T(8,128)(2,1)}, bf16[48,128]{1,0:T(8,128)(2,1)S(1)}, u32[]{:S(2)}) copy-start(bf16[48,128]{1,0:T(8,128)(2,1)S(1)} %collective-permute-done.3.from_right_ref) | copy-start | bytes 36868
  18.5 0.6 copy-start.7
  42.0 16.7 %collective-permute-start.4 = (bf16[1536,128]{1,0:T(8,128)(2,1)}, bf16[1536,128]{1,0:T(8,128)(2,1)S(1)}, u32[]{:S(2)}, u32[]{:S(2)}) collective-permute-start(bf16[1536,128]{1,0:T(8,128)(2,1)} %get-tuple-element.52.mine_ref), channel_id=1, source_target_pairs={{0,16},{16,0},{1,17},{17,1},{2,18},{18,2},{3,19},{19,3},{4,20},{20... | collective-permute-start | bytes 1179656 | tf_op jit(solution)/shard_map/ppermute | solution.py:434
  43.5 0.7 %copy-start.10 = (f32[1,1,256]{2,1,0:T(1,128)S(1)}, f32[1,1,256]{2,1,0:T(1,128)}, u32[]{:S(2)}) copy-start(f32[1,1,256]{2,1,0:T(1,128)} %param.21) | copy-start | bytes 3076
  44.9 0.7 %copy-start.11 = (f32[1,1,256]{2,1,0:T(1,128)S(1)}, f32[1,1,256]{2,1,0:T(1,128)}, u32[]{:S(2)}) copy-start(f32[1,1,256]{2,1,0:T(1,128)} %param.20) | copy-start | bytes 3076
  46.2 12.4 %all-to-all-start = ((f32[32,8,128]{2,1,0:T(8,128)}), f32[32,8,128]{2,1,0:T(8,128)S(1)}, u32[]{:S(2)}, u32[]{:S(2)}) async-start(f32[32,8,128]{2,1,0:T(8,128)} %broadcast_in_dim.4), calls=%async_computation | async-start | bytes 262144 | tf_op jit(solution)/shard_map/all_to_all | solution.py:431
  58.7 0.7 %copy-start = (f32[32,8,128]{2,1,0:T(8,128)}, f32[32,8,128]{2,1,0:T(8,128)S(1)}, u32[]{:S(2)}) copy-start(f32[32,8,128]{2,1,0:T(8,128)S(1)} %all-to-all-done) | copy-start | bytes 393220
  58.7 0.8 %copy-start.1 = (bf16[1536,128]{1,0:T(8,128)(2,1)}, bf16[1536,128]{1,0:T(8,128)(2,1)S(1)}, u32[]{:S(2)}) copy-start(bf16[1536,128]{1,0:T(8,128)(2,1)S(1)} %collective-permute-done.4.other_ref) | copy-start | bytes 1179652

commit v2 on v1

--- a/solution.py
+++ b/solution.py
@@ -14,6 +14,7 @@
 F32 = jnp.float32
 BF16 = jnp.bfloat16
 PAD = 8
+SMALL = 4 << 20
 
 
 def lanes_of(shape):
@@ -43,12 +44,14 @@
         ],
         out_specs=[pl.BlockSpec((2 * nvar, cols), lambda i: (0, 0))] * 2,
         scratch_shapes=[pltpu.VMEM((nvar * tile, cols), F32)],
+        compiler_params=pltpu.CompilerParams(vmem_limit_bytes=SMALL),
         name="edge_rows",
     )(x, x)
 
 
-def columns_kernel(x_ref, north_ref, south_ref, left_ref, right_ref, stage):
+def spread_kernel(x_ref, taps_ref, own_ref, stage, xf):
     nvar, rows, cols = x_ref.shape
+    block = 3 * nvar + PAD
     wanted = (0, 1, cols - 2, cols - 1)
     k = lax.broadcasted_iota(jnp.int32, (8, cols), 0)
     lane = lanes_of((8, cols))
@@ -58,48 +61,82 @@
     pick = pick.astype(BF16)
     per = cols // rows
     flat = x_ref[...].reshape(nvar * rows, cols)
+    xf[...] = flat.astype(F32)
     taken = lax.dot_general(pick, flat, (((1,), (1,)), ((), ())), preferred_element_type=F32)
     for v in range(nvar):
-        block = taken[:, (v // per) * cols : (v // per + 1) * cols]
+        part = taken[:, (v // per) * cols : (v // per + 1) * cols]
         shift = (2 - (v % per) * rows) % cols
-        stage[8 * v : 8 * v + 8, :] = pltpu.roll(block, shift, 1)
-    lane = lanes_of((nvar, cols))
-    halo = []
-    for ref, first in ((north_ref, 0), (south_ref, rows + 2)):
-        for i in range(2):
-            halo.append((first + i, ref[i * nvar : (i + 1) * nvar, :].astype(F32)))
-    outs = []
-    for i, c in enumerate(wanted):
-        column = stage[pl.ds(i, nvar, stride=8), :]
-        column = jnp.where(lane < rows + 2, column, 0.0)
-        for at, row in halo:
-            column = jnp.where(lane == at, pltpu.roll(row, (at - c) % cols, 1), column)
-        outs.append(column)
-    left_ref[...] = jnp.concatenate(outs[:2], axis=0).astype(BF16)
-    right_ref[...] = jnp.concatenate(outs[2:], axis=0).astype(BF16)
-
-
-def edge_columns(x, north, south):
+        stage[8 * v : 8 * v + 8, :] = pltpu.roll(part, shift, 1)
+    for i in range(len(wanted)):
+        own_ref[i * nvar : (i + 1) * nvar, :] = stage[pl.ds(i, nvar, stride=8), :]
+    ones = jnp.ones((PAD, cols), F32)
+
+    def fill(r, carry):
+        row = xf[pl.ds(r, nvar, stride=rows), :]
+        tap = jnp.concatenate([row, pltpu.roll(row, 1, 1), pltpu.roll(row, cols - 1, 1), ones], axis=0)
+        at = pl.multiple_of(r * block, 16)
+        taps_ref[pl.ds(at, block), :] = tap.astype(BF16)
+        return carry
+
+    lax.fori_loop(0, rows, fill, 0, unroll=4)
+
+
+def spread(x):
     nvar, rows, cols = x.shape
+    block = 3 * nvar + PAD
+    return pl.pallas_call(
+        spread_kernel,
+        out_shape=(
+            jax.ShapeDtypeStruct((rows * block, cols), BF16),
+            jax.ShapeDtypeStruct((4 * nvar, cols), F32),
+        ),
+        scratch_shapes=[pltpu.VMEM((8 * nvar, cols), F32), pltpu.VMEM((nvar * rows, cols), F32)],
+        compiler_params=pltpu.CompilerParams(vmem_limit_bytes=SMALL),
+        cost_estimate=pl.CostEstimate(flops=10**8, bytes_accessed=4 * 10**6, transcendentals=0),
+        name="spread",
+    )(x)
+
+
+def edge_columns(own, north, south, rows):
+    nvar, cols = own.shape[0] // 4, own.shape[1]
+    wanted = (0, 1, cols - 2, cols - 1)
+
+    def kernel(own_ref, north_ref, south_ref, left_ref, right_ref):
+        lane = lanes_of((nvar, cols))
+        halo = []
+        for ref, first in ((north_ref, 0), (south_ref, rows + 2)):
+            for i in range(2):
+                halo.append((first + i, ref[i * nvar : (i + 1) * nvar, :].astype(F32)))
+        outs = []
+        for i, c in enumerate(wanted):
+            column = own_ref[i * nvar : (i + 1) * nvar, :]
+            column = jnp.where(lane < rows + 2, column, 0.0)
+            for at, row in halo:
+                column = jnp.where(lane == at, pltpu.roll(row, (at - c) % cols, 1), column)
+            outs.append(column)
+        left_ref[...] = jnp.concatenate(outs[:2], axis=0).astype(BF16)
+        right_ref[...] = jnp.concatenate(outs[2:], axis=0).astype(BF16)
+
     out = jax.ShapeDtypeStruct((2 * nvar, cols), BF16)
     return pl.pallas_call(
-        columns_kernel,
+        kernel,
         out_shape=(out, out),
-        scratch_shapes=[pltpu.VMEM((8 * nvar, cols), F32)],
+        compiler_params=pltpu.CompilerParams(vmem_limit_bytes=SMALL),
         name="edge_columns",
-    )(x, north, south)
+    )(own, north, south)
 
 
 def gelu2(pre):
-    inner = pre * (GELU_A + GELU_B * (pre * pre))
+    pre = pre.astype(BF16)
+    inner = pre * (jnp.asarray(GELU_A, BF16) + jnp.asarray(GELU_B, BF16) * (pre * pre))
     return pre + pre * jnp.tanh(inner)
 
 
 def forecast_kernel(
     spot_ref,
     north_in_ref,
-    inside_ref,
-    x_ref,
+    count_ref,
+    taps_ref,
     north_ref,
     south_ref,
     own_left_ref,
@@ -109,16 +146,18 @@
     conv_ref,
     out_w_ref,
     lane_ref,
+    value_ref,
+    weight_ref,
     forecast_ref,
-    picked_ref,
-    xf,
+    notes_ref,
     first,
     second,
     final,
     seen,
 ):
-    nvar, rows, cols = x_ref.shape
+    nvar, cols = north_ref.shape[0] // 2, north_ref.shape[1]
     block = 3 * nvar + PAD
+    rows = taps_ref.shape[0] // block
     deep = 3 * block
     lane = lanes_of((nvar, cols))
     ones = jnp.ones((PAD, cols), F32)
@@ -132,11 +171,10 @@
 
     def advance(patches, centre):
         pre = jnp.dot(conv_ref[...], patches, preferred_element_type=F32)
-        hidden = gelu2(pre).astype(BF16)
+        hidden = gelu2(pre)
         change = jnp.dot(out_w_ref[...], hidden, preferred_element_type=F32)
         return (centre + change[:nvar]).astype(BF16).astype(F32)
 
-    xf[...] = x_ref[...].reshape(nvar * rows, cols).astype(F32)
     from_left = from_left_ref[...].astype(F32)
     from_right = from_right_ref[...].astype(F32)
     own_left = own_left_ref[...].astype(F32)
@@ -150,10 +188,20 @@
             row = ref[i * nvar : (i + 1) * nvar, :].astype(F32)
             first[(start + i) * block : (start + i + 1) * block, :] = tap_rows(row, west, east, start + i)
 
+    group = lax.broadcasted_iota(jnp.int32, (block, cols), 0)
+    wide = lanes_of((block, cols))
+    is_left = (group >= nvar) & (group < 2 * nvar) & (wide == 0)
+    is_right = (group >= 2 * nvar) & (group < 3 * nvar) & (wide == cols - 1)
+    fix = jnp.where(is_left | is_right, 1.0, 0.0).astype(BF16) > 0
+    nothing = jnp.zeros((nvar, cols), F32)
+    source = jnp.concatenate([nothing, west, pltpu.roll(east, cols - 1, 1), jnp.zeros((PAD, cols), F32)], axis=0)
+    source = source.astype(BF16)
+
     def fill(r, carry):
-        row = xf[pl.ds(r, nvar, stride=rows), :]
-        at = pl.multiple_of((r + 2) * block, 16)
-        first[pl.ds(at, block), :] = tap_rows(row, west, east, r + 2)
+        at = pl.multiple_of(r * block, 16)
+        mine = pltpu.roll(source, cols - 2 - r, 1)
+        to = pl.multiple_of((r + 2) * block, 16)
+        first[pl.ds(to, block), :] = jnp.where(fix, mine, taps_ref[pl.ds(at, block), :])
         return carry
 
     lax.fori_loop(0, rows, fill, 0, unroll=4)
@@ -193,7 +241,7 @@
             second[pl.ds(at, block), :] = tap_rows(row, mid_west, mid_east, m + 1)
         return carry
 
-    lax.fori_loop(0, rows // 2 + 1, first_step, 0, unroll=3)
+    lax.fori_loop(0, rows // 2 + 1, first_step, 0, unroll=11)
 
     def second_step(j, carry):
         both = pair(second, 2 * j)
@@ -203,45 +251,53 @@
         forecast_ref[pl.ds(at, 2 * nvar), :] = both.astype(BF16)
         return carry
 
-    lax.fori_loop(0, rows // 2, second_step, 0, unroll=4)
+    lax.fori_loop(0, rows // 2, second_step, 0, unroll=8)
 
     def look(o, carry):
         seen[pl.ds(o, 1), :] = final[pl.ds(spot_ref[o], 1), :]
         return carry
 
     slots = seen.shape[0]
-    lax.fori_loop(0, slots, look, 0, unroll=8)
+    lax.fori_loop(0, slots, look, 0, unroll=16)
     masked = jnp.where(lane_ref[...] == lanes_of((slots, cols)), seen[...], 0.0).astype(BF16)
     values = lax.dot_general(
         jnp.ones((8, cols), BF16), masked, (((1,), (1,)), ((), ())), preferred_element_type=F32
     )
-    picked_ref[...] = values
-    del inside_ref
-
-
-def run_forecast(spot, inside, x, north, south, own_left, own_right, from_left, from_right, conv, out_w, lane):
-    nvar, rows, cols = x.shape
+    fold = value_ref.shape[0]
+    live = lanes_of((fold, cols)) + cols * lax.broadcasted_iota(jnp.int32, (fold, cols), 0) < count_ref[0]
+    note = [values[0:1, i * cols : (i + 1) * cols] for i in range(fold)]
+    note += [value_ref[...], jnp.where(live, weight_ref[...], 0.0)]
+    note.append(jnp.zeros((notes_ref.shape[1] - 3 * fold, cols), F32))
+    note = jnp.concatenate(note, axis=0)
+    for d in range(notes_ref.shape[0]):
+        notes_ref[d] = note
+
+
+def run_forecast(spot, inside, count, taps, north, south, own_left, own_right, from_left, from_right, conv, out_w, lane, value, weight, devices):
+    nvar, cols = north.shape[0] // 2, north.shape[1]
     slots = spot.shape[0]
     block = 3 * nvar + PAD
+    rows = taps.shape[0] // block
+    note_rows = -(-3 * value.shape[0] // 8) * 8
     smem = pl.BlockSpec(memory_space=pltpu.SMEM)
     vmem = pl.BlockSpec(memory_space=pltpu.VMEM)
     return pl.pallas_call(
         forecast_kernel,
         out_shape=(
             jax.ShapeDtypeStruct((rows * nvar, cols), BF16),
-            jax.ShapeDtypeStruct((8, slots), F32),
+            jax.ShapeDtypeStruct((devices, note_rows, cols), F32),
         ),
-        in_specs=[smem, smem, smem] + [vmem] * 10,
+        in_specs=[smem, smem, smem] + [vmem] * 12,
         out_specs=(vmem, vmem),
         scratch_shapes=[
-            pltpu.VMEM((nvar * rows, cols), F32),
             pltpu.VMEM(((rows + 4) * block, cols), BF16),
             pltpu.VMEM(((rows + 2) * block, cols), BF16),
             pltpu.VMEM((rows * nvar, cols), F32),
             pltpu.VMEM((slots, cols), F32),
         ],
+        compiler_params=pltpu.CompilerParams(vmem_limit_bytes=16 << 20),
         name="forecast",
-    )(spot, inside, inside, x, north, south, own_left, own_right, from_left, from_right, conv, out_w, lane)
+    )(spot, inside, count, taps, north, south, own_left, own_right, from_left, from_right, conv, out_w, lane, value, weight)
 
 
 def pair_weights(gram, proj):
@@ -318,6 +374,7 @@
         in_specs=[pl.BlockSpec(memory_space=pltpu.SMEM), vmem, vmem, vmem],
         out_specs=vmem,
         scratch_shapes=[pltpu.VMEM((nvar * rows, cols), F32)],
+        compiler_params=pltpu.CompilerParams(vmem_limit_bytes=8 << 20),
         name="analysis",
     )(me, told, mine, other)
 
@@ -360,17 +417,36 @@
 
 def packed_weights(conv_weight, conv_bias, out_weight, nvar):
     hid = conv_bias.shape[0]
-    taps = conv_weight.reshape(3, 3, nvar, hid)
-    taps = jnp.stack([taps[:, 1], taps[:, 0], taps[:, 2]], axis=1).reshape(3, 3 * nvar, hid)
-    high = conv_bias.astype(BF16)
-    rest = conv_bias - high.astype(F32)
-    middle = rest.astype(BF16)
-    low = (rest - middle.astype(F32)).astype(BF16)
-    bias = jnp.zeros((3, PAD, hid), BF16)
-    bias = bias.at[1, 0].set(high).at[1, 1].set(middle).at[1, 2].set(low)
-    conv = jnp.concatenate([taps, bias], axis=1).reshape(-1, hid).T
-    half = (out_weight.astype(F32) * 0.5).astype(BF16).T
-    return conv, half
+    block = 3 * nvar + PAD
+
+    def kernel(conv_ref, bias_ref, out_ref, packed_ref, half_ref):
+        bias = bias_ref[...]
+        high = bias.astype(BF16).astype(F32)
+        middle = (bias - high).astype(BF16).astype(F32)
+        low = (bias - high - middle).astype(BF16).astype(F32)
+        rest = jnp.zeros((PAD - 3, hid), F32)
+        pieces = []
+        for a in range(3):
+            for b in (1, 0, 2):
+                at = (3 * a + b) * nvar
+                pieces.append(conv_ref[at : at + nvar, :].astype(F32))
+            if a == 1:
+                pieces.append(jnp.concatenate([high, middle, low, rest], axis=0))
+            else:
+                pieces.append(jnp.zeros((PAD, hid), F32))
+        packed_ref[...] = jnp.concatenate(pieces, axis=0).T.astype(BF16)
+        half_ref[...] = (out_ref[...].astype(F32) * 0.5).astype(BF16)
+
+    return pl.pallas_call(
+        kernel,
+        out_shape=(
+            jax.ShapeDtypeStruct((hid, 3 * block), BF16),
+            jax.ShapeDtypeStruct((nvar, hid), BF16),
+        ),
+        compiler_params=pltpu.CompilerParams(vmem_limit_bytes=SMALL),
+        cost_estimate=pl.CostEstimate(flops=10**7, bytes_accessed=10**6, transcendentals=0),
+        name="packed_weights",
+    )(conv_weight, conv_bias[None], out_weight.T)
 
 
 def per_device(
@@ -394,7 +470,8 @@
     first_rows, last_rows = edge_rows(x)
     north = lax.ppermute(last_rows, "lat", down_lat)
     south = lax.ppermute(first_rows, "lat", up_lat)
-    own_left, own_right = edge_columns(x, north, south)
+    taps, own = spread(x)
+    own_left, own_right = edge_columns(own, north, south, rows)
     from_left = lax.ppermute(own_right, "lon", right_lon)
     from_right = lax.ppermute(own_left, "lon", left_lon)
 
@@ -404,10 +481,13 @@
     spot = jnp.clip(row * nvar + var, 0, rows * nvar - 1)
     here = lax.axis_index("lat")
     inside = jnp.stack([here > 0, here < n_lat - 1]).astype(jnp.int32)
-    forecast, picked = run_forecast(
+    fold = (slots.shape[0] // cols, cols)
+    devices = n_ens * n_lat * n_lon
+    forecast, notes = run_forecast(
         spot,
         inside,
-        x,
+        obs_count.reshape(1),
+        taps,
         north,
         south,
         own_left,
@@ -417,19 +497,12 @@
         conv,
         out_w,
         lane[:, None],
+        obs_value.reshape(fold),
+        obs_weight.reshape(fold),
+        devices,
     )
-
-    count = slots.shape[0]
-    live = (jnp.arange(count, dtype=jnp.int32) < obs_count.reshape(())).astype(F32)
-    weight = obs_weight.reshape(-1) * live
-    fold = (count // cols, cols)
-    note = jnp.concatenate(
-        [picked[0].reshape(fold), obs_value.reshape(fold), weight.reshape(fold), jnp.zeros(fold, F32)], axis=0
-    )
-    devices = n_ens * n_lat * n_lon
-    notes = jnp.broadcast_to(note[None], (devices,) + note.shape)
     told = lax.all_to_all(notes, ("ens", "lat", "lon"), 0, 0, tiled=True)
-    told = told.reshape(n_ens, n_lat * n_lon, *note.shape)
+    told = told.reshape(n_ens, n_lat * n_lon, *notes.shape[1:])
     if n_ens == 2:
         other = lax.ppermute(forecast, "ens", [(0, 1), (1, 0)])
         me = lax.axis_index("ens").reshape(1)

time: 62.4 us -> 52.3 us (0.84)
  Pallas kernels: 29 us -> 23.1 us
  local copies, waits for them, and re-layouts: 5.7 us -> 2.83 us
  other arithmetic: 2.57 us -> 0.83 us
  starting transfers between devices: 12.6 us -> 14 us
  waiting for transfers between devices: 11.3 us -> 10.4 us
    pallas_call x1, Pallas kernels: 22.9 us -> 19.5 us  [run_forecast(): pl.pallas_call(forecast_kernel, out_shape=(jax.ShapeDtypeStruct((rows * n...]
    ppermute x1, waiting for transfers between devices: 2.23 us -> 0.01 us  [per_device(): south = lax.ppermute(first_rows, 'lat', up_lat)]
    pallas_call x1, Pallas kernels: 1.62 us -> 0.05 us  [edge_rows(): pl.pallas_call(rows_kernel, out_shape=(out, out), grid=(1,), in_specs=[pl...]
    unnamed x24 -> x14, local copies, waits for them, and re-layouts: 3.34 us -> 2.02 us
    pallas_call x1, Pallas kernels: 2.59 us -> 1.41 us  [run_analysis(): pl.pallas_call(analysis_kernel, out_shape=jax.ShapeDtypeStruct(shape, BF1...]
    all_to_all x1, starting transfers between devices: 4.22 us -> 5.37 us  [per_device(): told = lax.all_to_all(notes, ('ens', 'lat', 'lon'), 0, 0, tiled=True)]
    ppermute x1, waiting for transfers between devices: 0.88 us -> 1.71 us  [per_device(): from_left = lax.ppermute(own_right, 'lon', right_lon)]
    reshape x1 -> x0, local copies, waits for them, and re-layouts: 0.76 us -> none  [packed_weights(): conv = jnp.concatenate([taps, bias], axis=1).reshape(-1, hid).T]
  transfers between devices with their start and end apart: 6 -> 6, of which waited for: 3 -> 3; matrix products, arithmetic and copies ran while one was open for 8% -> 3% of each run, Pallas kernels for 0% -> 4%
where the time goes in v2:
time: 52.3 us; the launch traced here: 52 us
  Pallas kernels  23.1 us (44%)
  starting transfers between devices  14 us (27%)
  waiting for transfers between devices  10.4 us (20%)
  local copies, waits for them, and re-layouts  2.83 us (5%)
  other arithmetic  0.83 us (2%)
  between operations  0.79 us (2%)
    pallas_call x1, Pallas kernels, run_forecast(): pl.pallas_call(forecast_kernel, out_shape=(jax.ShapeDtypeStruct((rows * n...  19.5 us
    all_to_all x1, waiting for transfers between devices, per_device(): told = lax.all_to_all(notes, ('ens', 'lat', 'lon'), 0, 0, tiled=True)  8.2 us
    all_to_all x1, starting transfers between devices, per_device(): told = lax.all_to_all(notes, ('ens', 'lat', 'lon'), 0, 0, tiled=True)  5.37 us
    ppermute x1, starting transfers between devices, per_device(): north = lax.ppermute(last_rows, 'lat', down_lat)  5.09 us
    unnamed x14, local copies, waits for them, and re-layouts  2.02 us
    pallas_call x1, Pallas kernels, spread(): pl.pallas_call(spread_kernel, out_shape=(jax.ShapeDtypeStruct((rows * blo...  1.93 us
    ppermute x1, waiting for transfers between devices, per_device(): from_left = lax.ppermute(own_right, 'lon', right_lon)  1.71 us
    ppermute x1, starting transfers between devices, per_device(): other = lax.ppermute(forecast, 'ens', [(0, 1), (1, 0)])  1.52 us
  transfers between devices with their start and end apart: 6, of which 3 were waited for; matrix products, arithmetic and copies ran while one was open for 3% of the time, Pallas kernels for 4%

profile of v2, /device:TPU:0, one launch (start us, length us, event | category | flops | bytes accessed | tf_op | source)
XLA Modules:
  0.0 52.0 jit_solution(9640305749740795812)
XLA Ops:
  0.0 1.0 %copy-done = bf16[1,24,64,128]{3,2,1,0:T(8,128)(2,1)S(1)} copy-done((bf16[1,24,64,128]{3,2,1,0:T(8,128)(2,1)S(1)}, bf16[1,24,64,128]{3,2,1,0:T(8,128)(2,1)}, u32[]{:S(2)}) %copy-start) | copy-done | bytes 393240
  1.0 0.1 edge_rows.1
  1.1 5.1 %collective-permute-start = (bf16[48,128]{1,0:T(8,128)(2,1)S(1)}, bf16[48,128]{1,0:T(8,128)(2,1)S(1)}, u32[]{:S(2)}, u32[]{:S(2)}) collective-permute-start(bf16[48,128]{1,0:T(8,128)(2,1)S(1)} %get-tuple-element.16), channel_id=1, source_target_pairs={{0,4},{4,8},{8,12},{1,5},{5,9},{9,13},{2,6},{6,10},{10,14},{3,7},{... | collective-permute-start | bytes 36872 | tf_op jit(solution)/shard_map/ppermute | solution.py:471
  6.2 1.3 %collective-permute-start.1 = (bf16[48,128]{1,0:T(8,128)(2,1)S(1)}, bf16[48,128]{1,0:T(8,128)(2,1)S(1)}, u32[]{:S(2)}, u32[]{:S(2)}) collective-permute-start(bf16[48,128]{1,0:T(8,128)(2,1)S(1)} %get-tuple-element.17), channel_id=1, source_target_pairs={{4,0},{8,4},{12,8},{5,1},{9,5},{13,9},{6,2},{10,6},{14,10},{7,3},{... | collective-permute-start | bytes 36872 | tf_op jit(solution)/shard_map/ppermute | solution.py:472
  7.5 0.8 %copy.9 = s32[256,1]{1,0:T(8,128)S(1)} copy(s32[256,1]{0,1:T(1,128)} %bitcast.22) | data formatting | bytes 2048 | tf_op jit(solution)/shard_map/reshape | solution.py:479
  8.3 0.1 add_select_fusion.lane_ref
  8.3 0.7 %fusion.4.spot_ref = s32[256]{0:T(256)S(1)} fusion(s32[256]{0:T(256)} %bitcast.23), kind=kLoop, calls=%fused_computation.18 | loop fusion | flops 9984 | bytes 2048 | tf_op jit(solution)/shard_map/jit(clip)/min | solution.py:481
  9.1 0.0 copy-start.1
  9.1 1.0 %copy-done.1 = bf16[1,24,64,128]{3,2,1,0:T(8,128)(2,1)S(1)} copy-done((bf16[1,24,64,128]{3,2,1,0:T(8,128)(2,1)S(1)}, bf16[1,24,64,128]{3,2,1,0:T(8,128)(2,1)}, u32[]{:S(2)}) %copy-start.1) | copy-done | bytes 393240
  10.1 1.9 %spread.1 = (bf16[5120,128]{1,0:T(8,128)(2,1)S(1)}, f32[96,128]{1,0:T(8,128)S(1)}) custom-call(bf16[24,64,128]{2,1,0:T(8,128)(2,1)S(1)} %bitcast.16), custom_call_target="tpu_custom_call" | custom-call | flops 100000000 | bytes 4000000 | tf_op jit(solution)/shard_map/spread/pallas_call | solution.py:87
  12.0 0.0 collective-permute-done.north_ref
  12.0 0.0 collective-permute-done.1.south_ref
  12.0 0.1 edge_columns.1
  12.1 0.7 %collective-permute-start.3 = (bf16[48,128]{1,0:T(8,128)(2,1)S(1)}, bf16[48,128]{1,0:T(8,128)(2,1)S(1)}, u32[]{:S(2)}, u32[]{:S(2)}) collective-permute-start(bf16[48,128]{1,0:T(8,128)(2,1)S(1)} %get-tuple-element.19.own_left_ref), channel_id=1, source_target_pairs={{1,0},{2,1},{3,2},{0,3},{5,4},{6,5},{7,6},{4,7},{9,8},{10,9},{11,1... | collective-permute-start | bytes 36872 | tf_op jit(solution)/shard_map/ppermute | solution.py:476
  12.8 0.0 collective-permute-start.2
  12.8 0.1 add_convert_fusion.north_in_ref
  13.6 0.1 packed_weights.1
  13.7 0.5 %collective-permute-done.3.from_right_ref = bf16[48,128]{1,0:T(8,128)(2,1)S(1)} collective-permute-done((bf16[48,128]{1,0:T(8,128)(2,1)S(1)}, bf16[48,128]{1,0:T(8,128)(2,1)S(1)}, u32[]{:S(2)}, u32[]{:S(2)}) %collective-permute-start.3) | collective-permute-done | bytes 12320 | tf_op jit(solution)/shard_map/ppermute | solution.py:476
  14.2 1.7 %collective-permute-done.2.from_left_ref = bf16[48,128]{1,0:T(8,128)(2,1)S(1)} collective-permute-done((bf16[48,128]{1,0:T(8,128)(2,1)S(1)}, bf16[48,128]{1,0:T(8,128)(2,1)S(1)}, u32[]{:S(2)}, u32[]{:S(2)}) %collective-permute-start.2) | collective-permute-done | bytes 12320 | tf_op jit(solution)/shard_map/ppermute | solution.py:475
  15.9 19.5 %forecast.1 = (bf16[1536,128]{1,0:T(8,128)(2,1)S(1)}, f32[32,8,128]{2,1,0:T(8,128)}) custom-call(s32[256]{0:T(256)S(1)} %fusion.4.spot_ref, s32[2]{0:T(128)S(1)} %add_convert_fusion.north_in_ref, s32[1]{0:T(128)} %bitcast.13.count_ref, bf16[5120,128]{1,0:T(8,128)(2,1)S(1)} %get-tuple-element.15.taps_ref, bf16[48,128]{1,0:T(8,128)(2,1)S(1)} %collective-permute-done.north_ref, ...), custom_call_target="tpu_custom_call" | custom-call | tf_op jit(solution)/shard_map/forecast/pallas_call | solution.py:284
  35.4 1.5 %collective-permute-start.4 = (bf16[1536,128]{1,0:T(8,128)(2,1)S(1)}, bf16[1536,128]{1,0:T(8,128)(2,1)S(1)}, u32[]{:S(2)}, u32[]{:S(2)}) collective-permute-start(bf16[1536,128]{1,0:T(8,128)(2,1)S(1)} %get-tuple-element.24.mine_ref), channel_id=1, source_target_pairs={{0,16},{16,0},{1,17},{17,1},{2,18},{18,2},{3,19},{19,3},{4,20},{20... | collective-permute-start | bytes 1179656 | tf_op jit(solution)/shard_map/ppermute | solution.py:507
  37.0 5.4 %all-to-all-start = ((f32[32,8,128]{2,1,0:T(8,128)}), f32[32,8,128]{2,1,0:T(8,128)S(1)}, u32[]{:S(2)}, u32[]{:S(2)}) async-start(f32[32,8,128]{2,1,0:T(8,128)} %get-tuple-element.23), calls=%async_computation | async-start | bytes 262144 | tf_op jit(solution)/shard_map/all_to_all | solution.py:504
  42.4 8.2 %all-to-all-done = f32[32,8,128]{2,1,0:T(8,128)S(1)} async-done(((f32[32,8,128]{2,1,0:T(8,128)}), f32[32,8,128]{2,1,0:T(8,128)S(1)}, u32[]{:S(2)}, u32[]{:S(2)}) %all-to-all-start) | async-done | bytes 131104 | tf_op jit(solution)/shard_map/all_to_all | solution.py:504
  50.6 1.4 %analysis.1 = bf16[24,64,128]{2,1,0:T(8,128)(2,1)} custom-call(s32[1]{0:T(128)} %bitcast.me_ref, f32[2,16,8,128]{3,2,1,0:T(8,128)S(1)} %bitcast.17, bf16[1536,128]{1,0:T(8,128)(2,1)S(1)} %get-tuple-element.24.mine_ref, bf16[1536,128]{1,0:T(8,128)(2,1)S(1)} %collective-permute-done.4.other_ref), custom_call_target="tpu_custom_call" | custom-call | tf_op jit(solution)/shard_map/analysis/pallas_call | solution.py:371
  (12 shorter events, 0.0 us)
Async XLA Ops:
  0.0 13.5 %copy-start.4 = (f32[256]{0:T(256)S(1)}, f32[256]{0:T(256)}, u32[]{:S(2)}) copy-start(f32[256]{0:T(256)} %param.10) | copy-start | bytes 3076
  0.0 1.0 %copy-start = (bf16[1,24,64,128]{3,2,1,0:T(8,128)(2,1)S(1)}, bf16[1,24,64,128]{3,2,1,0:T(8,128)(2,1)}, u32[]{:S(2)}) copy-start(bf16[1,24,64,128]{3,2,1,0:T(8,128)(2,1)} %param.8) | copy-start | bytes 1179652
  1.0 12.5 %copy-start.2 = (bf16[216,256]{1,0:T(8,128)(2,1)S(1)}, bf16[216,256]{1,0:T(8,128)(2,1)}, u32[]{:S(2)}) copy-start(bf16[216,256]{1,0:T(8,128)(2,1)} %conv_ref.1) | copy-start | bytes 331780
  1.0 12.6 %copy-start.3 = (bf16[256,24]{0,1:T(8,128)(2,1)S(1)}, bf16[256,24]{0,1:T(8,128)(2,1)}, u32[]{:S(2)}) copy-start(bf16[256,24]{0,1:T(8,128)(2,1)} %param.11) | copy-start | bytes 36868
  1.0 14.9 %copy-start.5 = (f32[1,1,256]{2,1,0:T(1,128)S(1)}, f32[1,1,256]{2,1,0:T(1,128)}, u32[]{:S(2)}) copy-start(f32[1,1,256]{2,1,0:T(1,128)} %param.14) | copy-start | bytes 3076
  1.0 14.9 %copy-start.6 = (f32[1,1,256]{2,1,0:T(1,128)S(1)}, f32[1,1,256]{2,1,0:T(1,128)}, u32[]{:S(2)}) copy-start(f32[1,1,256]{2,1,0:T(1,128)} %param.15) | copy-start | bytes 3076
  1.1 10.9 %collective-permute-start = (bf16[48,128]{1,0:T(8,128)(2,1)S(1)}, bf16[48,128]{1,0:T(8,128)(2,1)S(1)}, u32[]{:S(2)}, u32[]{:S(2)}) collective-permute-start(bf16[48,128]{1,0:T(8,128)(2,1)S(1)} %get-tuple-element.16), channel_id=1, source_target_pairs={{0,4},{4,8},{8,12},{1,5},{5,9},{9,13},{2,6},{6,10},{10,14},{3,7},{... | collective-permute-start | bytes 36872 | tf_op jit(solution)/shard_map/ppermute | solution.py:471
  6.2 5.8 %collective-permute-start.1 = (bf16[48,128]{1,0:T(8,128)(2,1)S(1)}, bf16[48,128]{1,0:T(8,128)(2,1)S(1)}, u32[]{:S(2)}, u32[]{:S(2)}) collective-permute-start(bf16[48,128]{1,0:T(8,128)(2,1)S(1)} %get-tuple-element.17), channel_id=1, source_target_pairs={{4,0},{8,4},{12,8},{5,1},{9,5},{13,9},{6,2},{10,6},{14,10},{7,3},{... | collective-permute-start | bytes 36872 | tf_op jit(solution)/shard_map/ppermute | solution.py:472
  9.1 1.0 %copy-start.1 = (bf16[1,24,64,128]{3,2,1,0:T(8,128)(2,1)S(1)}, bf16[1,24,64,128]{3,2,1,0:T(8,128)(2,1)}, u32[]{:S(2)}) copy-start(bf16[1,24,64,128]{3,2,1,0:T(8,128)(2,1)} %param.8) | copy-start | bytes 1179652
  12.1 2.1 %collective-permute-start.3 = (bf16[48,128]{1,0:T(8,128)(2,1)S(1)}, bf16[48,128]{1,0:T(8,128)(2,1)S(1)}, u32[]{:S(2)}, u32[]{:S(2)}) collective-permute-start(bf16[48,128]{1,0:T(8,128)(2,1)S(1)} %get-tuple-element.19.own_left_ref), channel_id=1, source_target_pairs={{1,0},{2,1},{3,2},{0,3},{5,4},{6,5},{7,6},{4,7},{9,8},{10,9},{11,1... | collective-permute-start | bytes 36872 | tf_op jit(solution)/shard_map/ppermute | solution.py:476
  12.8 3.1 %collective-permute-start.2 = (bf16[48,128]{1,0:T(8,128)(2,1)S(1)}, bf16[48,128]{1,0:T(8,128)(2,1)S(1)}, u32[]{:S(2)}, u32[]{:S(2)}) collective-permute-start(bf16[48,128]{1,0:T(8,128)(2,1)S(1)} %get-tuple-element.20.own_right_ref), channel_id=1, source_target_pairs={{0,1},{1,2},{2,3},{3,0},{4,5},{5,6},{6,7},{7,4},{8,9},{9,10},{10,1... | collective-permute-start | bytes 36872 | tf_op jit(solution)/shard_map/ppermute | solution.py:475
  35.4 15.1 %collective-permute-start.4 = (bf16[1536,128]{1,0:T(8,128)(2,1)S(1)}, bf16[1536,128]{1,0:T(8,128)(2,1)S(1)}, u32[]{:S(2)}, u32[]{:S(2)}) collective-permute-start(bf16[1536,128]{1,0:T(8,128)(2,1)S(1)} %get-tuple-element.24.mine_ref), channel_id=1, source_target_pairs={{0,16},{16,0},{1,17},{17,1},{2,18},{18,2},{3,19},{19,3},{4,20},{20... | collective-permute-start | bytes 1179656 | tf_op jit(solution)/shard_map/ppermute | solution.py:507
  37.0 13.6 %all-to-all-start = ((f32[32,8,128]{2,1,0:T(8,128)}), f32[32,8,128]{2,1,0:T(8,128)S(1)}, u32[]{:S(2)}, u32[]{:S(2)}) async-start(f32[32,8,128]{2,1,0:T(8,128)} %get-tuple-element.23), calls=%async_computation | async-start | bytes 262144 | tf_op jit(solution)/shard_map/all_to_all | solution.py:504

commit v3 on v2

--- a/solution.py
+++ b/solution.py
@@ -15,10 +15,15 @@
 BF16 = jnp.bfloat16
 PAD = 8
 SMALL = 4 << 20
+GROUP = 12
 
 
 def lanes_of(shape):
     return lax.broadcasted_iota(jnp.int32, shape, len(shape) - 1)
+
+
+def most_of(total, limit):
+    return max(d for d in range(1, limit + 1) if total % d == 0)
 
 
 def rows_kernel(top_ref, bottom_ref, up_ref, down_ref, stage):
@@ -153,6 +158,7 @@
     first,
     second,
     final,
+    hidden,
     seen,
 ):
     nvar, cols = north_ref.shape[0] // 2, north_ref.shape[1]
@@ -169,11 +175,12 @@
         )
         return jnp.concatenate([row, left, right, ones], axis=0).astype(BF16)
 
-    def advance(patches, centre):
-        pre = jnp.dot(conv_ref[...], patches, preferred_element_type=F32)
-        hidden = gelu2(pre)
+    def hidden_of(patches):
+        return gelu2(jnp.dot(conv_ref[...], patches, preferred_element_type=F32))
+
+    def moved(centre, hidden):
         change = jnp.dot(out_w_ref[...], hidden, preferred_element_type=F32)
-        return (centre + change[:nvar]).astype(BF16).astype(F32)
+        return (centre + change).astype(BF16).astype(F32)
 
     from_left = from_left_ref[...].astype(F32)
     from_right = from_right_ref[...].astype(F32)
@@ -215,43 +222,57 @@
             stack.append(ones)
         sides.append(jnp.concatenate(stack, axis=0).astype(BF16))
     patches = jnp.concatenate(sides, axis=1)
-    beside = advance(patches, jnp.concatenate([west, east], axis=1))
+    beside = moved(jnp.concatenate([west, east], axis=1), hidden_of(patches))
     keep = jnp.where(lane == 1, north_in_ref[0], jnp.where(lane == rows + 2, north_in_ref[1], 1)) > 0
     mid_west = jnp.where(keep, beside[:, :cols], 0.0)
     mid_east = jnp.where(keep, beside[:, cols:], 0.0)
 
-    def pair(source, at):
+    def ahead(source, at, slot):
         at = pl.multiple_of(at * block, 16)
         patches = jnp.concatenate(
             [source[pl.ds(at, deep), :], source[pl.ds(at + block, deep), :]], axis=1
         )
+        hidden[slot] = hidden_of(patches)
+
+    def finish(source, at, slot):
+        at = pl.multiple_of(at * block, 16)
         centre = jnp.concatenate(
             [source[pl.ds(at + block, nvar), :], source[pl.ds(at + 2 * block, nvar), :]], axis=1
         ).astype(F32)
-        return advance(patches, centre)
-
-    def first_step(i, carry):
-        both = pair(first, 2 * i)
-        for half in range(2):
-            m = 2 * i + half
-            good = (jnp.where(m == 0, north_in_ref[0], 1) * jnp.where(m == rows + 1, north_in_ref[1], 1)) > 0
-            row = both[:, half * cols : (half + 1) * cols]
-            row = jnp.where(good, row, 0.0)
-            at = pl.multiple_of(m * block, 16)
-            second[pl.ds(at, block), :] = tap_rows(row, mid_west, mid_east, m + 1)
+        return moved(centre, hidden[slot])
+
+    def first_step(g, carry):
+        for q in range(group1):
+            ahead(first, 2 * (g * group1 + q), q)
+        for q in range(group1):
+            i = g * group1 + q
+            both = finish(first, 2 * i, q)
+            for half in range(2):
+                m = 2 * i + half
+                good = (jnp.where(m == 0, north_in_ref[0], 1) * jnp.where(m == rows + 1, north_in_ref[1], 1)) > 0
+                row = both[:, half * cols : (half + 1) * cols]
+                row = jnp.where(good, row, 0.0)
+                at = pl.multiple_of(m * block, 16)
+                second[pl.ds(at, block), :] = tap_rows(row, mid_west, mid_east, m + 1)
         return carry
 
-    lax.fori_loop(0, rows // 2 + 1, first_step, 0, unroll=11)
-
-    def second_step(j, carry):
-        both = pair(second, 2 * j)
-        both = jnp.concatenate([both[:, :cols], both[:, cols:]], axis=0)
-        at = pl.multiple_of(j * 2 * nvar, 16)
-        final[pl.ds(at, 2 * nvar), :] = both
-        forecast_ref[pl.ds(at, 2 * nvar), :] = both.astype(BF16)
+    group1 = most_of(rows // 2 + 1, hidden.shape[0])
+    lax.fori_loop(0, (rows // 2 + 1) // group1, first_step, 0)
+
+    def second_step(g, carry):
+        for q in range(group2):
+            ahead(second, 2 * (g * group2 + q), q)
+        for q in range(group2):
+            j = g * group2 + q
+            both = finish(second, 2 * j, q)
+            both = jnp.concatenate([both[:, :cols], both[:, cols:]], axis=0)
+            at = pl.multiple_of(j * 2 * nvar, 16)
+            final[pl.ds(at, 2 * nvar), :] = both
+            forecast_ref[pl.ds(at, 2 * nvar), :] = both.astype(BF16)
         return carry
 
-    lax.fori_loop(0, rows // 2, second_step, 0, unroll=8)
+    group2 = most_of(rows // 2, hidden.shape[0])
+    lax.fori_loop(0, (rows // 2) // group2, second_step, 0)
 
     def look(o, carry):
         seen[pl.ds(o, 1), :] = final[pl.ds(spot_ref[o], 1), :]
@@ -293,6 +314,7 @@
             pltpu.VMEM(((rows + 4) * block, cols), BF16),
             pltpu.VMEM(((rows + 2) * block, cols), BF16),
             pltpu.VMEM((rows * nvar, cols), F32),
+            pltpu.VMEM((GROUP, conv.shape[0], 2 * cols), BF16),
             pltpu.VMEM((slots, cols), F32),
         ],
         compiler_params=pltpu.CompilerParams(vmem_limit_bytes=16 << 20),

time: 52.3 us -> 41.8 us (0.80)
  Pallas kernels: 23.1 us -> 12.6 us
    pallas_call x1, Pallas kernels: 19.5 us -> 9 us  [run_forecast(): pl.pallas_call(forecast_kernel, out_shape=(jax.ShapeDtypeStruct((rows * n...]
  transfers between devices with their start and end apart: 6 -> 6, of which waited for: 3 -> 3; matrix products, arithmetic and copies ran while one was open for 3% -> 4% of each run, Pallas kernels for 4% -> 5%
where the time goes in v3:
time: 41.8 us; the launch traced here: 41.5 us
  starting transfers between devices  14 us (33%)
  Pallas kernels  12.6 us (30%)
  waiting for transfers between devices  10.4 us (25%)
  local copies, waits for them, and re-layouts  2.83 us (7%)
  other arithmetic  0.83 us (2%)
  between operations  0.79 us (2%)
    pallas_call x1, Pallas kernels, run_forecast(): pl.pallas_call(forecast_kernel, out_shape=(jax.ShapeDtypeStruct((rows * n...  9 us
    all_to_all x1, waiting for transfers between devices, per_device(): told = lax.all_to_all(notes, ('ens', 'lat', 'lon'), 0, 0, tiled=True)  8.2 us
    all_to_all x1, starting transfers between devices, per_device(): told = lax.all_to_all(notes, ('ens', 'lat', 'lon'), 0, 0, tiled=True)  5.37 us
    ppermute x1, starting transfers between devices, per_device(): north = lax.ppermute(last_rows, 'lat', down_lat)  5.09 us
    unnamed x14, local copies, waits for them, and re-layouts  2.02 us
    pallas_call x1, Pallas kernels, spread(): pl.pallas_call(spread_kernel, out_shape=(jax.ShapeDtypeStruct((rows * blo...  1.93 us
    ppermute x1, waiting for transfers between devices, per_device(): from_left = lax.ppermute(own_right, 'lon', right_lon)  1.71 us
    ppermute x1, starting transfers between devices, per_device(): other = lax.ppermute(forecast, 'ens', [(0, 1), (1, 0)])  1.52 us
  transfers between devices with their start and end apart: 6, of which 3 were waited for; matrix products, arithmetic and copies ran while one was open for 4% of the time, Pallas kernels for 5%

profile of v3, /device:TPU:0, one launch (start us, length us, event | category | flops | bytes accessed | tf_op | source)
XLA Modules:
  0.0 41.5 jit_solution(15471545273357719357)
XLA Ops:
  0.0 1.0 %copy-done = bf16[1,24,64,128]{3,2,1,0:T(8,128)(2,1)S(1)} copy-done((bf16[1,24,64,128]{3,2,1,0:T(8,128)(2,1)S(1)}, bf16[1,24,64,128]{3,2,1,0:T(8,128)(2,1)}, u32[]{:S(2)}) %copy-start) | copy-done | bytes 393240
  1.0 0.1 edge_rows.1
  1.1 5.1 %collective-permute-start = (bf16[48,128]{1,0:T(8,128)(2,1)S(1)}, bf16[48,128]{1,0:T(8,128)(2,1)S(1)}, u32[]{:S(2)}, u32[]{:S(2)}) collective-permute-start(bf16[48,128]{1,0:T(8,128)(2,1)S(1)} %get-tuple-element.16), channel_id=1, source_target_pairs={{0,4},{4,8},{8,12},{1,5},{5,9},{9,13},{2,6},{6,10},{10,14},{3,7},{... | collective-permute-start | bytes 36872 | tf_op jit(solution)/shard_map/ppermute | solution.py:493
  6.2 1.3 %collective-permute-start.1 = (bf16[48,128]{1,0:T(8,128)(2,1)S(1)}, bf16[48,128]{1,0:T(8,128)(2,1)S(1)}, u32[]{:S(2)}, u32[]{:S(2)}) collective-permute-start(bf16[48,128]{1,0:T(8,128)(2,1)S(1)} %get-tuple-element.17), channel_id=1, source_target_pairs={{4,0},{8,4},{12,8},{5,1},{9,5},{13,9},{6,2},{10,6},{14,10},{7,3},{... | collective-permute-start | bytes 36872 | tf_op jit(solution)/shard_map/ppermute | solution.py:494
  7.5 0.8 %copy.9 = s32[256,1]{1,0:T(8,128)S(1)} copy(s32[256,1]{0,1:T(1,128)} %bitcast.22) | data formatting | bytes 2048 | tf_op jit(solution)/shard_map/reshape | solution.py:501
  8.3 0.1 add_select_fusion.lane_ref
  8.3 0.7 %fusion.4.spot_ref = s32[256]{0:T(256)S(1)} fusion(s32[256]{0:T(256)} %bitcast.23), kind=kLoop, calls=%fused_computation.18 | loop fusion | flops 9984 | bytes 2048 | tf_op jit(solution)/shard_map/jit(clip)/min | solution.py:503
  9.1 0.0 copy-start.1
  9.1 1.0 %copy-done.1 = bf16[1,24,64,128]{3,2,1,0:T(8,128)(2,1)S(1)} copy-done((bf16[1,24,64,128]{3,2,1,0:T(8,128)(2,1)S(1)}, bf16[1,24,64,128]{3,2,1,0:T(8,128)(2,1)}, u32[]{:S(2)}) %copy-start.1) | copy-done | bytes 393240
  10.1 1.9 %spread.1 = (bf16[5120,128]{1,0:T(8,128)(2,1)S(1)}, f32[96,128]{1,0:T(8,128)S(1)}) custom-call(bf16[24,64,128]{2,1,0:T(8,128)(2,1)S(1)} %bitcast.16), custom_call_target="tpu_custom_call" | custom-call | flops 100000000 | bytes 4000000 | tf_op jit(solution)/shard_map/spread/pallas_call | solution.py:92
  12.0 0.0 collective-permute-done.1.south_ref
  12.0 0.1 edge_columns.1
  12.1 0.7 %collective-permute-start.3 = (bf16[48,128]{1,0:T(8,128)(2,1)S(1)}, bf16[48,128]{1,0:T(8,128)(2,1)S(1)}, u32[]{:S(2)}, u32[]{:S(2)}) collective-permute-start(bf16[48,128]{1,0:T(8,128)(2,1)S(1)} %get-tuple-element.19.own_left_ref), channel_id=1, source_target_pairs={{1,0},{2,1},{3,2},{0,3},{5,4},{6,5},{7,6},{4,7},{9,8},{10,9},{11,1... | collective-permute-start | bytes 36872 | tf_op jit(solution)/shard_map/ppermute | solution.py:498
  12.8 0.0 collective-permute-start.2
  12.8 0.1 add_convert_fusion.north_in_ref
  13.6 0.1 packed_weights.1
  13.7 0.5 %collective-permute-done.3.from_right_ref = bf16[48,128]{1,0:T(8,128)(2,1)S(1)} collective-permute-done((bf16[48,128]{1,0:T(8,128)(2,1)S(1)}, bf16[48,128]{1,0:T(8,128)(2,1)S(1)}, u32[]{:S(2)}, u32[]{:S(2)}) %collective-permute-start.3) | collective-permute-done | bytes 12320 | tf_op jit(solution)/shard_map/ppermute | solution.py:498
  14.2 1.7 %collective-permute-done.2.from_left_ref = bf16[48,128]{1,0:T(8,128)(2,1)S(1)} collective-permute-done((bf16[48,128]{1,0:T(8,128)(2,1)S(1)}, bf16[48,128]{1,0:T(8,128)(2,1)S(1)}, u32[]{:S(2)}, u32[]{:S(2)}) %collective-permute-start.2) | collective-permute-done | bytes 12320 | tf_op jit(solution)/shard_map/ppermute | solution.py:497
  15.9 9.0 %forecast.1 = (bf16[1536,128]{1,0:T(8,128)(2,1)S(1)}, f32[32,8,128]{2,1,0:T(8,128)}) custom-call(s32[256]{0:T(256)S(1)} %fusion.4.spot_ref, s32[2]{0:T(128)S(1)} %add_convert_fusion.north_in_ref, s32[1]{0:T(128)} %bitcast.13.count_ref, bf16[5120,128]{1,0:T(8,128)(2,1)S(1)} %get-tuple-element.15.taps_ref, bf16[48,128]{1,0:T(8,128)(2,1)S(1)} %collective-permute-done.north_ref, ...), custom_call_target="tpu_custom_call" | custom-call | tf_op jit(solution)/shard_map/forecast/pallas_call | solution.py:305
  24.9 1.5 %collective-permute-start.4 = (bf16[1536,128]{1,0:T(8,128)(2,1)S(1)}, bf16[1536,128]{1,0:T(8,128)(2,1)S(1)}, u32[]{:S(2)}, u32[]{:S(2)}) collective-permute-start(bf16[1536,128]{1,0:T(8,128)(2,1)S(1)} %get-tuple-element.24.mine_ref), channel_id=1, source_target_pairs={{0,16},{16,0},{1,17},{17,1},{2,18},{18,2},{3,19},{19,3},{4,20},{20... | collective-permute-start | bytes 1179656 | tf_op jit(solution)/shard_map/ppermute | solution.py:529
  26.5 5.4 %all-to-all-start = ((f32[32,8,128]{2,1,0:T(8,128)}), f32[32,8,128]{2,1,0:T(8,128)S(1)}, u32[]{:S(2)}, u32[]{:S(2)}) async-start(f32[32,8,128]{2,1,0:T(8,128)} %get-tuple-element.23), calls=%async_computation | async-start | bytes 262144 | tf_op jit(solution)/shard_map/all_to_all | solution.py:526
  31.8 8.2 %all-to-all-done = f32[32,8,128]{2,1,0:T(8,128)S(1)} async-done(((f32[32,8,128]{2,1,0:T(8,128)}), f32[32,8,128]{2,1,0:T(8,128)S(1)}, u32[]{:S(2)}, u32[]{:S(2)}) %all-to-all-start) | async-done | bytes 131104 | tf_op jit(solution)/shard_map/all_to_all | solution.py:526
  40.0 0.0 collective-permute-done.4.other_ref
  40.0 1.4 %analysis.1 = bf16[24,64,128]{2,1,0:T(8,128)(2,1)} custom-call(s32[1]{0:T(128)} %bitcast.me_ref, f32[2,16,8,128]{3,2,1,0:T(8,128)S(1)} %bitcast.17, bf16[1536,128]{1,0:T(8,128)(2,1)S(1)} %get-tuple-element.24.mine_ref, bf16[1536,128]{1,0:T(8,128)(2,1)S(1)} %collective-permute-done.4.other_ref), custom_call_target="tpu_custom_call" | custom-call | tf_op jit(solution)/shard_map/analysis/pallas_call | solution.py:393
  (12 shorter events, 0.0 us)
Async XLA Ops:
  0.0 13.5 %copy-start.4 = (f32[256]{0:T(256)S(1)}, f32[256]{0:T(256)}, u32[]{:S(2)}) copy-start(f32[256]{0:T(256)} %param.10) | copy-start | bytes 3076
  0.0 1.0 %copy-start = (bf16[1,24,64,128]{3,2,1,0:T(8,128)(2,1)S(1)}, bf16[1,24,64,128]{3,2,1,0:T(8,128)(2,1)}, u32[]{:S(2)}) copy-start(bf16[1,24,64,128]{3,2,1,0:T(8,128)(2,1)} %param.8) | copy-start | bytes 1179652
  1.0 12.5 %copy-start.2 = (bf16[216,256]{1,0:T(8,128)(2,1)S(1)}, bf16[216,256]{1,0:T(8,128)(2,1)}, u32[]{:S(2)}) copy-start(bf16[216,256]{1,0:T(8,128)(2,1)} %conv_ref.1) | copy-start | bytes 331780
  1.0 12.6 %copy-start.3 = (bf16[256,24]{0,1:T(8,128)(2,1)S(1)}, bf16[256,24]{0,1:T(8,128)(2,1)}, u32[]{:S(2)}) copy-start(bf16[256,24]{0,1:T(8,128)(2,1)} %param.11) | copy-start | bytes 36868
  1.0 14.9 %copy-start.5 = (f32[1,1,256]{2,1,0:T(1,128)S(1)}, f32[1,1,256]{2,1,0:T(1,128)}, u32[]{:S(2)}) copy-start(f32[1,1,256]{2,1,0:T(1,128)} %param.14) | copy-start | bytes 3076
  1.0 14.9 %copy-start.6 = (f32[1,1,256]{2,1,0:T(1,128)S(1)}, f32[1,1,256]{2,1,0:T(1,128)}, u32[]{:S(2)}) copy-start(f32[1,1,256]{2,1,0:T(1,128)} %param.15) | copy-start | bytes 3076
  1.1 10.9 %collective-permute-start = (bf16[48,128]{1,0:T(8,128)(2,1)S(1)}, bf16[48,128]{1,0:T(8,128)(2,1)S(1)}, u32[]{:S(2)}, u32[]{:S(2)}) collective-permute-start(bf16[48,128]{1,0:T(8,128)(2,1)S(1)} %get-tuple-element.16), channel_id=1, source_target_pairs={{0,4},{4,8},{8,12},{1,5},{5,9},{9,13},{2,6},{6,10},{10,14},{3,7},{... | collective-permute-start | bytes 36872 | tf_op jit(solution)/shard_map/ppermute | solution.py:493
  6.2 5.8 %collective-permute-start.1 = (bf16[48,128]{1,0:T(8,128)(2,1)S(1)}, bf16[48,128]{1,0:T(8,128)(2,1)S(1)}, u32[]{:S(2)}, u32[]{:S(2)}) collective-permute-start(bf16[48,128]{1,0:T(8,128)(2,1)S(1)} %get-tuple-element.17), channel_id=1, source_target_pairs={{4,0},{8,4},{12,8},{5,1},{9,5},{13,9},{6,2},{10,6},{14,10},{7,3},{... | collective-permute-start | bytes 36872 | tf_op jit(solution)/shard_map/ppermute | solution.py:494
  9.1 1.0 %copy-start.1 = (bf16[1,24,64,128]{3,2,1,0:T(8,128)(2,1)S(1)}, bf16[1,24,64,128]{3,2,1,0:T(8,128)(2,1)}, u32[]{:S(2)}) copy-start(bf16[1,24,64,128]{3,2,1,0:T(8,128)(2,1)} %param.8) | copy-start | bytes 1179652
  12.1 2.1 %collective-permute-start.3 = (bf16[48,128]{1,0:T(8,128)(2,1)S(1)}, bf16[48,128]{1,0:T(8,128)(2,1)S(1)}, u32[]{:S(2)}, u32[]{:S(2)}) collective-permute-start(bf16[48,128]{1,0:T(8,128)(2,1)S(1)} %get-tuple-element.19.own_left_ref), channel_id=1, source_target_pairs={{1,0},{2,1},{3,2},{0,3},{5,4},{6,5},{7,6},{4,7},{9,8},{10,9},{11,1... | collective-permute-start | bytes 36872 | tf_op jit(solution)/shard_map/ppermute | solution.py:498
  12.8 3.1 %collective-permute-start.2 = (bf16[48,128]{1,0:T(8,128)(2,1)S(1)}, bf16[48,128]{1,0:T(8,128)(2,1)S(1)}, u32[]{:S(2)}, u32[]{:S(2)}) collective-permute-start(bf16[48,128]{1,0:T(8,128)(2,1)S(1)} %get-tuple-element.20.own_right_ref), channel_id=1, source_target_pairs={{0,1},{1,2},{2,3},{3,0},{4,5},{5,6},{6,7},{7,4},{8,9},{9,10},{10,1... | collective-permute-start | bytes 36872 | tf_op jit(solution)/shard_map/ppermute | solution.py:497
  24.9 15.1 %collective-permute-start.4 = (bf16[1536,128]{1,0:T(8,128)(2,1)S(1)}, bf16[1536,128]{1,0:T(8,128)(2,1)S(1)}, u32[]{:S(2)}, u32[]{:S(2)}) collective-permute-start(bf16[1536,128]{1,0:T(8,128)(2,1)S(1)} %get-tuple-element.24.mine_ref), channel_id=1, source_target_pairs={{0,16},{16,0},{1,17},{17,1},{2,18},{18,2},{3,19},{19,3},{4,20},{20... | collective-permute-start | bytes 1179656 | tf_op jit(solution)/shard_map/ppermute | solution.py:529
  26.5 13.6 %all-to-all-start = ((f32[32,8,128]{2,1,0:T(8,128)}), f32[32,8,128]{2,1,0:T(8,128)S(1)}, u32[]{:S(2)}, u32[]{:S(2)}) async-start(f32[32,8,128]{2,1,0:T(8,128)} %get-tuple-element.23), calls=%async_computation | async-start | bytes 262144 | tf_op jit(solution)/shard_map/all_to_all | solution.py:526

commit v4 on v3

--- a/solution.py
+++ b/solution.py
@@ -26,32 +26,34 @@
     return max(d for d in range(1, limit + 1) if total % d == 0)
 
 
-def rows_kernel(top_ref, bottom_ref, up_ref, down_ref, stage):
-    nvar, tile, cols = top_ref.shape
-    for ref, out, first in ((top_ref, up_ref, 0), (bottom_ref, down_ref, tile - 2)):
-        stage[...] = ref[...].reshape(nvar * tile, cols).astype(F32)
-        both = [stage[pl.ds(first + i, nvar, stride=tile), :] for i in range(2)]
-        out[...] = jnp.concatenate(both, axis=0).astype(BF16)
-
-
 def edge_rows(x):
     nvar, rows, cols = x.shape
     tile = 16
-    last = rows // tile - 1
+
+    def kernel(x_ref, up_ref, down_ref, part, stage, sems):
+        copies = []
+        for i, first in enumerate((0, rows - tile)):
+            copies.append(pltpu.make_async_copy(x_ref.at[:, first : first + tile, :], part.at[i], sems.at[i]))
+            copies[i].start()
+        for i, (out, first) in enumerate(((up_ref, 0), (down_ref, tile - 2))):
+            copies[i].wait()
+            stage[...] = part[i].reshape(nvar * tile, cols).astype(F32)
+            both = [stage[pl.ds(first + j, nvar, stride=tile), :] for j in range(2)]
+            out[...] = jnp.concatenate(both, axis=0).astype(BF16)
+
     out = jax.ShapeDtypeStruct((2 * nvar, cols), BF16)
     return pl.pallas_call(
-        rows_kernel,
+        kernel,
         out_shape=(out, out),
-        grid=(1,),
-        in_specs=[
-            pl.BlockSpec((nvar, tile, cols), lambda i: (0, 0, 0)),
-            pl.BlockSpec((nvar, tile, cols), lambda i: (0, last, 0)),
+        in_specs=[pl.BlockSpec(memory_space=pltpu.HBM)],
+        scratch_shapes=[
+            pltpu.VMEM((2, nvar, tile, cols), BF16),
+            pltpu.VMEM((nvar * tile, cols), F32),
+            pltpu.SemaphoreType.DMA((2,)),
         ],
-        out_specs=[pl.BlockSpec((2 * nvar, cols), lambda i: (0, 0))] * 2,
-        scratch_shapes=[pltpu.VMEM((nvar * tile, cols), F32)],
         compiler_params=pltpu.CompilerParams(vmem_limit_bytes=SMALL),
         name="edge_rows",
-    )(x, x)
+    )(x)
 
 
 def spread_kernel(x_ref, taps_ref, own_ref, stage, xf):
@@ -66,7 +68,10 @@
     pick = pick.astype(BF16)
     per = cols // rows
     flat = x_ref[...].reshape(nvar * rows, cols)
-    xf[...] = flat.astype(F32)
+    for v in range(nvar):
+        column = x_ref[v].astype(F32)
+        for r in range(0, rows, 8):
+            xf[pl.ds(r * nvar + v, 8, stride=nvar), :] = column[r : r + 8]
     taken = lax.dot_general(pick, flat, (((1,), (1,)), ((), ())), preferred_element_type=F32)
     for v in range(nvar):
         part = taken[:, (v // per) * cols : (v // per + 1) * cols]
@@ -77,7 +82,7 @@
     ones = jnp.ones((PAD, cols), F32)
 
     def fill(r, carry):
-        row = xf[pl.ds(r, nvar, stride=rows), :]
+        row = xf[pl.ds(pl.multiple_of(r * nvar, 8), nvar), :]
         tap = jnp.concatenate([row, pltpu.roll(row, 1, 1), pltpu.roll(row, cols - 1, 1), ones], axis=0)
         at = pl.multiple_of(r * block, 16)
         taps_ref[pl.ds(at, block), :] = tap.astype(BF16)
@@ -139,7 +144,6 @@
 
 def forecast_kernel(
     spot_ref,
-    north_in_ref,
     count_ref,
     taps_ref,
     north_ref,
@@ -150,7 +154,7 @@
     from_right_ref,
     conv_ref,
     out_w_ref,
-    lane_ref,
+    chosen_ref,
     value_ref,
     weight_ref,
     forecast_ref,
@@ -223,7 +227,10 @@
         sides.append(jnp.concatenate(stack, axis=0).astype(BF16))
     patches = jnp.concatenate(sides, axis=1)
     beside = moved(jnp.concatenate([west, east], axis=1), hidden_of(patches))
-    keep = jnp.where(lane == 1, north_in_ref[0], jnp.where(lane == rows + 2, north_in_ref[1], 1)) > 0
+    here = lax.axis_index("lat")
+    north_in = (here > 0).astype(jnp.int32)
+    south_in = (here < lax.axis_size("lat") - 1).astype(jnp.int32)
+    keep = jnp.where(lane == 1, north_in, jnp.where(lane == rows + 2, south_in, 1)) > 0
     mid_west = jnp.where(keep, beside[:, :cols], 0.0)
     mid_east = jnp.where(keep, beside[:, cols:], 0.0)
 
@@ -249,7 +256,7 @@
             both = finish(first, 2 * i, q)
             for half in range(2):
                 m = 2 * i + half
-                good = (jnp.where(m == 0, north_in_ref[0], 1) * jnp.where(m == rows + 1, north_in_ref[1], 1)) > 0
+                good = (jnp.where(m == 0, north_in, 1) * jnp.where(m == rows + 1, south_in, 1)) > 0
                 row = both[:, half * cols : (half + 1) * cols]
                 row = jnp.where(good, row, 0.0)
                 at = pl.multiple_of(m * block, 16)
@@ -275,40 +282,40 @@
     lax.fori_loop(0, (rows // 2) // group2, second_step, 0)
 
     def look(o, carry):
-        seen[pl.ds(o, 1), :] = final[pl.ds(spot_ref[o], 1), :]
+        seen[pl.ds(o, 1), :] = final[pl.ds(spot_ref[o // cols, o % cols], 1), :]
         return carry
 
     slots = seen.shape[0]
     lax.fori_loop(0, slots, look, 0, unroll=16)
-    masked = jnp.where(lane_ref[...] == lanes_of((slots, cols)), seen[...], 0.0).astype(BF16)
+    masked = seen[...].astype(BF16) * chosen_ref[...]
     values = lax.dot_general(
         jnp.ones((8, cols), BF16), masked, (((1,), (1,)), ((), ())), preferred_element_type=F32
     )
     fold = value_ref.shape[0]
-    live = lanes_of((fold, cols)) + cols * lax.broadcasted_iota(jnp.int32, (fold, cols), 0) < count_ref[0]
-    note = [values[0:1, i * cols : (i + 1) * cols] for i in range(fold)]
-    note += [value_ref[...], jnp.where(live, weight_ref[...], 0.0)]
-    note.append(jnp.zeros((notes_ref.shape[1] - 3 * fold, cols), F32))
-    note = jnp.concatenate(note, axis=0)
+    live = lanes_of((fold, cols)) + cols * lax.broadcasted_iota(jnp.int32, (fold, cols), 0) < count_ref[0, 0]
+    member = lax.axis_index("ens")
+    weight = jnp.where(live, weight_ref[...], 0.0)
+    extra = jnp.where(member == 0, value_ref[...], jnp.where(member == 1, weight, 0.0))
+    note = [values[0:1, i * cols : (i + 1) * cols] for i in range(fold)] + [extra]
+    note = jnp.concatenate(note, axis=0).astype(BF16)
     for d in range(notes_ref.shape[0]):
         notes_ref[d] = note
 
 
-def run_forecast(spot, inside, count, taps, north, south, own_left, own_right, from_left, from_right, conv, out_w, lane, value, weight, devices):
+def run_forecast(spot, count, taps, north, south, own_left, own_right, from_left, from_right, conv, out_w, chosen, value, weight, devices):
     nvar, cols = north.shape[0] // 2, north.shape[1]
-    slots = spot.shape[0]
+    slots = spot.shape[0] * spot.shape[1]
     block = 3 * nvar + PAD
     rows = taps.shape[0] // block
-    note_rows = -(-3 * value.shape[0] // 8) * 8
     smem = pl.BlockSpec(memory_space=pltpu.SMEM)
     vmem = pl.BlockSpec(memory_space=pltpu.VMEM)
     return pl.pallas_call(
         forecast_kernel,
         out_shape=(
             jax.ShapeDtypeStruct((rows * nvar, cols), BF16),
-            jax.ShapeDtypeStruct((devices, note_rows, cols), F32),
+            jax.ShapeDtypeStruct((devices, 2 * value.shape[0], cols), BF16),
         ),
-        in_specs=[smem, smem, smem] + [vmem] * 12,
+        in_specs=[smem, smem] + [vmem] * 12,
         out_specs=(vmem, vmem),
         scratch_shapes=[
             pltpu.VMEM(((rows + 4) * block, cols), BF16),
@@ -319,7 +326,7 @@
         ],
         compiler_params=pltpu.CompilerParams(vmem_limit_bytes=16 << 20),
         name="forecast",
-    )(spot, inside, count, taps, north, south, own_left, own_right, from_left, from_right, conv, out_w, lane, value, weight)
+    )(spot, count, taps, north, south, own_left, own_right, from_left, from_right, conv, out_w, chosen, value, weight)
 
 
 def pair_weights(gram, proj):
@@ -352,53 +359,70 @@
     return [[1.0 / count + full[k][m] - centre[m] for m in range(count)] for k in range(count)]
 
 
-def analysis_kernel(me_ref, told_ref, mine_ref, other_ref, out_ref, blended):
-    count, shards = told_ref.shape[0], told_ref.shape[1]
-    nvar, rows, cols = out_ref.shape
-    pairs = [(k, m) for k in range(count) for m in range(k, count)]
-    sums = {key: 0.0 for key in pairs}
+def analysis_kernel(told_ref, mine_ref, other_ref, out_ref, blended, packed, sems):
+    count = lax.axis_size("ens")
+    nvar, rows, cols = packed.shape[1], out_ref.shape[1], packed.shape[3]
+    depth = told_ref.shape[1]
+    told = told_ref[...].astype(F32).reshape(count, -1, cols)
+    fold = depth // 2
+    size = told.shape[1]
+    hx = [told[k] for k in range(count)]
+    value = pltpu.roll(told[0], size - fold, 0)
+    weight = pltpu.roll(told[1], size - fold, 0)
+    used = lax.broadcasted_iota(jnp.int32, (size, cols), 0) % depth < fold
+    weight = jnp.where(used, weight, 0.0)
+    mean = sum(hx) / count
+    spread_of = [h - mean for h in hx]
+    innov = value - mean
+    tile = (8, cols)
+
+    def total(term):
+        return jnp.broadcast_to(jnp.sum(term, keepdims=True), tile)
+
+    scaled = [part * weight for part in spread_of]
+    gram = [[None] * count for k in range(count)]
     for k in range(count):
-        sums[k] = 0.0
-    for s in range(shards):
-        hx = [told_ref[k, s, 0:2, :] for k in range(count)]
-        value = told_ref[0, s, 2:4, :]
-        weight = told_ref[0, s, 4:6, :]
-        mean = sum(hx) / count
-        spread = [h - mean for h in hx]
-        innov = value - mean
-        for k in range(count):
-            scaled = spread[k] * weight
-            sums[k] = sums[k] + scaled * innov
-            for m in range(k, count):
-                sums[k, m] = sums[k, m] + scaled * spread[m]
-    tile = (8, cols)
-    whole = {key: jnp.broadcast_to(jnp.sum(term, keepdims=True), tile) for key, term in sums.items()}
-    gram = [[whole[min(k, m), max(k, m)] for m in range(count)] for k in range(count)]
-    weights = pair_weights(gram, [whole[k] for k in range(count)])
-    me = me_ref[0]
+        for m in range(k, count):
+            gram[k][m] = gram[m][k] = total(scaled[k] * spread_of[m])
+    weights = pair_weights(gram, [total(scaled[k] * innov) for k in range(count)])
+    me = lax.axis_index("ens")
     mine = jnp.where(me == 0, weights[0][0], weights[1][1])[0:1, :]
     other = jnp.where(me == 0, weights[1][0], weights[0][1])[0:1, :]
-    blended[...] = mine * mine_ref[...].astype(F32) + other * other_ref[...].astype(F32)
-    for v in range(nvar):
-        for r in range(0, rows, 16):
-            halves = [
-                blended[pl.ds((r + 8 * i) * nvar + v, 8, stride=nvar), :] for i in range(2)
-            ]
-            out_ref[v, r : r + 16, :] = jnp.concatenate(halves, axis=0).astype(BF16)
-
-
-def run_analysis(me, told, mine, other, shape):
+    high = packed.shape[2]
+
+    def copy_of(c):
+        return pltpu.make_async_copy(packed.at[c], out_ref.at[:, pl.ds(c * high, high), :], sems.at[c])
+
+    for c in range(rows // high):
+        at = c * high * nvar
+        part = slice(at, at + high * nvar)
+        blended[c] = mine * mine_ref[part, :].astype(F32) + other * other_ref[part, :].astype(F32)
+        for v in range(nvar):
+            for r in range(0, high, 16):
+                halves = [blended[c, pl.ds((r + 8 * i) * nvar + v, 8, stride=nvar), :] for i in range(2)]
+                packed[c, v, r : r + 16, :] = jnp.concatenate(halves, axis=0).astype(BF16)
+        copy_of(c).start()
+    for c in range(rows // high):
+        copy_of(c).wait()
+
+
+def run_analysis(told, mine, other, shape):
     nvar, rows, cols = shape
+    high = 16
     vmem = pl.BlockSpec(memory_space=pltpu.VMEM)
     return pl.pallas_call(
         analysis_kernel,
         out_shape=jax.ShapeDtypeStruct(shape, BF16),
-        in_specs=[pl.BlockSpec(memory_space=pltpu.SMEM), vmem, vmem, vmem],
-        out_specs=vmem,
-        scratch_shapes=[pltpu.VMEM((nvar * rows, cols), F32)],
+        in_specs=[vmem, vmem, vmem],
+        out_specs=pl.BlockSpec(memory_space=pltpu.HBM),
+        scratch_shapes=[
+            pltpu.VMEM((rows // high, high * nvar, cols), F32),
+            pltpu.VMEM((rows // high, nvar, high, cols), BF16),
+            pltpu.SemaphoreType.DMA((rows // high,)),
+        ],
         compiler_params=pltpu.CompilerParams(vmem_limit_bytes=8 << 20),
         name="analysis",
-    )(me, told, mine, other)
+    )(told, mine, other)
 
 
 def blend_weights(gram, proj):
@@ -421,9 +445,11 @@
 
 def many_members(told, forecast, shape):
     nvar, rows, cols = shape
-    members = told[:, :, 0:2, :].reshape(told.shape[0], -1)
-    value = told[0, :, 2:4, :].reshape(-1)
-    weight = told[0, :, 4:6, :].reshape(-1)
+    fold = told.shape[1] // 2
+    told = told.astype(F32).reshape(lax.axis_size("ens"), -1, *told.shape[1:])
+    members = told[:, :, :fold, :].reshape(told.shape[0], -1)
+    value = told[0, :, fold:, :].reshape(-1)
+    weight = told[1, :, fold:, :].reshape(-1)
     mean = jnp.mean(members, axis=0)
     spread = members - mean[None, :]
     innov = value - mean
@@ -437,11 +463,13 @@
     return blended.astype(BF16).reshape(rows, nvar, cols).transpose(1, 0, 2)
 
 
-def packed_weights(conv_weight, conv_bias, out_weight, nvar):
+def prepare(conv_weight, conv_bias, out_weight, index, shape):
+    nvar, rows, cols = shape
+    fold = index.shape[0]
     hid = conv_bias.shape[0]
     block = 3 * nvar + PAD
 
-    def kernel(conv_ref, bias_ref, out_ref, packed_ref, half_ref):
+    def kernel(conv_ref, bias_ref, out_ref, index_ref, packed_ref, half_ref, spot_ref, chosen_ref):
         bias = bias_ref[...]
         high = bias.astype(BF16).astype(F32)
         middle = (bias - high).astype(BF16).astype(F32)
@@ -458,17 +486,28 @@
                 pieces.append(jnp.zeros((PAD, hid), F32))
         packed_ref[...] = jnp.concatenate(pieces, axis=0).T.astype(BF16)
         half_ref[...] = (out_ref[...].astype(F32) * 0.5).astype(BF16)
+        index = index_ref[...]
+        row = index // cols % rows
+        var = index // (rows * cols)
+        spot_ref[...] = jnp.clip(row * nvar + var, 0, rows * nvar - 1)
+        lane = (index % cols).astype(F32)
+        for i in range(fold):
+            across = jnp.broadcast_to(lane[i : i + 1, :], (cols, cols)).T
+            hot = across == lanes_of((cols, cols)).astype(F32)
+            chosen_ref[i * cols : (i + 1) * cols, :] = jnp.where(hot, 1.0, 0.0).astype(BF16)
 
     return pl.pallas_call(
         kernel,
         out_shape=(
             jax.ShapeDtypeStruct((hid, 3 * block), BF16),
             jax.ShapeDtypeStruct((nvar, hid), BF16),
+            jax.ShapeDtypeStruct((fold, cols), jnp.int32),
+            jax.ShapeDtypeStruct((fold * cols, cols), BF16),
         ),
         compiler_params=pltpu.CompilerParams(vmem_limit_bytes=SMALL),
         cost_estimate=pl.CostEstimate(flops=10**7, bytes_accessed=10**6, transcendentals=0),
-        name="packed_weights",
-    )(conv_weight, conv_bias[None], out_weight.T)
+        name="prepare",
+    )(conv_weight, conv_bias[None], out_weight.T, index)
 
 
 def per_device(
@@ -497,18 +536,12 @@
     from_left = lax.ppermute(own_right, "lon", right_lon)
     from_right = lax.ppermute(own_left, "lon", left_lon)
 
-    conv, out_w = packed_weights(conv_weight, conv_bias, out_weight, nvar)
-    slots = obs_index.reshape(-1)
-    var, row, lane = slots // (rows * cols), slots // cols % rows, slots % cols
-    spot = jnp.clip(row * nvar + var, 0, rows * nvar - 1)
-    here = lax.axis_index("lat")
-    inside = jnp.stack([here > 0, here < n_lat - 1]).astype(jnp.int32)
-    fold = (slots.shape[0] // cols, cols)
-    devices = n_ens * n_lat * n_lon
+    fold = (obs_index.size // cols, cols)
+    index, own_left, own_right = lax.optimization_barrier((obs_index, own_left, own_right))
+    conv, out_w, spot, chosen = prepare(conv_weight, conv_bias, out_weight, index.reshape(fold), x.shape)
     forecast, notes = run_forecast(
         spot,
-        inside,
-        obs_count.reshape(1),
+        obs_count,
         taps,
         north,
         south,
@@ -518,17 +551,15 @@
         from_right,
         conv,
         out_w,
-        lane[:, None],
+        chosen,
         obs_value.reshape(fold),
         obs_weight.reshape(fold),
-        devices,
+        n_ens * n_lat * n_lon,
     )
     told = lax.all_to_all(notes, ("ens", "lat", "lon"), 0, 0, tiled=True)
-    told = told.reshape(n_ens, n_lat * n_lon, *notes.shape[1:])
     if n_ens == 2:
         other = lax.ppermute(forecast, "ens", [(0, 1), (1, 0)])
-        me = lax.axis_index("ens").reshape(1)
-        return run_analysis(me, told, forecast, other, x.shape)[None]
+        return run_analysis(told, forecast, other, x.shape)[None]
     return many_members(told, forecast, x.shape)[None]
 
 

time: 41.8 us -> 41.6 us (level)
  blocking collectives: 0 us -> 10.9 us
  waiting for transfers between devices: 10.4 us -> 2.49 us
  starting transfers between devices: 14 us -> 8.39 us
  local copies, waits for them, and re-layouts: 2.83 us -> 5.3 us
  other arithmetic: 0.83 us -> 0 us
  Pallas kernels: 12.6 us -> 13.3 us
    all_to_all x0 -> x1, blocking collectives: none -> 10.9 us  [per_device(): told = lax.all_to_all(notes, ('ens', 'lat', 'lon'), 0, 0, tiled=True)]
    all_to_all x1 -> x0, waiting for transfers between devices: 8.2 us -> none  [per_device(): told = lax.all_to_all(notes, ('ens', 'lat', 'lon'), 0, 0, tiled=True)]
    all_to_all x1 -> x0, starting transfers between devices: 5.37 us -> none  [per_device(): told = lax.all_to_all(notes, ('ens', 'lat', 'lon'), 0, 0, tiled=True)]
    unnamed x14, local copies, waits for them, and re-layouts: 2.02 us -> 5.3 us
    ppermute x1, waiting for transfers between devices: 0.01 us -> 2.48 us  [per_device(): south = lax.ppermute(first_rows, 'lat', up_lat)]
    ppermute x1, waiting for transfers between devices: 1.71 us -> 0.01 us  [per_device(): from_left = lax.ppermute(own_right, 'lon', right_lon)]
    pallas_call x1, Pallas kernels: 9 us -> 9.89 us  [run_forecast(): pl.pallas_call(forecast_kernel, out_shape=(jax.ShapeDtypeStruct((rows * n...]
    reshape x1 -> x0, local copies, waits for them, and re-layouts: 0.81 us -> none  [per_device(): slots = obs_index.reshape(-1)]
  transfers between devices with their start and end apart: 6 -> 5, of which waited for: 3 -> 1; matrix products, arithmetic and copies ran while one was open for 4% -> 0% of each run, Pallas kernels for 5% -> 5%
where the time goes in v4:
time: 41.6 us; the launch traced here: 41.2 us
  Pallas kernels  13.3 us (32%)
  blocking collectives  10.9 us (26%)
  starting transfers between devices  8.39 us (20%)
  local copies, waits for them, and re-layouts  5.3 us (13%)
  waiting for transfers between devices  2.49 us (6%)
  between operations  0.76 us (2%)
    all_to_all x1, blocking collectives, per_device(): told = lax.all_to_all(notes, ('ens', 'lat', 'lon'), 0, 0, tiled=True)  10.9 us
    pallas_call x1, Pallas kernels, run_forecast(): pl.pallas_call(forecast_kernel, out_shape=(jax.ShapeDtypeStruct((rows * n...  9.89 us
    unnamed x14, local copies, waits for them, and re-layouts  5.3 us
    ppermute x1, starting transfers between devices, per_device(): north = lax.ppermute(last_rows, 'lat', down_lat)  4.96 us
    ppermute x1, waiting for transfers between devices, per_device(): south = lax.ppermute(first_rows, 'lat', up_lat)  2.48 us
    pallas_call x1, Pallas kernels, spread(): pl.pallas_call(spread_kernel, out_shape=(jax.ShapeDtypeStruct((rows * blo...  1.8 us
    ppermute x1, starting transfers between devices, per_device(): other = lax.ppermute(forecast, 'ens', [(0, 1), (1, 0)])  1.58 us
    pallas_call x1, Pallas kernels, run_analysis(): pl.pallas_call(analysis_kernel, out_shape=jax.ShapeDtypeStruct(shape, BF1...  1.3 us
  transfers between devices with their start and end apart: 5, of which 1 were waited for; matrix products, arithmetic and copies ran while one was open for 0% of the time, Pallas kernels for 5%

profile of v4, /device:TPU:0, one launch (start us, length us, event | category | flops | bytes accessed | tf_op | source)
XLA Modules:
  0.0 41.2 jit_solution(3759773217724350805)
XLA Ops:
  0.0 1.0 %copy-done = bf16[1,24,64,128]{3,2,1,0:T(8,128)(2,1)S(1)} copy-done((bf16[1,24,64,128]{3,2,1,0:T(8,128)(2,1)S(1)}, bf16[1,24,64,128]{3,2,1,0:T(8,128)(2,1)}, u32[]{:S(2)}) %copy-start) | copy-done | bytes 393240
  1.0 0.1 edge_rows.1
  1.1 5.0 %collective-permute-start = (bf16[48,128]{1,0:T(8,128)(2,1)S(1)}, bf16[48,128]{1,0:T(8,128)(2,1)S(1)}, u32[]{:S(2)}, u32[]{:S(2)}) collective-permute-start(bf16[48,128]{1,0:T(8,128)(2,1)S(1)} %get-tuple-element.21), channel_id=1, source_target_pairs={{0,4},{4,8},{8,12},{1,5},{5,9},{9,13},{2,6},{6,10},{10,14},{3,7},{... | collective-permute-start | bytes 36872 | tf_op jit(solution)/shard_map/ppermute | solution.py:532
  6.1 1.3 %collective-permute-start.1 = (bf16[48,128]{1,0:T(8,128)(2,1)S(1)}, bf16[48,128]{1,0:T(8,128)(2,1)S(1)}, u32[]{:S(2)}, u32[]{:S(2)}) collective-permute-start(bf16[48,128]{1,0:T(8,128)(2,1)S(1)} %get-tuple-element.22), channel_id=1, source_target_pairs={{4,0},{8,4},{12,8},{5,1},{9,5},{13,9},{6,2},{10,6},{14,10},{7,3},{... | collective-permute-start | bytes 36872 | tf_op jit(solution)/shard_map/ppermute | solution.py:533
  7.4 1.8 %spread.1 = (bf16[5120,128]{1,0:T(8,128)(2,1)S(1)}, f32[96,128]{1,0:T(8,128)S(1)}) custom-call(bf16[24,64,128]{2,1,0:T(8,128)(2,1)S(1)} %bitcast.8), custom_call_target="tpu_custom_call" | custom-call | flops 100000000 | bytes 4000000 | tf_op jit(solution)/shard_map/spread/pallas_call | solution.py:97
  9.2 0.0 collective-permute-done.north_ref
  9.2 2.5 %collective-permute-done.1.south_ref = bf16[48,128]{1,0:T(8,128)(2,1)S(1)} collective-permute-done((bf16[48,128]{1,0:T(8,128)(2,1)S(1)}, bf16[48,128]{1,0:T(8,128)(2,1)S(1)}, u32[]{:S(2)}, u32[]{:S(2)}) %collective-permute-start.1) | collective-permute-done | bytes 12320 | tf_op jit(solution)/shard_map/ppermute | solution.py:533
  11.7 0.1 edge_columns.1
  11.8 0.1 collective-permute-start.3
  11.8 0.5 %collective-permute-start.2 = (bf16[48,128]{1,0:T(8,128)(2,1)S(1)}, bf16[48,128]{1,0:T(8,128)(2,1)S(1)}, u32[]{:S(2)}, u32[]{:S(2)}) collective-permute-start(bf16[48,128]{1,0:T(8,128)(2,1)S(1)} %get-tuple-element.29.own_right_ref), channel_id=1, source_target_pairs={{0,1},{1,2},{2,3},{3,0},{4,5},{5,6},{6,7},{7,4},{8,9},{9,10},{10,1... | collective-permute-start | bytes 36872 | tf_op jit(solution)/shard_map/ppermute | solution.py:536
  13.0 0.0 copy-start.1
  13.0 0.9 %copy-done.1 = bf16[216,256]{1,0:T(8,128)(2,1)S(1)} copy-done((bf16[216,256]{1,0:T(8,128)(2,1)S(1)}, bf16[216,256]{1,0:T(8,128)(2,1)}, u32[]{:S(2)}) %copy-start.1) | copy-done | bytes 110616
  13.9 0.7 %copy-done.2 = bf16[256,24]{0,1:T(8,128)(2,1)S(1)} copy-done((bf16[256,24]{0,1:T(8,128)(2,1)S(1)}, bf16[256,24]{0,1:T(8,128)(2,1)}, u32[]{:S(2)}) %copy-start.2) | copy-done | bytes 12312
  14.6 0.7 %copy-done.3 = f32[256]{0:T(256)S(1)} copy-done((f32[256]{0:T(256)S(1)}, f32[256]{0:T(256)}, u32[]{:S(2)}) %copy-start.3) | copy-done | bytes 1048
  15.3 0.7 %copy-done.4 = s32[1,1,256]{2,1,0:T(1,128)S(1)} copy-done((s32[1,1,256]{2,1,0:T(1,128)S(1)}, s32[1,1,256]{2,1,0:T(1,128)}, u32[]{:S(2)}) %copy-start.4) | copy-done | bytes 1048
  15.9 0.1 prepare.1
  16.1 0.0 collective-permute-done.3.from_right_ref
  16.1 0.0 copy-start.5
  16.1 0.7 %copy-done.5 = f32[1,1,256]{2,1,0:T(1,128)S(1)} copy-done((f32[1,1,256]{2,1,0:T(1,128)S(1)}, f32[1,1,256]{2,1,0:T(1,128)}, u32[]{:S(2)}) %copy-start.5) | copy-done | bytes 1048
  16.8 0.7 %copy-done.6 = f32[1,1,256]{2,1,0:T(1,128)S(1)} copy-done((f32[1,1,256]{2,1,0:T(1,128)S(1)}, f32[1,1,256]{2,1,0:T(1,128)}, u32[]{:S(2)}) %copy-start.6) | copy-done | bytes 1048
  17.5 9.9 %forecast.1 = (bf16[1536,128]{1,0:T(8,128)(2,1)S(1)}, bf16[32,4,128]{2,1,0:T(4,128)(2,1)S(1)}) custom-call(s32[2,128]{1,0:T(2,128)S(1)} %get-tuple-element.26.spot_ref, s32[1,1]{1,0:T(1,128)S(6)} %copy.9.count_ref, bf16[5120,128]{1,0:T(8,128)(2,1)S(1)} %get-tuple-element.27.taps_ref, bf16[48,128]{1,0:T(8,128)(2,1)S(1)} %collective-permute-done.north_ref, ...), custom_call_target="tpu_custom_call" | custom-call | tf_op jit(solution)/shard_map/forecast/pallas_call | solution.py:312
  27.4 1.6 %collective-permute-start.4 = (bf16[1536,128]{1,0:T(8,128)(2,1)S(1)}, bf16[1536,128]{1,0:T(8,128)(2,1)S(1)}, u32[]{:S(2)}, u32[]{:S(2)}) collective-permute-start(bf16[1536,128]{1,0:T(8,128)(2,1)S(1)} %get-tuple-element.34.mine_ref), channel_id=1, source_target_pairs={{0,16},{16,0},{1,17},{17,1},{2,18},{18,2},{3,19},{19,3},{4,20},{20... | collective-permute-start | bytes 1179656 | tf_op jit(solution)/shard_map/ppermute | solution.py:561
  29.0 10.9 %all_to_all.5.told_ref = bf16[32,4,128]{2,1,0:T(4,128)(2,1)S(1)} all-to-all(bf16[32,4,128]{2,1,0:T(4,128)(2,1)S(1)} %get-tuple-element.33), channel_id=1, replica_groups=mesh['ens'=2,'lat'=4,'lon'=4] {'ens','lat','lon'}, dimensions={0} | all-to-all | bytes 65536 | tf_op jit(solution)/shard_map/all_to_all | solution.py:559
  39.9 1.3 %analysis.1 = bf16[24,64,128]{2,1,0:T(8,128)(2,1)} custom-call(bf16[32,4,128]{2,1,0:T(4,128)(2,1)S(1)} %all_to_all.5.told_ref, bf16[1536,128]{1,0:T(8,128)(2,1)S(1)} %get-tuple-element.34.mine_ref, bf16[1536,128]{1,0:T(8,128)(2,1)S(1)} %collective-permute-done.4.other_ref), custom_call_target="tpu_custom_call" | custom-call | tf_op jit(solution)/shard_map/analysis/pallas_call | solution.py:413
  (7 shorter events, 0.0 us)
Async XLA Ops:
  0.0 1.0 %copy-start = (bf16[1,24,64,128]{3,2,1,0:T(8,128)(2,1)S(1)}, bf16[1,24,64,128]{3,2,1,0:T(8,128)(2,1)}, u32[]{:S(2)}) copy-start(bf16[1,24,64,128]{3,2,1,0:T(8,128)(2,1)} %param.8) | copy-start | bytes 1179652
  1.1 8.1 %collective-permute-start = (bf16[48,128]{1,0:T(8,128)(2,1)S(1)}, bf16[48,128]{1,0:T(8,128)(2,1)S(1)}, u32[]{:S(2)}, u32[]{:S(2)}) collective-permute-start(bf16[48,128]{1,0:T(8,128)(2,1)S(1)} %get-tuple-element.21), channel_id=1, source_target_pairs={{0,4},{4,8},{8,12},{1,5},{5,9},{9,13},{2,6},{6,10},{10,14},{3,7},{... | collective-permute-start | bytes 36872 | tf_op jit(solution)/shard_map/ppermute | solution.py:532
  6.1 5.6 %collective-permute-start.1 = (bf16[48,128]{1,0:T(8,128)(2,1)S(1)}, bf16[48,128]{1,0:T(8,128)(2,1)S(1)}, u32[]{:S(2)}, u32[]{:S(2)}) collective-permute-start(bf16[48,128]{1,0:T(8,128)(2,1)S(1)} %get-tuple-element.22), channel_id=1, source_target_pairs={{4,0},{8,4},{12,8},{5,1},{9,5},{13,9},{6,2},{10,6},{14,10},{7,3},{... | collective-permute-start | bytes 36872 | tf_op jit(solution)/shard_map/ppermute | solution.py:533
  11.8 4.3 %collective-permute-start.3 = (bf16[48,128]{1,0:T(8,128)(2,1)S(1)}, bf16[48,128]{1,0:T(8,128)(2,1)S(1)}, u32[]{:S(2)}, u32[]{:S(2)}) collective-permute-start(bf16[48,128]{1,0:T(8,128)(2,1)S(1)} %get-tuple-element.28.own_left_ref), channel_id=1, source_target_pairs={{1,0},{2,1},{3,2},{0,3},{5,4},{6,5},{7,6},{4,7},{9,8},{10,9},{11,1... | collective-permute-start | bytes 36872 | tf_op jit(solution)/shard_map/ppermute | solution.py:537
  11.8 4.3 %collective-permute-start.2 = (bf16[48,128]{1,0:T(8,128)(2,1)S(1)}, bf16[48,128]{1,0:T(8,128)(2,1)S(1)}, u32[]{:S(2)}, u32[]{:S(2)}) collective-permute-start(bf16[48,128]{1,0:T(8,128)(2,1)S(1)} %get-tuple-element.29.own_right_ref), channel_id=1, source_target_pairs={{0,1},{1,2},{2,3},{3,0},{4,5},{5,6},{6,7},{7,4},{8,9},{9,10},{10,1... | collective-permute-start | bytes 36872 | tf_op jit(solution)/shard_map/ppermute | solution.py:536
  13.0 0.9 %copy-start.1 = (bf16[216,256]{1,0:T(8,128)(2,1)S(1)}, bf16[216,256]{1,0:T(8,128)(2,1)}, u32[]{:S(2)}) copy-start(bf16[216,256]{1,0:T(8,128)(2,1)} %conv_ref.1) | copy-start | bytes 331780
  13.9 0.7 %copy-start.2 = (bf16[256,24]{0,1:T(8,128)(2,1)S(1)}, bf16[256,24]{0,1:T(8,128)(2,1)}, u32[]{:S(2)}) copy-start(bf16[256,24]{0,1:T(8,128)(2,1)} %param.11) | copy-start | bytes 36868
  14.6 0.7 %copy-start.3 = (f32[256]{0:T(256)S(1)}, f32[256]{0:T(256)}, u32[]{:S(2)}) copy-start(f32[256]{0:T(256)} %param.10) | copy-start | bytes 3076
  15.3 0.7 %copy-start.4 = (s32[1,1,256]{2,1,0:T(1,128)S(1)}, s32[1,1,256]{2,1,0:T(1,128)}, u32[]{:S(2)}) copy-start(s32[1,1,256]{2,1,0:T(1,128)} %param.12) | copy-start | bytes 3076
  16.1 0.7 %copy-start.5 = (f32[1,1,256]{2,1,0:T(1,128)S(1)}, f32[1,1,256]{2,1,0:T(1,128)}, u32[]{:S(2)}) copy-start(f32[1,1,256]{2,1,0:T(1,128)} %param.14) | copy-start | bytes 3076
  16.8 0.7 %copy-start.6 = (f32[1,1,256]{2,1,0:T(1,128)S(1)}, f32[1,1,256]{2,1,0:T(1,128)}, u32[]{:S(2)}) copy-start(f32[1,1,256]{2,1,0:T(1,128)} %param.15) | copy-start | bytes 3076
  27.4 12.5 %collective-permute-start.4 = (bf16[1536,128]{1,0:T(8,128)(2,1)S(1)}, bf16[1536,128]{1,0:T(8,128)(2,1)S(1)}, u32[]{:S(2)}, u32[]{:S(2)}) collective-permute-start(bf16[1536,128]{1,0:T(8,128)(2,1)S(1)} %get-tuple-element.34.mine_ref), channel_id=1, source_target_pairs={{0,16},{16,0},{1,17},{17,1},{2,18},{18,2},{3,19},{19,3},{4,20},{20... | collective-permute-start | bytes 1179656 | tf_op jit(solution)/shard_map/ppermute | solution.py:561

commit v5 on v4

--- a/solution.py
+++ b/solution.py
@@ -53,10 +53,10 @@
         ],
         compiler_params=pltpu.CompilerParams(vmem_limit_bytes=SMALL),
         name="edge_rows",
-    )(x)
-
-
-def spread_kernel(x_ref, taps_ref, own_ref, stage, xf):
+    )(pltpu.with_memory_space_constraint(x, pltpu.HBM))
+
+
+def spread_kernel(x_hbm, taps_ref, own_ref, x_ref, stage, xf, sems):
     nvar, rows, cols = x_ref.shape
     block = 3 * nvar + PAD
     wanted = (0, 1, cols - 2, cols - 1)
@@ -67,11 +67,20 @@
         pick = jnp.where((k == i) & (lane == c), 1.0, pick)
     pick = pick.astype(BF16)
     per = cols // rows
-    flat = x_ref[...].reshape(nvar * rows, cols)
+    parts = sems.shape[0]
+    each = nvar // parts
+    copies = []
+    for i in range(parts):
+        part = slice(i * each, (i + 1) * each)
+        copies.append(pltpu.make_async_copy(x_hbm.at[part], x_ref.at[part], sems.at[i]))
+        copies[i].start()
     for v in range(nvar):
+        if v % each == 0:
+            copies[v // each].wait()
         column = x_ref[v].astype(F32)
         for r in range(0, rows, 8):
             xf[pl.ds(r * nvar + v, 8, stride=nvar), :] = column[r : r + 8]
+    flat = x_ref[...].reshape(nvar * rows, cols)
     taken = lax.dot_general(pick, flat, (((1,), (1,)), ((), ())), preferred_element_type=F32)
     for v in range(nvar):
         part = taken[:, (v // per) * cols : (v // per + 1) * cols]
@@ -100,11 +109,17 @@
             jax.ShapeDtypeStruct((rows * block, cols), BF16),
             jax.ShapeDtypeStruct((4 * nvar, cols), F32),
         ),
-        scratch_shapes=[pltpu.VMEM((8 * nvar, cols), F32), pltpu.VMEM((nvar * rows, cols), F32)],
+        in_specs=[pl.BlockSpec(memory_space=pltpu.HBM)],
+        scratch_shapes=[
+            pltpu.VMEM((nvar, rows, cols), BF16),
+            pltpu.VMEM((8 * nvar, cols), F32),
+            pltpu.VMEM((nvar * rows, cols), F32),
+            pltpu.SemaphoreType.DMA((most_of(nvar, 4),)),
+        ],
         compiler_params=pltpu.CompilerParams(vmem_limit_bytes=SMALL),
         cost_estimate=pl.CostEstimate(flops=10**8, bytes_accessed=4 * 10**6, transcendentals=0),
         name="spread",
-    )(x)
+    )(pltpu.with_memory_space_constraint(x, pltpu.HBM))
 
 
 def edge_columns(own, north, south, rows):
@@ -144,7 +159,6 @@
 
 def forecast_kernel(
     spot_ref,
-    count_ref,
     taps_ref,
     north_ref,
     south_ref,
@@ -155,8 +169,7 @@
     conv_ref,
     out_w_ref,
     chosen_ref,
-    value_ref,
-    weight_ref,
+    extra_ref,
     forecast_ref,
     notes_ref,
     first,
@@ -281,28 +294,25 @@
     group2 = most_of(rows // 2, hidden.shape[0])
     lax.fori_loop(0, (rows // 2) // group2, second_step, 0)
 
-    def look(o, carry):
-        seen[pl.ds(o, 1), :] = final[pl.ds(spot_ref[o // cols, o % cols], 1), :]
-        return carry
-
-    slots = seen.shape[0]
-    lax.fori_loop(0, slots, look, 0, unroll=16)
+    for half in range(spot_ref.shape[0]):
+
+        def look(o, carry, half=half):
+            seen[pl.ds(half * cols + o, 1), :] = final[pl.ds(spot_ref[half, o], 1), :]
+            return carry
+
+        lax.fori_loop(0, cols, look, 0, unroll=32)
     masked = seen[...].astype(BF16) * chosen_ref[...]
     values = lax.dot_general(
         jnp.ones((8, cols), BF16), masked, (((1,), (1,)), ((), ())), preferred_element_type=F32
     )
-    fold = value_ref.shape[0]
-    live = lanes_of((fold, cols)) + cols * lax.broadcasted_iota(jnp.int32, (fold, cols), 0) < count_ref[0, 0]
-    member = lax.axis_index("ens")
-    weight = jnp.where(live, weight_ref[...], 0.0)
-    extra = jnp.where(member == 0, value_ref[...], jnp.where(member == 1, weight, 0.0))
-    note = [values[0:1, i * cols : (i + 1) * cols] for i in range(fold)] + [extra]
+    fold = extra_ref.shape[0]
+    note = [values[0:1, i * cols : (i + 1) * cols] for i in range(fold)] + [extra_ref[...]]
     note = jnp.concatenate(note, axis=0).astype(BF16)
     for d in range(notes_ref.shape[0]):
         notes_ref[d] = note
 
 
-def run_forecast(spot, count, taps, north, south, own_left, own_right, from_left, from_right, conv, out_w, chosen, value, weight, devices):
+def run_forecast(spot, taps, north, south, own_left, own_right, from_left, from_right, conv, out_w, chosen, extra, devices):
     nvar, cols = north.shape[0] // 2, north.shape[1]
     slots = spot.shape[0] * spot.shape[1]
     block = 3 * nvar + PAD
@@ -313,9 +323,9 @@
         forecast_kernel,
         out_shape=(
             jax.ShapeDtypeStruct((rows * nvar, cols), BF16),
-            jax.ShapeDtypeStruct((devices, 2 * value.shape[0], cols), BF16),
+            jax.ShapeDtypeStruct((devices, 2 * extra.shape[0], cols), BF16),
         ),
-        in_specs=[smem, smem] + [vmem] * 12,
+        in_specs=[smem] + [vmem] * 11,
         out_specs=(vmem, vmem),
         scratch_shapes=[
             pltpu.VMEM(((rows + 4) * block, cols), BF16),
@@ -326,7 +336,7 @@
         ],
         compiler_params=pltpu.CompilerParams(vmem_limit_bytes=16 << 20),
         name="forecast",
-    )(spot, count, taps, north, south, own_left, own_right, from_left, from_right, conv, out_w, chosen, value, weight)
+    )(spot, taps, north, south, own_left, own_right, from_left, from_right, conv, out_w, chosen, extra)
 
 
 def pair_weights(gram, proj):
@@ -463,13 +473,15 @@
     return blended.astype(BF16).reshape(rows, nvar, cols).transpose(1, 0, 2)
 
 
-def prepare(conv_weight, conv_bias, out_weight, index, shape):
+def prepare(conv_weight, conv_bias, out_weight, index, count, value, weight, shape):
     nvar, rows, cols = shape
     fold = index.shape[0]
     hid = conv_bias.shape[0]
     block = 3 * nvar + PAD
 
-    def kernel(conv_ref, bias_ref, out_ref, index_ref, packed_ref, half_ref, spot_ref, chosen_ref):
+    def kernel(
+        count_ref, conv_ref, bias_ref, out_ref, index_ref, value_ref, weight_ref, packed_ref, half_ref, spot_ref, chosen_ref, extra_ref
+    ):
         bias = bias_ref[...]
         high = bias.astype(BF16).astype(F32)
         middle = (bias - high).astype(BF16).astype(F32)
@@ -495,6 +507,10 @@
             across = jnp.broadcast_to(lane[i : i + 1, :], (cols, cols)).T
             hot = across == lanes_of((cols, cols)).astype(F32)
             chosen_ref[i * cols : (i + 1) * cols, :] = jnp.where(hot, 1.0, 0.0).astype(BF16)
+        slot = lanes_of((fold, cols)) + cols * lax.broadcasted_iota(jnp.int32, (fold, cols), 0)
+        live = jnp.where(slot < count_ref[0, 0], weight_ref[...], 0.0)
+        member = lax.axis_index("ens")
+        extra_ref[...] = jnp.where(member == 0, value_ref[...], jnp.where(member == 1, live, 0.0))
 
     return pl.pallas_call(
         kernel,
@@ -503,11 +519,19 @@
             jax.ShapeDtypeStruct((nvar, hid), BF16),
             jax.ShapeDtypeStruct((fold, cols), jnp.int32),
             jax.ShapeDtypeStruct((fold * cols, cols), BF16),
+            jax.ShapeDtypeStruct((fold, cols), F32),
         ),
+        in_specs=[pl.BlockSpec(memory_space=pltpu.SMEM)] + [pl.BlockSpec(memory_space=pltpu.VMEM)] * 6,
         compiler_params=pltpu.CompilerParams(vmem_limit_bytes=SMALL),
         cost_estimate=pl.CostEstimate(flops=10**7, bytes_accessed=10**6, transcendentals=0),
         name="prepare",
-    )(conv_weight, conv_bias[None], out_weight.T, index)
+    )(
+        count,
+        *(
+            pltpu.with_memory_space_constraint(entry, pltpu.HBM)
+            for entry in (conv_weight, conv_bias[None], out_weight.T, index, value, weight)
+        ),
+    )
 
 
 def per_device(
@@ -538,10 +562,18 @@
 
     fold = (obs_index.size // cols, cols)
     index, own_left, own_right = lax.optimization_barrier((obs_index, own_left, own_right))
-    conv, out_w, spot, chosen = prepare(conv_weight, conv_bias, out_weight, index.reshape(fold), x.shape)
+    conv, out_w, spot, chosen, extra = prepare(
+        conv_weight,
+        conv_bias,
+        out_weight,
+        index.reshape(fold),
+        obs_count,
+        obs_value.reshape(fold),
+        obs_weight.reshape(fold),
+        x.shape,
+    )
     forecast, notes = run_forecast(
         spot,
-        obs_count,
         taps,
         north,
         south,
@@ -552,8 +584,7 @@
         conv,
         out_w,
         chosen,
-        obs_value.reshape(fold),
-        obs_weight.reshape(fold),
+        extra,
         n_ens * n_lat * n_lon,
     )
     told = lax.all_to_all(notes, ("ens", "lat", "lon"), 0, 0, tiled=True)

time: 41.6 us -> 37.9 us (0.911)
  local copies, waits for them, and re-layouts: 5.3 us -> 0 us
  Pallas kernels: 13.3 us -> 14.6 us
  blocking collectives: 10.9 us -> 11.4 us
    unnamed x14 -> x0, local copies, waits for them, and re-layouts: 5.3 us -> none
    pallas_call x1, Pallas kernels: 9.89 us -> 8.4 us  [run_forecast(): pl.pallas_call(forecast_kernel, out_shape=(jax.ShapeDtypeStruct((rows * n...]
    ppermute x1, waiting for transfers between devices: 0.01 us -> 1.03 us  [per_device(): from_left = lax.ppermute(own_right, 'lon', right_lon)]
    pallas_call x1, Pallas kernels: 0.15 us -> 1.09 us  [prepare(): pl.pallas_call(kernel, out_shape=(jax.ShapeDtypeStruct((hid, 3 * block),...]
    ppermute x1, waiting for transfers between devices: 2.48 us -> 1.53 us  [per_device(): south = lax.ppermute(first_rows, 'lat', up_lat)]
    pallas_call x1, Pallas kernels: 1.8 us -> 2.74 us  [spread(): pl.pallas_call(spread_kernel, out_shape=(jax.ShapeDtypeStruct((rows * blo...]
    pallas_call x1, Pallas kernels: 0.1 us -> 0.98 us  [edge_rows(): pl.pallas_call(kernel, out_shape=(out, out), in_specs=[pl.BlockSpec(memor...]
    all_to_all x1, blocking collectives: 10.9 us -> 11.4 us  [per_device(): told = lax.all_to_all(notes, ('ens', 'lat', 'lon'), 0, 0, tiled=True)]
  transfers between devices with their start and end apart: 5 -> 5, of which waited for: 1 -> 2; matrix products, arithmetic and copies ran while one was open for 0% -> 0% of each run, Pallas kernels for 5% -> 10%
where the time goes in v5:
time: 37.9 us; the launch traced here: 37.7 us
  Pallas kernels  14.6 us (39%)
  blocking collectives  11.4 us (30%)
  starting transfers between devices  8.39 us (22%)
  waiting for transfers between devices  2.57 us (7%)
  between operations  0.73 us (2%)
    all_to_all x1, blocking collectives, per_device(): told = lax.all_to_all(notes, ('ens', 'lat', 'lon'), 0, 0, tiled=True)  11.4 us
    pallas_call x1, Pallas kernels, run_forecast(): pl.pallas_call(forecast_kernel, out_shape=(jax.ShapeDtypeStruct((rows * n...  8.4 us
    ppermute x1, starting transfers between devices, per_device(): north = lax.ppermute(last_rows, 'lat', down_lat)  4.96 us
    pallas_call x1, Pallas kernels, spread(): pl.pallas_call(spread_kernel, out_shape=(jax.ShapeDtypeStruct((rows * blo...  2.74 us
    ppermute x1, starting transfers between devices, per_device(): other = lax.ppermute(forecast, 'ens', [(0, 1), (1, 0)])  1.58 us
    ppermute x1, waiting for transfers between devices, per_device(): south = lax.ppermute(first_rows, 'lat', up_lat)  1.53 us
    pallas_call x1, Pallas kernels, run_analysis(): pl.pallas_call(analysis_kernel, out_shape=jax.ShapeDtypeStruct(shape, BF1...  1.3 us
    ppermute x1, starting transfers between devices, per_device(): south = lax.ppermute(first_rows, 'lat', up_lat)  1.29 us
  transfers between devices with their start and end apart: 5, of which 2 were waited for; matrix products, arithmetic and copies ran while one was open for 0% of the time, Pallas kernels for 10%

profile of v5, /device:TPU:0, one launch (start us, length us, event | category | flops | bytes accessed | tf_op | source)
XLA Modules:
  0.0 37.7 jit_solution(5335125880383880220)
XLA Ops:
  0.0 1.0 %edge_rows.1 = (bf16[48,128]{1,0:T(8,128)(2,1)S(1)}, bf16[48,128]{1,0:T(8,128)(2,1)S(1)}) custom-call(bf16[24,64,128]{2,1,0:T(8,128)(2,1)} %bitcast.7), custom_call_target="tpu_custom_call" | custom-call | tf_op jit(solution)/shard_map/edge_rows/pallas_call | solution.py:45
  1.0 5.0 %collective-permute-start = (bf16[48,128]{1,0:T(8,128)(2,1)S(1)}, bf16[48,128]{1,0:T(8,128)(2,1)S(1)}, u32[]{:S(2)}, u32[]{:S(2)}) collective-permute-start(bf16[48,128]{1,0:T(8,128)(2,1)S(1)} %get-tuple-element.22), channel_id=1, source_target_pairs={{0,4},{4,8},{8,12},{1,5},{5,9},{9,13},{2,6},{6,10},{10,14},{3,7},{... | collective-permute-start | bytes 36872 | tf_op jit(solution)/shard_map/ppermute | solution.py:556
  6.0 1.3 %collective-permute-start.1 = (bf16[48,128]{1,0:T(8,128)(2,1)S(1)}, bf16[48,128]{1,0:T(8,128)(2,1)S(1)}, u32[]{:S(2)}, u32[]{:S(2)}) collective-permute-start(bf16[48,128]{1,0:T(8,128)(2,1)S(1)} %get-tuple-element.23), channel_id=1, source_target_pairs={{4,0},{8,4},{12,8},{5,1},{9,5},{13,9},{6,2},{10,6},{14,10},{7,3},{... | collective-permute-start | bytes 36872 | tf_op jit(solution)/shard_map/ppermute | solution.py:557
  7.3 2.7 %spread.1 = (bf16[5120,128]{1,0:T(8,128)(2,1)S(1)}, f32[96,128]{1,0:T(8,128)S(1)}) custom-call(bf16[24,64,128]{2,1,0:T(8,128)(2,1)} %bitcast.8), custom_call_target="tpu_custom_call" | custom-call | flops 100000000 | bytes 4000000 | tf_op jit(solution)/shard_map/spread/pallas_call | solution.py:106
  10.0 0.0 collective-permute-done.north_ref
  10.0 1.5 %collective-permute-done.1.south_ref = bf16[48,128]{1,0:T(8,128)(2,1)S(1)} collective-permute-done((bf16[48,128]{1,0:T(8,128)(2,1)S(1)}, bf16[48,128]{1,0:T(8,128)(2,1)S(1)}, u32[]{:S(2)}, u32[]{:S(2)}) %collective-permute-start.1) | collective-permute-done | bytes 12320 | tf_op jit(solution)/shard_map/ppermute | solution.py:557
  11.5 0.1 edge_columns.1
  11.6 0.1 collective-permute-start.3
  11.7 0.5 %collective-permute-start.2 = (bf16[48,128]{1,0:T(8,128)(2,1)S(1)}, bf16[48,128]{1,0:T(8,128)(2,1)S(1)}, u32[]{:S(2)}, u32[]{:S(2)}) collective-permute-start(bf16[48,128]{1,0:T(8,128)(2,1)S(1)} %get-tuple-element.30.own_right_ref), channel_id=1, source_target_pairs={{0,1},{1,2},{2,3},{3,0},{4,5},{5,6},{6,7},{7,4},{8,9},{9,10},{10,1... | collective-permute-start | bytes 36872 | tf_op jit(solution)/shard_map/ppermute | solution.py:560
  12.9 1.1 %prepare.1 = (bf16[256,240]{1,0:T(8,128)(2,1)S(1)}, bf16[24,256]{1,0:T(8,128)(2,1)S(1)}, s32[2,128]{1,0:T(2,128)S(1)}, bf16[256,128]{1,0:T(8,128)(2,1)S(1)}, f32[2,128]{1,0:T(2,128)S(1)}) custom-call(s32[1,1]{1,0:T(1,128)S(6)} %copy.9.count_ref, bf16[216,256]{1,0:T(8,128)(2,1)} %conv_ref.1, f32[1,256]{1,0:T(1,128)} %bitcast.10, bf16[24,256]{1,0:T(8,128)(2,1)} %bitcast.9, ...), custom_call_target="tpu_custom_call" | custom-call | flops 10000000 | bytes 1000000 | tf_op jit(solution)/shard_map/prepare/pallas_call | solution.py:515
  14.0 0.0 collective-permute-done.3.from_right_ref
  14.0 1.0 %collective-permute-done.2.from_left_ref = bf16[48,128]{1,0:T(8,128)(2,1)S(1)} collective-permute-done((bf16[48,128]{1,0:T(8,128)(2,1)S(1)}, bf16[48,128]{1,0:T(8,128)(2,1)S(1)}, u32[]{:S(2)}, u32[]{:S(2)}) %collective-permute-start.2) | collective-permute-done | bytes 12320 | tf_op jit(solution)/shard_map/ppermute | solution.py:560
  15.0 8.4 %forecast.1 = (bf16[1536,128]{1,0:T(8,128)(2,1)S(1)}, bf16[32,4,128]{2,1,0:T(4,128)(2,1)S(1)}) custom-call(s32[2,128]{1,0:T(2,128)S(1)} %get-tuple-element.27.spot_ref, bf16[5120,128]{1,0:T(8,128)(2,1)S(1)} %get-tuple-element.28.taps_ref, bf16[48,128]{1,0:T(8,128)(2,1)S(1)} %collective-permute-done.north_ref, ...), custom_call_target="tpu_custom_call" | custom-call | tf_op jit(solution)/shard_map/forecast/pallas_call | solution.py:322
  23.4 1.6 %collective-permute-start.4 = (bf16[1536,128]{1,0:T(8,128)(2,1)S(1)}, bf16[1536,128]{1,0:T(8,128)(2,1)S(1)}, u32[]{:S(2)}, u32[]{:S(2)}) collective-permute-start(bf16[1536,128]{1,0:T(8,128)(2,1)S(1)} %get-tuple-element.36.mine_ref), channel_id=1, source_target_pairs={{0,16},{16,0},{1,17},{17,1},{2,18},{18,2},{3,19},{19,3},{4,20},{20... | collective-permute-start | bytes 1179656 | tf_op jit(solution)/shard_map/ppermute | solution.py:592
  25.0 11.4 %all_to_all.5.told_ref = bf16[32,4,128]{2,1,0:T(4,128)(2,1)S(1)} all-to-all(bf16[32,4,128]{2,1,0:T(4,128)(2,1)S(1)} %get-tuple-element.35), channel_id=1, replica_groups=mesh['ens'=2,'lat'=4,'lon'=4] {'ens','lat','lon'}, dimensions={0} | all-to-all | bytes 65536 | tf_op jit(solution)/shard_map/all_to_all | solution.py:590
  36.4 0.0 collective-permute-done.4.other_ref
  36.4 1.3 %analysis.1 = bf16[24,64,128]{2,1,0:T(8,128)(2,1)} custom-call(bf16[32,4,128]{2,1,0:T(4,128)(2,1)S(1)} %all_to_all.5.told_ref, bf16[1536,128]{1,0:T(8,128)(2,1)S(1)} %get-tuple-element.36.mine_ref, bf16[1536,128]{1,0:T(8,128)(2,1)S(1)} %collective-permute-done.4.other_ref), custom_call_target="tpu_custom_call" | custom-call | tf_op jit(solution)/shard_map/analysis/pallas_call | solution.py:423
Async XLA Ops:
  1.0 9.0 %collective-permute-start = (bf16[48,128]{1,0:T(8,128)(2,1)S(1)}, bf16[48,128]{1,0:T(8,128)(2,1)S(1)}, u32[]{:S(2)}, u32[]{:S(2)}) collective-permute-start(bf16[48,128]{1,0:T(8,128)(2,1)S(1)} %get-tuple-element.22), channel_id=1, source_target_pairs={{0,4},{4,8},{8,12},{1,5},{5,9},{9,13},{2,6},{6,10},{10,14},{3,7},{... | collective-permute-start | bytes 36872 | tf_op jit(solution)/shard_map/ppermute | solution.py:556
  6.0 5.6 %collective-permute-start.1 = (bf16[48,128]{1,0:T(8,128)(2,1)S(1)}, bf16[48,128]{1,0:T(8,128)(2,1)S(1)}, u32[]{:S(2)}, u32[]{:S(2)}) collective-permute-start(bf16[48,128]{1,0:T(8,128)(2,1)S(1)} %get-tuple-element.23), channel_id=1, source_target_pairs={{4,0},{8,4},{12,8},{5,1},{9,5},{13,9},{6,2},{10,6},{14,10},{7,3},{... | collective-permute-start | bytes 36872 | tf_op jit(solution)/shard_map/ppermute | solution.py:557
  11.6 2.3 %collective-permute-start.3 = (bf16[48,128]{1,0:T(8,128)(2,1)S(1)}, bf16[48,128]{1,0:T(8,128)(2,1)S(1)}, u32[]{:S(2)}, u32[]{:S(2)}) collective-permute-start(bf16[48,128]{1,0:T(8,128)(2,1)S(1)} %get-tuple-element.29.own_left_ref), channel_id=1, source_target_pairs={{1,0},{2,1},{3,2},{0,3},{5,4},{6,5},{7,6},{4,7},{9,8},{10,9},{11,1... | collective-permute-start | bytes 36872 | tf_op jit(solution)/shard_map/ppermute | solution.py:561
  11.7 3.3 %collective-permute-start.2 = (bf16[48,128]{1,0:T(8,128)(2,1)S(1)}, bf16[48,128]{1,0:T(8,128)(2,1)S(1)}, u32[]{:S(2)}, u32[]{:S(2)}) collective-permute-start(bf16[48,128]{1,0:T(8,128)(2,1)S(1)} %get-tuple-element.30.own_right_ref), channel_id=1, source_target_pairs={{0,1},{1,2},{2,3},{3,0},{4,5},{5,6},{6,7},{7,4},{8,9},{9,10},{10,1... | collective-permute-start | bytes 36872 | tf_op jit(solution)/shard_map/ppermute | solution.py:560
  23.4 13.0 %collective-permute-start.4 = (bf16[1536,128]{1,0:T(8,128)(2,1)S(1)}, bf16[1536,128]{1,0:T(8,128)(2,1)S(1)}, u32[]{:S(2)}, u32[]{:S(2)}) collective-permute-start(bf16[1536,128]{1,0:T(8,128)(2,1)S(1)} %get-tuple-element.36.mine_ref), channel_id=1, source_target_pairs={{0,16},{16,0},{1,17},{17,1},{2,18},{18,2},{3,19},{19,3},{4,20},{20... | collective-permute-start | bytes 1179656 | tf_op jit(solution)/shard_map/ppermute | solution.py:592

commit v6 on v5

--- a/solution.py
+++ b/solution.py
@@ -15,7 +15,7 @@
 BF16 = jnp.bfloat16
 PAD = 8
 SMALL = 4 << 20
-GROUP = 12
+GROUP = 34
 
 
 def lanes_of(shape):
@@ -56,9 +56,65 @@
     )(pltpu.with_memory_space_constraint(x, pltpu.HBM))
 
 
-def spread_kernel(x_hbm, taps_ref, own_ref, x_ref, stage, xf, sems):
+def packed_rows(conv, bias, nvar):
+    hid = bias.shape[1]
+    high = bias.astype(BF16).astype(F32)
+    middle = (bias - high).astype(BF16).astype(F32)
+    low = (bias - high - middle).astype(BF16).astype(F32)
+    rest = jnp.zeros((PAD - 3, hid), F32)
+    pieces = []
+    for a in range(3):
+        for b in (1, 0, 2):
+            at = (3 * a + b) * nvar
+            pieces.append(conv[at : at + nvar, :].astype(F32))
+        if a == 1:
+            pieces.append(jnp.concatenate([high, middle, low, rest], axis=0))
+        else:
+            pieces.append(jnp.zeros((PAD, hid), F32))
+    return jnp.concatenate(pieces, axis=0).T
+
+
+def spread_kernel(
+    x_hbm,
+    conv_hbm,
+    bias_hbm,
+    out_hbm,
+    index_hbm,
+    count_ref,
+    value_hbm,
+    weight_hbm,
+    taps_ref,
+    own_ref,
+    packed_ref,
+    half_ref,
+    extra_ref,
+    chosen_ref,
+    *rest,
+):
+    fold = extra_ref.shape[0]
+    spot_refs = rest[:fold]
+    x_ref, conv_ref, bias_ref, out_ref, index_ref, value_ref, weight_ref, stage, xf, sems = rest[fold:]
     nvar, rows, cols = x_ref.shape
     block = 3 * nvar + PAD
+    small = [
+        (conv_hbm, conv_ref),
+        (bias_hbm, bias_ref),
+        (out_hbm, out_ref),
+        (index_hbm, index_ref),
+        (value_hbm, value_ref),
+        (weight_hbm, weight_ref),
+    ]
+    parts = sems.shape[0] - len(small)
+    each = nvar // parts
+    copies = []
+    for i in range(parts):
+        part = slice(i * each, (i + 1) * each)
+        copies.append(pltpu.make_async_copy(x_hbm.at[part], x_ref.at[part], sems.at[i]))
+    for i, (source, target) in enumerate(small):
+        copies.append(pltpu.make_async_copy(source, target, sems.at[parts + i]))
+    for copy in copies:
+        copy.start()
+
     wanted = (0, 1, cols - 2, cols - 1)
     k = lax.broadcasted_iota(jnp.int32, (8, cols), 0)
     lane = lanes_of((8, cols))
@@ -67,13 +123,6 @@
         pick = jnp.where((k == i) & (lane == c), 1.0, pick)
     pick = pick.astype(BF16)
     per = cols // rows
-    parts = sems.shape[0]
-    each = nvar // parts
-    copies = []
-    for i in range(parts):
-        part = slice(i * each, (i + 1) * each)
-        copies.append(pltpu.make_async_copy(x_hbm.at[part], x_ref.at[part], sems.at[i]))
-        copies[i].start()
     for v in range(nvar):
         if v % each == 0:
             copies[v // each].wait()
@@ -97,29 +146,62 @@
         taps_ref[pl.ds(at, block), :] = tap.astype(BF16)
         return carry
 
-    lax.fori_loop(0, rows, fill, 0, unroll=4)
-
-
-def spread(x):
+    lax.fori_loop(0, rows, fill, 0, unroll=8)
+
+    for copy in copies[parts:]:
+        copy.wait()
+    packed_ref[...] = packed_rows(conv_ref[...], bias_ref[...], nvar).astype(BF16)
+    half_ref[...] = (out_ref[...].astype(F32) * 0.5).astype(BF16)
+    index = index_ref[...]
+    row = index // cols % rows
+    var = index // (rows * cols)
+    spot = jnp.clip(row * nvar + var, 0, rows * nvar - 1)
+    place = (index % cols).astype(F32)
+    for i in range(fold):
+        spot_refs[i][...] = spot[i : i + 1, :]
+        across = jnp.broadcast_to(place[i : i + 1, :], (cols, cols)).T
+        hot = across == lanes_of((cols, cols)).astype(F32)
+        chosen_ref[i * cols : (i + 1) * cols, :] = jnp.where(hot, 1.0, 0.0).astype(BF16)
+    slot = lanes_of((fold, cols)) + cols * lax.broadcasted_iota(jnp.int32, (fold, cols), 0)
+    live = jnp.where(slot < count_ref[0, 0], weight_ref[...], 0.0)
+    member = lax.axis_index("ens")
+    extra_ref[...] = jnp.where(member == 0, value_ref[...], jnp.where(member == 1, live, 0.0))
+
+
+def spread(x, conv_weight, conv_bias, out_weight, index, count, value, weight):
     nvar, rows, cols = x.shape
+    fold, hid = index.shape[0], conv_bias.shape[0]
     block = 3 * nvar + PAD
+    args = (x, conv_weight, conv_bias[None], out_weight.T, index, count, value, weight)
+    shape = jax.ShapeDtypeStruct
+    scratch = [pltpu.VMEM(arg.shape, arg.dtype) for arg in args]
+    del scratch[5]
+    in_specs = [pl.BlockSpec(memory_space=pltpu.HBM)] * len(args)
+    in_specs[5] = pl.BlockSpec(memory_space=pltpu.SMEM)
+    placed = [pltpu.with_memory_space_constraint(arg, pltpu.HBM) for arg in args]
+    placed[5] = count
     return pl.pallas_call(
         spread_kernel,
         out_shape=(
-            jax.ShapeDtypeStruct((rows * block, cols), BF16),
-            jax.ShapeDtypeStruct((4 * nvar, cols), F32),
-        ),
-        in_specs=[pl.BlockSpec(memory_space=pltpu.HBM)],
-        scratch_shapes=[
-            pltpu.VMEM((nvar, rows, cols), BF16),
+            shape((rows * block, cols), BF16),
+            shape((4 * nvar, cols), F32),
+            shape((hid, 3 * block), BF16),
+            shape((nvar, hid), BF16),
+            shape((fold, cols), F32),
+            shape((fold * cols, cols), BF16),
+        )
+        + (shape((1, cols), jnp.int32),) * fold,
+        in_specs=in_specs,
+        scratch_shapes=scratch
+        + [
             pltpu.VMEM((8 * nvar, cols), F32),
             pltpu.VMEM((nvar * rows, cols), F32),
-            pltpu.SemaphoreType.DMA((most_of(nvar, 4),)),
+            pltpu.SemaphoreType.DMA((most_of(nvar, 4) + len(args) - 2,)),
         ],
         compiler_params=pltpu.CompilerParams(vmem_limit_bytes=SMALL),
         cost_estimate=pl.CostEstimate(flops=10**8, bytes_accessed=4 * 10**6, transcendentals=0),
         name="spread",
-    )(pltpu.with_memory_space_constraint(x, pltpu.HBM))
+    )(*placed)
 
 
 def edge_columns(own, north, south, rows):
@@ -158,7 +240,11 @@
 
 
 def forecast_kernel(
-    spot_ref,
+    fold,
+    *refs,
+):
+    spot_refs = refs[:fold]
+    (
     taps_ref,
     north_ref,
     south_ref,
@@ -177,7 +263,9 @@
     final,
     hidden,
     seen,
-):
+    conv,
+    out_w,
+    ) = refs[fold:]
     nvar, cols = north_ref.shape[0] // 2, north_ref.shape[1]
     block = 3 * nvar + PAD
     rows = taps_ref.shape[0] // block
@@ -193,12 +281,14 @@
         return jnp.concatenate([row, left, right, ones], axis=0).astype(BF16)
 
     def hidden_of(patches):
-        return gelu2(jnp.dot(conv_ref[...], patches, preferred_element_type=F32))
+        return gelu2(jnp.dot(conv[...], patches, preferred_element_type=F32))
 
     def moved(centre, hidden):
-        change = jnp.dot(out_w_ref[...], hidden, preferred_element_type=F32)
+        change = jnp.dot(out_w[...], hidden, preferred_element_type=F32)
         return (centre + change).astype(BF16).astype(F32)
 
+    conv[...] = conv_ref[...]
+    out_w[...] = out_w_ref[...]
     from_left = from_left_ref[...].astype(F32)
     from_right = from_right_ref[...].astype(F32)
     own_left = own_left_ref[...].astype(F32)
@@ -294,10 +384,10 @@
     group2 = most_of(rows // 2, hidden.shape[0])
     lax.fori_loop(0, (rows // 2) // group2, second_step, 0)
 
-    for half in range(spot_ref.shape[0]):
+    for half in range(fold):
 
         def look(o, carry, half=half):
-            seen[pl.ds(half * cols + o, 1), :] = final[pl.ds(spot_ref[half, o], 1), :]
+            seen[pl.ds(half * cols + o, 1), :] = final[pl.ds(spot_refs[half][0, o], 1), :]
             return carry
 
         lax.fori_loop(0, cols, look, 0, unroll=32)
@@ -305,7 +395,6 @@
     values = lax.dot_general(
         jnp.ones((8, cols), BF16), masked, (((1,), (1,)), ((), ())), preferred_element_type=F32
     )
-    fold = extra_ref.shape[0]
     note = [values[0:1, i * cols : (i + 1) * cols] for i in range(fold)] + [extra_ref[...]]
     note = jnp.concatenate(note, axis=0).astype(BF16)
     for d in range(notes_ref.shape[0]):
@@ -314,18 +403,18 @@
 
 def run_forecast(spot, taps, north, south, own_left, own_right, from_left, from_right, conv, out_w, chosen, extra, devices):
     nvar, cols = north.shape[0] // 2, north.shape[1]
-    slots = spot.shape[0] * spot.shape[1]
+    slots = len(spot) * cols
     block = 3 * nvar + PAD
     rows = taps.shape[0] // block
     smem = pl.BlockSpec(memory_space=pltpu.SMEM)
     vmem = pl.BlockSpec(memory_space=pltpu.VMEM)
     return pl.pallas_call(
-        forecast_kernel,
+        functools.partial(forecast_kernel, len(spot)),
         out_shape=(
             jax.ShapeDtypeStruct((rows * nvar, cols), BF16),
             jax.ShapeDtypeStruct((devices, 2 * extra.shape[0], cols), BF16),
         ),
-        in_specs=[smem] + [vmem] * 11,
+        in_specs=[smem] * len(spot) + [vmem] * 11,
         out_specs=(vmem, vmem),
         scratch_shapes=[
             pltpu.VMEM(((rows + 4) * block, cols), BF16),
@@ -333,10 +422,12 @@
             pltpu.VMEM((rows * nvar, cols), F32),
             pltpu.VMEM((GROUP, conv.shape[0], 2 * cols), BF16),
             pltpu.VMEM((slots, cols), F32),
+            pltpu.VMEM(conv.shape, BF16),
+            pltpu.VMEM(out_w.shape, BF16),
         ],
-        compiler_params=pltpu.CompilerParams(vmem_limit_bytes=16 << 20),
+        compiler_params=pltpu.CompilerParams(vmem_limit_bytes=24 << 20),
         name="forecast",
-    )(spot, taps, north, south, own_left, own_right, from_left, from_right, conv, out_w, chosen, extra)
+    )(*spot, taps, north, south, own_left, own_right, from_left, from_right, conv, out_w, chosen, extra)
 
 
 def pair_weights(gram, proj):
@@ -473,67 +564,6 @@
     return blended.astype(BF16).reshape(rows, nvar, cols).transpose(1, 0, 2)
 
 
-def prepare(conv_weight, conv_bias, out_weight, index, count, value, weight, shape):
-    nvar, rows, cols = shape
-    fold = index.shape[0]
-    hid = conv_bias.shape[0]
-    block = 3 * nvar + PAD
-
-    def kernel(
-        count_ref, conv_ref, bias_ref, out_ref, index_ref, value_ref, weight_ref, packed_ref, half_ref, spot_ref, chosen_ref, extra_ref
-    ):
-        bias = bias_ref[...]
-        high = bias.astype(BF16).astype(F32)
-        middle = (bias - high).astype(BF16).astype(F32)
-        low = (bias - high - middle).astype(BF16).astype(F32)
-        rest = jnp.zeros((PAD - 3, hid), F32)
-        pieces = []
-        for a in range(3):
-            for b in (1, 0, 2):
-                at = (3 * a + b) * nvar
-                pieces.append(conv_ref[at : at + nvar, :].astype(F32))
-            if a == 1:
-                pieces.append(jnp.concatenate([high, middle, low, rest], axis=0))
-            else:
-                pieces.append(jnp.zeros((PAD, hid), F32))
-        packed_ref[...] = jnp.concatenate(pieces, axis=0).T.astype(BF16)
-        half_ref[...] = (out_ref[...].astype(F32) * 0.5).astype(BF16)
-        index = index_ref[...]
-        row = index // cols % rows
-        var = index // (rows * cols)
-        spot_ref[...] = jnp.clip(row * nvar + var, 0, rows * nvar - 1)
-        lane = (index % cols).astype(F32)
-        for i in range(fold):
-            across = jnp.broadcast_to(lane[i : i + 1, :], (cols, cols)).T
-            hot = across == lanes_of((cols, cols)).astype(F32)
-            chosen_ref[i * cols : (i + 1) * cols, :] = jnp.where(hot, 1.0, 0.0).astype(BF16)
-        slot = lanes_of((fold, cols)) + cols * lax.broadcasted_iota(jnp.int32, (fold, cols), 0)
-        live = jnp.where(slot < count_ref[0, 0], weight_ref[...], 0.0)
-        member = lax.axis_index("ens")
-        extra_ref[...] = jnp.where(member == 0, value_ref[...], jnp.where(member == 1, live, 0.0))
-
-    return pl.pallas_call(
-        kernel,
-        out_shape=(
-            jax.ShapeDtypeStruct((hid, 3 * block), BF16),
-            jax.ShapeDtypeStruct((nvar, hid), BF16),
-            jax.ShapeDtypeStruct((fold, cols), jnp.int32),
-            jax.ShapeDtypeStruct((fold * cols, cols), BF16),
-            jax.ShapeDtypeStruct((fold, cols), F32),
-        ),
-        in_specs=[pl.BlockSpec(memory_space=pltpu.SMEM)] + [pl.BlockSpec(memory_space=pltpu.VMEM)] * 6,
-        compiler_params=pltpu.CompilerParams(vmem_limit_bytes=SMALL),
-        cost_estimate=pl.CostEstimate(flops=10**7, bytes_accessed=10**6, transcendentals=0),
-        name="prepare",
-    )(
-        count,
-        *(
-            pltpu.with_memory_space_constraint(entry, pltpu.HBM)
-            for entry in (conv_weight, conv_bias[None], out_weight.T, index, value, weight)
-        ),
-    )
-
-
 def per_device(
     sample_quantities,
     conv_weight,
@@ -555,23 +585,21 @@
     first_rows, last_rows = edge_rows(x)
     north = lax.ppermute(last_rows, "lat", down_lat)
     south = lax.ppermute(first_rows, "lat", up_lat)
-    taps, own = spread(x)
+    fold = (obs_index.size // cols, cols)
+    taps, own, conv, out_w, extra, chosen, *spot = spread(
+        x,
+        conv_weight,
+        conv_bias,
+        out_weight,
+        obs_index.reshape(fold),
+        obs_count,
+        obs_value.reshape(fold),
+        obs_weight.reshape(fold),
+    )
     own_left, own_right = edge_columns(own, north, south, rows)
     from_left = lax.ppermute(own_right, "lon", right_lon)
     from_right = lax.ppermute(own_left, "lon", left_lon)
 
-    fold = (obs_index.size // cols, cols)
-    index, own_left, own_right = lax.optimization_barrier((obs_index, own_left, own_right))
-    conv, out_w, spot, chosen, extra = prepare(
-        conv_weight,
-        conv_bias,
-        out_weight,
-        index.reshape(fold),
-        obs_count,
-        obs_value.reshape(fold),
-        obs_weight.reshape(fold),
-        x.shape,
-    )
     forecast, notes = run_forecast(
         spot,
         taps,

time: 37.9 us -> 36.3 us (0.958)
  Pallas kernels: 14.6 us -> 11.3 us
  waiting for transfers between devices: 2.57 us -> 4.02 us
    pallas_call x3 -> x2, Pallas kernels: 12.2 us -> 8.9 us  [the longest x1 6.51 us: run_forecast(): pl.pallas_call(functools.partial(forecast_kernel, len(spot)), out_shape=(...]
    ppermute x1, waiting for transfers between devices: 0.01 us -> 0.9 us  [per_device(): from_right = lax.ppermute(own_left, 'lon', left_lon)]
    ppermute x1, waiting for transfers between devices: 1.03 us -> 1.89 us  [per_device(): from_left = lax.ppermute(own_right, 'lon', right_lon)]
  transfers between devices with their start and end apart: 5 -> 5, of which waited for: 2 -> 3; matrix products, arithmetic and copies ran while one was open for 0% -> 0% of each run, Pallas kernels for 10% -> 7%
where the time goes in v6:
time: 36.3 us; the launch traced here: 36.1 us
  blocking collectives  11.7 us (32%)
  Pallas kernels  11.3 us (31%)
  starting transfers between devices  8.39 us (23%)
  waiting for transfers between devices  4.02 us (11%)
  between operations  0.71 us (2%)
    all_to_all x1, blocking collectives, per_device(): told = lax.all_to_all(notes, ('ens', 'lat', 'lon'), 0, 0, tiled=True)  11.7 us
    pallas_call x1, Pallas kernels, run_forecast(): pl.pallas_call(functools.partial(forecast_kernel, len(spot)), out_shape=(...  6.51 us
    ppermute x1, starting transfers between devices, per_device(): north = lax.ppermute(last_rows, 'lat', down_lat)  4.96 us
    pallas_call x1, Pallas kernels, spread(): pl.pallas_call(spread_kernel, out_shape=(shape((rows * block, cols), BF16...  2.39 us
    ppermute x1, waiting for transfers between devices, per_device(): from_left = lax.ppermute(own_right, 'lon', right_lon)  1.89 us
    ppermute x1, starting transfers between devices, per_device(): other = lax.ppermute(forecast, 'ens', [(0, 1), (1, 0)])  1.59 us
    pallas_call x1, Pallas kernels, run_analysis(): pl.pallas_call(analysis_kernel, out_shape=jax.ShapeDtypeStruct(shape, BF1...  1.3 us
    ppermute x1, starting transfers between devices, per_device(): south = lax.ppermute(first_rows, 'lat', up_lat)  1.29 us
  transfers between devices with their start and end apart: 5, of which 3 were waited for; matrix products, arithmetic and copies ran while one was open for 0% of the time, Pallas kernels for 7%

profile of v6, /device:TPU:0, one launch (start us, length us, event | category | flops | bytes accessed | tf_op | source)
XLA Modules:
  0.0 36.1 jit_solution(6142653716261407352)
XLA Ops:
  0.0 1.0 %edge_rows.1 = (bf16[48,128]{1,0:T(8,128)(2,1)S(1)}, bf16[48,128]{1,0:T(8,128)(2,1)S(1)}) custom-call(bf16[24,64,128]{2,1,0:T(8,128)(2,1)} %bitcast.7), custom_call_target="tpu_custom_call" | custom-call | tf_op jit(solution)/shard_map/edge_rows/pallas_call | solution.py:45
  1.0 5.0 %collective-permute-start = (bf16[48,128]{1,0:T(8,128)(2,1)S(1)}, bf16[48,128]{1,0:T(8,128)(2,1)S(1)}, u32[]{:S(2)}, u32[]{:S(2)}) collective-permute-start(bf16[48,128]{1,0:T(8,128)(2,1)S(1)} %get-tuple-element.22), channel_id=1, source_target_pairs={{0,4},{4,8},{8,12},{1,5},{5,9},{9,13},{2,6},{6,10},{10,14},{3,7},{... | collective-permute-start | bytes 36872 | tf_op jit(solution)/shard_map/ppermute | solution.py:586
  6.0 1.3 %collective-permute-start.1 = (bf16[48,128]{1,0:T(8,128)(2,1)S(1)}, bf16[48,128]{1,0:T(8,128)(2,1)S(1)}, u32[]{:S(2)}, u32[]{:S(2)}) collective-permute-start(bf16[48,128]{1,0:T(8,128)(2,1)S(1)} %get-tuple-element.23), channel_id=1, source_target_pairs={{4,0},{8,4},{12,8},{5,1},{9,5},{13,9},{6,2},{10,6},{14,10},{7,3},{... | collective-permute-start | bytes 36872 | tf_op jit(solution)/shard_map/ppermute | solution.py:587
  7.9 2.4 %spread.1 = (bf16[5120,128]{1,0:T(8,128)(2,1)S(1)}, f32[96,128]{1,0:T(8,128)S(1)}, bf16[256,240]{1,0:T(8,128)(2,1)S(1)}, bf16[24,256]{1,0:T(8,128)(2,1)S(1)}, f3...) custom-call(bf16[24,64,128]{2,1,0:T(8,128)(2,1)} %bitcast.8, ...), custom_call_target="tpu_custom_call" | custom-call | flops 100000000 | bytes 4000000 | tf_op jit(solution)/shard_map/spread/pallas_call | solution.py:183
  10.3 0.0 collective-permute-done.north_ref.refs_3_
  10.3 1.2 %collective-permute-done.1.south_ref.refs_4_ = bf16[48,128]{1,0:T(8,128)(2,1)S(1)} collective-permute-done((bf16[48,128]{1,0:T(8,128)(2,1)S(1)}, bf16[48,128]{1,0:T(8,128)(2,1)S(1)}, u32[]{:S(2)}, u32[]{:S(2)}) %collective-permute-start.1) | collective-permute-done | bytes 12320 | tf_op jit(solution)/shard_map/ppermute | solution.py:587
  11.5 0.1 edge_columns.1
  11.6 0.1 collective-permute-start.3
  11.7 0.5 %collective-permute-start.2 = (bf16[48,128]{1,0:T(8,128)(2,1)S(1)}, bf16[48,128]{1,0:T(8,128)(2,1)S(1)}, u32[]{:S(2)}, u32[]{:S(2)}) collective-permute-start(bf16[48,128]{1,0:T(8,128)(2,1)S(1)} %get-tuple-element.26.refs_6_), channel_id=1, source_target_pairs={{0,1},{1,2},{2,3},{3,0},{4,5},{5,6},{6,7},{7,4},{8,9},{9,10},{10,1... | collective-permute-start | bytes 36872 | tf_op jit(solution)/shard_map/ppermute | solution.py:600
  12.2 0.9 %collective-permute-done.3.refs_8_ = bf16[48,128]{1,0:T(8,128)(2,1)S(1)} collective-permute-done((bf16[48,128]{1,0:T(8,128)(2,1)S(1)}, bf16[48,128]{1,0:T(8,128)(2,1)S(1)}, u32[]{:S(2)}, u32[]{:S(2)}) %collective-permute-start.3) | collective-permute-done | bytes 12320 | tf_op jit(solution)/shard_map/ppermute | solution.py:601
  13.1 1.9 %collective-permute-done.2.refs_7_ = bf16[48,128]{1,0:T(8,128)(2,1)S(1)} collective-permute-done((bf16[48,128]{1,0:T(8,128)(2,1)S(1)}, bf16[48,128]{1,0:T(8,128)(2,1)S(1)}, u32[]{:S(2)}, u32[]{:S(2)}) %collective-permute-start.2) | collective-permute-done | bytes 12320 | tf_op jit(solution)/shard_map/ppermute | solution.py:600
  15.0 6.5 %forecast.1 = (bf16[1536,128]{1,0:T(8,128)(2,1)S(1)}, bf16[32,4,128]{2,1,0:T(4,128)(2,1)S(1)}) custom-call(s32[1,128]{1,0:T(1,128)S(1)} %get-tuple-element.19.refs_0_, s32[1,128]{1,0:T(1,128)S(1)} %get-tuple-element.20.refs_1_, bf16[5120,128]{1,0:T(8,128)(2,1)S(1)} %get-tuple-element.21.refs_2_, bf16[48,128]{1,0:T(8,128)(2,1)S(1)} %collective-permute-done.north_ref.refs_3_, ...), custom_call_target="tpu_custom_call" | custom-call | tf_op jit(solution)/shard_map/forecast/pallas_call | solution.py:411
  21.5 1.6 %collective-permute-start.4 = (bf16[1536,128]{1,0:T(8,128)(2,1)S(1)}, bf16[1536,128]{1,0:T(8,128)(2,1)S(1)}, u32[]{:S(2)}, u32[]{:S(2)}) collective-permute-start(bf16[1536,128]{1,0:T(8,128)(2,1)S(1)} %get-tuple-element.32.mine_ref), channel_id=1, source_target_pairs={{0,16},{16,0},{1,17},{17,1},{2,18},{18,2},{3,19},{19,3},{4,20},{20... | collective-permute-start | bytes 1179656 | tf_op jit(solution)/shard_map/ppermute | solution.py:620
  23.1 11.7 %all_to_all.5.told_ref = bf16[32,4,128]{2,1,0:T(4,128)(2,1)S(1)} all-to-all(bf16[32,4,128]{2,1,0:T(4,128)(2,1)S(1)} %get-tuple-element.31), channel_id=1, replica_groups=mesh['ens'=2,'lat'=4,'lon'=4] {'ens','lat','lon'}, dimensions={0} | all-to-all | bytes 65536 | tf_op jit(solution)/shard_map/all_to_all | solution.py:618
  34.8 0.0 collective-permute-done.4.other_ref
  34.8 1.3 %analysis.1 = bf16[24,64,128]{2,1,0:T(8,128)(2,1)} custom-call(bf16[32,4,128]{2,1,0:T(4,128)(2,1)S(1)} %all_to_all.5.told_ref, bf16[1536,128]{1,0:T(8,128)(2,1)S(1)} %get-tuple-element.32.mine_ref, bf16[1536,128]{1,0:T(8,128)(2,1)S(1)} %collective-permute-done.4.other_ref), custom_call_target="tpu_custom_call" | custom-call | tf_op jit(solution)/shard_map/analysis/pallas_call | solution.py:514
Async XLA Ops:
  1.0 9.3 %collective-permute-start = (bf16[48,128]{1,0:T(8,128)(2,1)S(1)}, bf16[48,128]{1,0:T(8,128)(2,1)S(1)}, u32[]{:S(2)}, u32[]{:S(2)}) collective-permute-start(bf16[48,128]{1,0:T(8,128)(2,1)S(1)} %get-tuple-element.22), channel_id=1, source_target_pairs={{0,4},{4,8},{8,12},{1,5},{5,9},{9,13},{2,6},{6,10},{10,14},{3,7},{... | collective-permute-start | bytes 36872 | tf_op jit(solution)/shard_map/ppermute | solution.py:586
  6.0 5.6 %collective-permute-start.1 = (bf16[48,128]{1,0:T(8,128)(2,1)S(1)}, bf16[48,128]{1,0:T(8,128)(2,1)S(1)}, u32[]{:S(2)}, u32[]{:S(2)}) collective-permute-start(bf16[48,128]{1,0:T(8,128)(2,1)S(1)} %get-tuple-element.23), channel_id=1, source_target_pairs={{4,0},{8,4},{12,8},{5,1},{9,5},{13,9},{6,2},{10,6},{14,10},{7,3},{... | collective-permute-start | bytes 36872 | tf_op jit(solution)/shard_map/ppermute | solution.py:587
  11.6 1.5 %collective-permute-start.3 = (bf16[48,128]{1,0:T(8,128)(2,1)S(1)}, bf16[48,128]{1,0:T(8,128)(2,1)S(1)}, u32[]{:S(2)}, u32[]{:S(2)}) collective-permute-start(bf16[48,128]{1,0:T(8,128)(2,1)S(1)} %get-tuple-element.25.refs_5_), channel_id=1, source_target_pairs={{1,0},{2,1},{3,2},{0,3},{5,4},{6,5},{7,6},{4,7},{9,8},{10,9},{11,1... | collective-permute-start | bytes 36872 | tf_op jit(solution)/shard_map/ppermute | solution.py:601
  11.7 3.3 %collective-permute-start.2 = (bf16[48,128]{1,0:T(8,128)(2,1)S(1)}, bf16[48,128]{1,0:T(8,128)(2,1)S(1)}, u32[]{:S(2)}, u32[]{:S(2)}) collective-permute-start(bf16[48,128]{1,0:T(8,128)(2,1)S(1)} %get-tuple-element.26.refs_6_), channel_id=1, source_target_pairs={{0,1},{1,2},{2,3},{3,0},{4,5},{5,6},{6,7},{7,4},{8,9},{9,10},{10,1... | collective-permute-start | bytes 36872 | tf_op jit(solution)/shard_map/ppermute | solution.py:600
  21.5 13.3 %collective-permute-start.4 = (bf16[1536,128]{1,0:T(8,128)(2,1)S(1)}, bf16[1536,128]{1,0:T(8,128)(2,1)S(1)}, u32[]{:S(2)}, u32[]{:S(2)}) collective-permute-start(bf16[1536,128]{1,0:T(8,128)(2,1)S(1)} %get-tuple-element.32.mine_ref), channel_id=1, source_target_pairs={{0,16},{16,0},{1,17},{17,1},{2,18},{18,2},{3,19},{19,3},{4,20},{20... | collective-permute-start | bytes 1179656 | tf_op jit(solution)/shard_map/ppermute | solution.py:620

commit v7 on v6

--- a/solution.py
+++ b/solution.py
@@ -445,7 +445,7 @@
 
     current = [[entry / scale for entry in line] for line in system]
     inverse = eye
-    for turn in range(NS_ITERS):
+    for _ in range(NS_ITERS):
         both = times(inverse, current)
         factor = [[1.5 * eye[k][m] - 0.5 * both[k][m] for m in range(count)] for k in range(count)]
         current = times(current, factor)
@@ -481,7 +481,7 @@
         return jnp.broadcast_to(jnp.sum(term, keepdims=True), tile)
 
     scaled = [part * weight for part in spread_of]
-    gram = [[None] * count for k in range(count)]
+    gram = [[None] * count for _ in range(count)]
     for k in range(count):
         for m in range(k, count):
             gram[k][m] = gram[m][k] = total(scaled[k] * spread_of[m])
@@ -533,7 +533,7 @@
     scale = jnp.sqrt(jnp.sum(system * system))
     current = system / scale
     inverse = eye
-    for turn in range(NS_ITERS):
+    for _ in range(NS_ITERS):
         factor = 1.5 * eye - 0.5 * jnp.dot(inverse, current, precision=lax.Precision.HIGHEST)
         current = jnp.dot(current, factor, precision=lax.Precision.HIGHEST)
         inverse = jnp.dot(factor, inverse, precision=lax.Precision.HIGHEST)
@@ -575,7 +575,7 @@
     obs_weight,
 ):
     x = sample_quantities[0]
-    nvar, rows, cols = x.shape
+    _, rows, cols = x.shape
     n_ens, n_lat, n_lon = (lax.axis_size(axis) for axis in ("ens", "lat", "lon"))
     down_lat = [(i, i + 1) for i in range(n_lat - 1)]
     up_lat = [(j, i) for i, j in down_lat]

time: 36.3 us -> 36.3 us (level)
  no operation moved by 1% of the time
where the time goes in v7:
time: 36.3 us; the launch traced here: 36.1 us
  blocking collectives  11.7 us (32%)
  Pallas kernels  11.3 us (31%)
  starting transfers between devices  8.39 us (23%)
  waiting for transfers between devices  4.02 us (11%)
  between operations  0.71 us (2%)
    all_to_all x1, blocking collectives, per_device(): told = lax.all_to_all(notes, ('ens', 'lat', 'lon'), 0, 0, tiled=True)  11.7 us
    pallas_call x1, Pallas kernels, run_forecast(): pl.pallas_call(functools.partial(forecast_kernel, len(spot)), out_shape=(...  6.51 us
    ppermute x1, starting transfers between devices, per_device(): north = lax.ppermute(last_rows, 'lat', down_lat)  4.96 us
    pallas_call x1, Pallas kernels, spread(): pl.pallas_call(spread_kernel, out_shape=(shape((rows * block, cols), BF16...  2.39 us
    ppermute x1, waiting for transfers between devices, per_device(): from_left = lax.ppermute(own_right, 'lon', right_lon)  1.89 us
    ppermute x1, starting transfers between devices, per_device(): other = lax.ppermute(forecast, 'ens', [(0, 1), (1, 0)])  1.59 us
    pallas_call x1, Pallas kernels, run_analysis(): pl.pallas_call(analysis_kernel, out_shape=jax.ShapeDtypeStruct(shape, BF1...  1.3 us
    ppermute x1, starting transfers between devices, per_device(): south = lax.ppermute(first_rows, 'lat', up_lat)  1.29 us
  transfers between devices with their start and end apart: 5, of which 3 were waited for; matrix products, arithmetic and copies ran while one was open for 0% of the time, Pallas kernels for 7%

profile of v7, /device:TPU:0, one launch (start us, length us, event | category | flops | bytes accessed | tf_op | source)
XLA Modules:
  0.0 36.1 jit_solution(6142653716261407352)
XLA Ops:
  0.0 1.0 %edge_rows.1 = (bf16[48,128]{1,0:T(8,128)(2,1)S(1)}, bf16[48,128]{1,0:T(8,128)(2,1)S(1)}) custom-call(bf16[24,64,128]{2,1,0:T(8,128)(2,1)} %bitcast.7), custom_call_target="tpu_custom_call" | custom-call | tf_op jit(solution)/shard_map/edge_rows/pallas_call | solution.py:45
  1.0 5.0 %collective-permute-start = (bf16[48,128]{1,0:T(8,128)(2,1)S(1)}, bf16[48,128]{1,0:T(8,128)(2,1)S(1)}, u32[]{:S(2)}, u32[]{:S(2)}) collective-permute-start(bf16[48,128]{1,0:T(8,128)(2,1)S(1)} %get-tuple-element.22), channel_id=1, source_target_pairs={{0,4},{4,8},{8,12},{1,5},{5,9},{9,13},{2,6},{6,10},{10,14},{3,7},{... | collective-permute-start | bytes 36872 | tf_op jit(solution)/shard_map/ppermute | solution.py:586
  6.0 1.3 %collective-permute-start.1 = (bf16[48,128]{1,0:T(8,128)(2,1)S(1)}, bf16[48,128]{1,0:T(8,128)(2,1)S(1)}, u32[]{:S(2)}, u32[]{:S(2)}) collective-permute-start(bf16[48,128]{1,0:T(8,128)(2,1)S(1)} %get-tuple-element.23), channel_id=1, source_target_pairs={{4,0},{8,4},{12,8},{5,1},{9,5},{13,9},{6,2},{10,6},{14,10},{7,3},{... | collective-permute-start | bytes 36872 | tf_op jit(solution)/shard_map/ppermute | solution.py:587
  7.9 2.4 %spread.1 = (bf16[5120,128]{1,0:T(8,128)(2,1)S(1)}, f32[96,128]{1,0:T(8,128)S(1)}, bf16[256,240]{1,0:T(8,128)(2,1)S(1)}, bf16[24,256]{1,0:T(8,128)(2,1)S(1)}, f3...) custom-call(bf16[24,64,128]{2,1,0:T(8,128)(2,1)} %bitcast.8, ...), custom_call_target="tpu_custom_call" | custom-call | flops 100000000 | bytes 4000000 | tf_op jit(solution)/shard_map/spread/pallas_call | solution.py:183
  10.3 0.0 collective-permute-done.north_ref.refs_3_
  10.3 1.2 %collective-permute-done.1.south_ref.refs_4_ = bf16[48,128]{1,0:T(8,128)(2,1)S(1)} collective-permute-done((bf16[48,128]{1,0:T(8,128)(2,1)S(1)}, bf16[48,128]{1,0:T(8,128)(2,1)S(1)}, u32[]{:S(2)}, u32[]{:S(2)}) %collective-permute-start.1) | collective-permute-done | bytes 12320 | tf_op jit(solution)/shard_map/ppermute | solution.py:587
  11.5 0.1 edge_columns.1
  11.6 0.1 collective-permute-start.3
  11.7 0.5 %collective-permute-start.2 = (bf16[48,128]{1,0:T(8,128)(2,1)S(1)}, bf16[48,128]{1,0:T(8,128)(2,1)S(1)}, u32[]{:S(2)}, u32[]{:S(2)}) collective-permute-start(bf16[48,128]{1,0:T(8,128)(2,1)S(1)} %get-tuple-element.26.refs_6_), channel_id=1, source_target_pairs={{0,1},{1,2},{2,3},{3,0},{4,5},{5,6},{6,7},{7,4},{8,9},{9,10},{10,1... | collective-permute-start | bytes 36872 | tf_op jit(solution)/shard_map/ppermute | solution.py:600
  12.2 0.9 %collective-permute-done.3.refs_8_ = bf16[48,128]{1,0:T(8,128)(2,1)S(1)} collective-permute-done((bf16[48,128]{1,0:T(8,128)(2,1)S(1)}, bf16[48,128]{1,0:T(8,128)(2,1)S(1)}, u32[]{:S(2)}, u32[]{:S(2)}) %collective-permute-start.3) | collective-permute-done | bytes 12320 | tf_op jit(solution)/shard_map/ppermute | solution.py:601
  13.1 1.9 %collective-permute-done.2.refs_7_ = bf16[48,128]{1,0:T(8,128)(2,1)S(1)} collective-permute-done((bf16[48,128]{1,0:T(8,128)(2,1)S(1)}, bf16[48,128]{1,0:T(8,128)(2,1)S(1)}, u32[]{:S(2)}, u32[]{:S(2)}) %collective-permute-start.2) | collective-permute-done | bytes 12320 | tf_op jit(solution)/shard_map/ppermute | solution.py:600
  15.0 6.5 %forecast.1 = (bf16[1536,128]{1,0:T(8,128)(2,1)S(1)}, bf16[32,4,128]{2,1,0:T(4,128)(2,1)S(1)}) custom-call(s32[1,128]{1,0:T(1,128)S(1)} %get-tuple-element.19.refs_0_, s32[1,128]{1,0:T(1,128)S(1)} %get-tuple-element.20.refs_1_, bf16[5120,128]{1,0:T(8,128)(2,1)S(1)} %get-tuple-element.21.refs_2_, bf16[48,128]{1,0:T(8,128)(2,1)S(1)} %collective-permute-done.north_ref.refs_3_, ...), custom_call_target="tpu_custom_call" | custom-call | tf_op jit(solution)/shard_map/forecast/pallas_call | solution.py:411
  21.5 1.6 %collective-permute-start.4 = (bf16[1536,128]{1,0:T(8,128)(2,1)S(1)}, bf16[1536,128]{1,0:T(8,128)(2,1)S(1)}, u32[]{:S(2)}, u32[]{:S(2)}) collective-permute-start(bf16[1536,128]{1,0:T(8,128)(2,1)S(1)} %get-tuple-element.32.mine_ref), channel_id=1, source_target_pairs={{0,16},{16,0},{1,17},{17,1},{2,18},{18,2},{3,19},{19,3},{4,20},{20... | collective-permute-start | bytes 1179656 | tf_op jit(solution)/shard_map/ppermute | solution.py:620
  23.1 11.7 %all_to_all.5.told_ref = bf16[32,4,128]{2,1,0:T(4,128)(2,1)S(1)} all-to-all(bf16[32,4,128]{2,1,0:T(4,128)(2,1)S(1)} %get-tuple-element.31), channel_id=1, replica_groups=mesh['ens'=2,'lat'=4,'lon'=4] {'ens','lat','lon'}, dimensions={0} | all-to-all | bytes 65536 | tf_op jit(solution)/shard_map/all_to_all | solution.py:618
  34.8 0.0 collective-permute-done.4.other_ref
  34.8 1.3 %analysis.1 = bf16[24,64,128]{2,1,0:T(8,128)(2,1)} custom-call(bf16[32,4,128]{2,1,0:T(4,128)(2,1)S(1)} %all_to_all.5.told_ref, bf16[1536,128]{1,0:T(8,128)(2,1)S(1)} %get-tuple-element.32.mine_ref, bf16[1536,128]{1,0:T(8,128)(2,1)S(1)} %collective-permute-done.4.other_ref), custom_call_target="tpu_custom_call" | custom-call | tf_op jit(solution)/shard_map/analysis/pallas_call | solution.py:514
Async XLA Ops:
  1.0 9.3 %collective-permute-start = (bf16[48,128]{1,0:T(8,128)(2,1)S(1)}, bf16[48,128]{1,0:T(8,128)(2,1)S(1)}, u32[]{:S(2)}, u32[]{:S(2)}) collective-permute-start(bf16[48,128]{1,0:T(8,128)(2,1)S(1)} %get-tuple-element.22), channel_id=1, source_target_pairs={{0,4},{4,8},{8,12},{1,5},{5,9},{9,13},{2,6},{6,10},{10,14},{3,7},{... | collective-permute-start | bytes 36872 | tf_op jit(solution)/shard_map/ppermute | solution.py:586
  6.0 5.6 %collective-permute-start.1 = (bf16[48,128]{1,0:T(8,128)(2,1)S(1)}, bf16[48,128]{1,0:T(8,128)(2,1)S(1)}, u32[]{:S(2)}, u32[]{:S(2)}) collective-permute-start(bf16[48,128]{1,0:T(8,128)(2,1)S(1)} %get-tuple-element.23), channel_id=1, source_target_pairs={{4,0},{8,4},{12,8},{5,1},{9,5},{13,9},{6,2},{10,6},{14,10},{7,3},{... | collective-permute-start | bytes 36872 | tf_op jit(solution)/shard_map/ppermute | solution.py:587
  11.6 1.5 %collective-permute-start.3 = (bf16[48,128]{1,0:T(8,128)(2,1)S(1)}, bf16[48,128]{1,0:T(8,128)(2,1)S(1)}, u32[]{:S(2)}, u32[]{:S(2)}) collective-permute-start(bf16[48,128]{1,0:T(8,128)(2,1)S(1)} %get-tuple-element.25.refs_5_), channel_id=1, source_target_pairs={{1,0},{2,1},{3,2},{0,3},{5,4},{6,5},{7,6},{4,7},{9,8},{10,9},{11,1... | collective-permute-start | bytes 36872 | tf_op jit(solution)/shard_map/ppermute | solution.py:601
  11.7 3.3 %collective-permute-start.2 = (bf16[48,128]{1,0:T(8,128)(2,1)S(1)}, bf16[48,128]{1,0:T(8,128)(2,1)S(1)}, u32[]{:S(2)}, u32[]{:S(2)}) collective-permute-start(bf16[48,128]{1,0:T(8,128)(2,1)S(1)} %get-tuple-element.26.refs_6_), channel_id=1, source_target_pairs={{0,1},{1,2},{2,3},{3,0},{4,5},{5,6},{6,7},{7,4},{8,9},{9,10},{10,1... | collective-permute-start | bytes 36872 | tf_op jit(solution)/shard_map/ppermute | solution.py:600
  21.5 13.3 %collective-permute-start.4 = (bf16[1536,128]{1,0:T(8,128)(2,1)S(1)}, bf16[1536,128]{1,0:T(8,128)(2,1)S(1)}, u32[]{:S(2)}, u32[]{:S(2)}) collective-permute-start(bf16[1536,128]{1,0:T(8,128)(2,1)S(1)} %get-tuple-element.32.mine_ref), channel_id=1, source_target_pairs={{0,16},{16,0},{1,17},{17,1},{2,18},{18,2},{3,19},{19,3},{4,20},{20... | collective-permute-start | bytes 1179656 | tf_op jit(solution)/shard_map/ppermute | solution.py:620

commit v8 on v7

--- a/solution.py
+++ b/solution.py
@@ -208,7 +208,7 @@
     nvar, cols = own.shape[0] // 4, own.shape[1]
     wanted = (0, 1, cols - 2, cols - 1)
 
-    def kernel(own_ref, north_ref, south_ref, left_ref, right_ref):
+    def kernel(own_ref, north_ref, south_ref, left_ref, right_ref, between_ref, within_ref):
         lane = lanes_of((nvar, cols))
         halo = []
         for ref, first in ((north_ref, 0), (south_ref, rows + 2)):
@@ -221,13 +221,17 @@
             for at, row in halo:
                 column = jnp.where(lane == at, pltpu.roll(row, (at - c) % cols, 1), column)
             outs.append(column)
-        left_ref[...] = jnp.concatenate(outs[:2], axis=0).astype(BF16)
-        right_ref[...] = jnp.concatenate(outs[2:], axis=0).astype(BF16)
+        left, right = jnp.concatenate(outs[:2], axis=0), jnp.concatenate(outs[2:], axis=0)
+        even = lax.axis_index("lon") % 2 == 0
+        left_ref[...] = left.astype(BF16)
+        right_ref[...] = right.astype(BF16)
+        between_ref[...] = jnp.where(even, left, right).astype(BF16)
+        within_ref[...] = jnp.where(even, right, left).astype(BF16)
 
     out = jax.ShapeDtypeStruct((2 * nvar, cols), BF16)
     return pl.pallas_call(
         kernel,
-        out_shape=(out, out),
+        out_shape=(out,) * 4,
         compiler_params=pltpu.CompilerParams(vmem_limit_bytes=SMALL),
         name="edge_columns",
     )(own, north, south)
@@ -250,8 +254,8 @@
     south_ref,
     own_left_ref,
     own_right_ref,
-    from_left_ref,
-    from_right_ref,
+    between_ref,
+    within_ref,
     conv_ref,
     out_w_ref,
     chosen_ref,
@@ -289,8 +293,11 @@
 
     conv[...] = conv_ref[...]
     out_w[...] = out_w_ref[...]
-    from_left = from_left_ref[...].astype(F32)
-    from_right = from_right_ref[...].astype(F32)
+    even = lax.axis_index("lon") % 2 == 0
+    between = between_ref[...].astype(F32)
+    within = within_ref[...].astype(F32)
+    from_left = jnp.where(even, between, within)
+    from_right = jnp.where(even, within, between)
     own_left = own_left_ref[...].astype(F32)
     own_right = own_right_ref[...].astype(F32)
     far_west, west = from_left[:nvar], from_left[nvar:]
@@ -401,7 +408,7 @@
         notes_ref[d] = note
 
 
-def run_forecast(spot, taps, north, south, own_left, own_right, from_left, from_right, conv, out_w, chosen, extra, devices):
+def run_forecast(spot, taps, north, south, own_left, own_right, between, within, conv, out_w, chosen, extra, devices):
     nvar, cols = north.shape[0] // 2, north.shape[1]
     slots = len(spot) * cols
     block = 3 * nvar + PAD
@@ -427,7 +434,7 @@
         ],
         compiler_params=pltpu.CompilerParams(vmem_limit_bytes=24 << 20),
         name="forecast",
-    )(*spot, taps, north, south, own_left, own_right, from_left, from_right, conv, out_w, chosen, extra)
+    )(*spot, taps, north, south, own_left, own_right, between, within, conv, out_w, chosen, extra)
 
 
 def pair_weights(gram, proj):
@@ -579,8 +586,9 @@
     n_ens, n_lat, n_lon = (lax.axis_size(axis) for axis in ("ens", "lat", "lon"))
     down_lat = [(i, i + 1) for i in range(n_lat - 1)]
     up_lat = [(j, i) for i, j in down_lat]
-    right_lon = [(i, (i + 1) % n_lon) for i in range(n_lon)]
-    left_lon = [(j, i) for i, j in right_lon]
+    assert n_lon % 2 == 0
+    odd_pairs = [(i, (i + 1) % n_lon) for i in range(1, n_lon, 2)]
+    even_pairs = [(i, i + 1) for i in range(0, n_lon, 2)]
 
     first_rows, last_rows = edge_rows(x)
     north = lax.ppermute(last_rows, "lat", down_lat)
@@ -596,10 +604,9 @@
         obs_value.reshape(fold),
         obs_weight.reshape(fold),
     )
-    own_left, own_right = edge_columns(own, north, south, rows)
-    from_left = lax.ppermute(own_right, "lon", right_lon)
-    from_right = lax.ppermute(own_left, "lon", left_lon)
-
+    own_left, own_right, outer, inner = edge_columns(own, north, south, rows)
+    between = lax.ppermute(outer, "lon", odd_pairs + [(j, i) for i, j in odd_pairs])
+    within = lax.ppermute(inner, "lon", even_pairs + [(j, i) for i, j in even_pairs])
     forecast, notes = run_forecast(
         spot,
         taps,
@@ -607,8 +614,8 @@
         south,
         own_left,
         own_right,
-        from_left,
-        from_right,
+        between,
+        within,
         conv,
         out_w,
         chosen,

time: 36.3 us -> 36.3 us (level)
  waiting for transfers between devices: 4.02 us -> 2.83 us
  starting transfers between devices: 8.39 us -> 9.5 us
    ppermute x2, waiting for transfers between devices: 2.79 us -> 1.6 us  [the longest x1 1.6 us: per_device(): lax.ppermute(outer, 'lon', odd_pairs + [(j, i) for i, j in odd_pairs])]
    ppermute x2, starting transfers between devices: 0.55 us -> 1.66 us  [the longest x1 1.59 us: per_device(): lax.ppermute(inner, 'lon', even_pairs + [(j, i) for i, j in even_pairs])]
  transfers between devices with their start and end apart: 5 -> 5, of which waited for: 3 -> 2; matrix products, arithmetic and copies ran while one was open for 0% -> 0% of each run, Pallas kernels for 7% -> 7%
where the time goes in v8:
time: 36.3 us; the launch traced here: 36 us
  blocking collectives  11.7 us (32%)
  Pallas kernels  11.3 us (31%)
  starting transfers between devices  9.5 us (26%)
  waiting for transfers between devices  2.83 us (8%)
  between operations  0.71 us (2%)
    all_to_all x1, blocking collectives, per_device(): told = lax.all_to_all(notes, ('ens', 'lat', 'lon'), 0, 0, tiled=True)  11.7 us
    pallas_call x1, Pallas kernels, run_forecast(): pl.pallas_call(functools.partial(forecast_kernel, len(spot)), out_shape=(...  6.52 us
    ppermute x1, starting transfers between devices, per_device(): north = lax.ppermute(last_rows, 'lat', down_lat)  4.96 us
    pallas_call x1, Pallas kernels, spread(): pl.pallas_call(spread_kernel, out_shape=(shape((rows * block, cols), BF16...  2.39 us
    ppermute x1, waiting for transfers between devices, per_device(): lax.ppermute(outer, 'lon', odd_pairs + [(j, i) for i, j in odd_pairs])  1.6 us
    ppermute x1, starting transfers between devices, per_device(): lax.ppermute(inner, 'lon', even_pairs + [(j, i) for i, j in even_pairs])  1.59 us
    ppermute x1, starting transfers between devices, per_device(): other = lax.ppermute(forecast, 'ens', [(0, 1), (1, 0)])  1.58 us
    pallas_call x1, Pallas kernels, run_analysis(): pl.pallas_call(analysis_kernel, out_shape=jax.ShapeDtypeStruct(shape, BF1...  1.3 us
  transfers between devices with their start and end apart: 5, of which 2 were waited for; matrix products, arithmetic and copies ran while one was open for 0% of the time, Pallas kernels for 7%

profile of v8, /device:TPU:0, one launch (start us, length us, event | category | flops | bytes accessed | tf_op | source)
XLA Modules:
  0.0 36.0 jit_solution(16157262616767477026)
XLA Ops:
  0.0 1.0 %edge_rows.1 = (bf16[48,128]{1,0:T(8,128)(2,1)S(1)}, bf16[48,128]{1,0:T(8,128)(2,1)S(1)}) custom-call(bf16[24,64,128]{2,1,0:T(8,128)(2,1)} %bitcast.7), custom_call_target="tpu_custom_call" | custom-call | tf_op jit(solution)/shard_map/edge_rows/pallas_call | solution.py:45
  1.0 5.0 %collective-permute-start = (bf16[48,128]{1,0:T(8,128)(2,1)S(1)}, bf16[48,128]{1,0:T(8,128)(2,1)S(1)}, u32[]{:S(2)}, u32[]{:S(2)}) collective-permute-start(bf16[48,128]{1,0:T(8,128)(2,1)S(1)} %get-tuple-element.24), channel_id=1, source_target_pairs={{0,4},{4,8},{8,12},{1,5},{5,9},{9,13},{2,6},{6,10},{10,14},{3,7},{... | collective-permute-start | bytes 36872 | tf_op jit(solution)/shard_map/ppermute | solution.py:594
  6.0 1.3 %collective-permute-start.1 = (bf16[48,128]{1,0:T(8,128)(2,1)S(1)}, bf16[48,128]{1,0:T(8,128)(2,1)S(1)}, u32[]{:S(2)}, u32[]{:S(2)}) collective-permute-start(bf16[48,128]{1,0:T(8,128)(2,1)S(1)} %get-tuple-element.25), channel_id=1, source_target_pairs={{4,0},{8,4},{12,8},{5,1},{9,5},{13,9},{6,2},{10,6},{14,10},{7,3},{... | collective-permute-start | bytes 36872 | tf_op jit(solution)/shard_map/ppermute | solution.py:595
  7.9 2.4 %spread.1 = (bf16[5120,128]{1,0:T(8,128)(2,1)S(1)}, f32[96,128]{1,0:T(8,128)S(1)}, bf16[256,240]{1,0:T(8,128)(2,1)S(1)}, bf16[24,256]{1,0:T(8,128)(2,1)S(1)}, f3...) custom-call(bf16[24,64,128]{2,1,0:T(8,128)(2,1)} %bitcast.8, ...), custom_call_target="tpu_custom_call" | custom-call | flops 100000000 | bytes 4000000 | tf_op jit(solution)/shard_map/spread/pallas_call | solution.py:183
  10.3 0.0 collective-permute-done.north_ref.refs_3_
  10.3 1.2 %collective-permute-done.1.south_ref.refs_4_ = bf16[48,128]{1,0:T(8,128)(2,1)S(1)} collective-permute-done((bf16[48,128]{1,0:T(8,128)(2,1)S(1)}, bf16[48,128]{1,0:T(8,128)(2,1)S(1)}, u32[]{:S(2)}, u32[]{:S(2)}) %collective-permute-start.1) | collective-permute-done | bytes 12320 | tf_op jit(solution)/shard_map/ppermute | solution.py:595
  11.5 0.1 edge_columns.1
  11.6 0.1 collective-permute-start.2
  11.7 1.6 %collective-permute-start.3 = (bf16[48,128]{1,0:T(8,128)(2,1)S(1)}, bf16[48,128]{1,0:T(8,128)(2,1)S(1)}, u32[]{:S(2)}, u32[]{:S(2)}) collective-permute-start(bf16[48,128]{1,0:T(8,128)(2,1)S(1)} %get-tuple-element.30), channel_id=1, source_target_pairs={{0,1},{2,3},{1,0},{3,2},{4,5},{6,7},{5,4},{7,6},{8,9},{10,11},{9,8... | collective-permute-start | bytes 36872 | tf_op jit(solution)/shard_map/ppermute | solution.py:609
  13.3 1.6 %collective-permute-done.2.refs_7_ = bf16[48,128]{1,0:T(8,128)(2,1)S(1)} collective-permute-done((bf16[48,128]{1,0:T(8,128)(2,1)S(1)}, bf16[48,128]{1,0:T(8,128)(2,1)S(1)}, u32[]{:S(2)}, u32[]{:S(2)}) %collective-permute-start.2) | collective-permute-done | bytes 12320 | tf_op jit(solution)/shard_map/ppermute | solution.py:608
  14.9 0.0 collective-permute-done.3.refs_8_
  14.9 6.5 %forecast.1 = (bf16[1536,128]{1,0:T(8,128)(2,1)S(1)}, bf16[32,4,128]{2,1,0:T(4,128)(2,1)S(1)}) custom-call(s32[1,128]{1,0:T(1,128)S(1)} %get-tuple-element.21.refs_0_, s32[1,128]{1,0:T(1,128)S(1)} %get-tuple-element.22.refs_1_, bf16[5120,128]{1,0:T(8,128)(2,1)S(1)} %get-tuple-element.23.refs_2_, bf16[48,128]{1,0:T(8,128)(2,1)S(1)} %collective-permute-done.north_ref.refs_3_, ...), custom_call_target="tpu_custom_call" | custom-call | tf_op jit(solution)/shard_map/forecast/pallas_call | solution.py:418
  21.5 1.6 %collective-permute-start.4 = (bf16[1536,128]{1,0:T(8,128)(2,1)S(1)}, bf16[1536,128]{1,0:T(8,128)(2,1)S(1)}, u32[]{:S(2)}, u32[]{:S(2)}) collective-permute-start(bf16[1536,128]{1,0:T(8,128)(2,1)S(1)} %get-tuple-element.36.mine_ref), channel_id=1, source_target_pairs={{0,16},{16,0},{1,17},{17,1},{2,18},{18,2},{3,19},{19,3},{4,20},{20... | collective-permute-start | bytes 1179656 | tf_op jit(solution)/shard_map/ppermute | solution.py:627
  23.0 11.7 %all_to_all.5.told_ref = bf16[32,4,128]{2,1,0:T(4,128)(2,1)S(1)} all-to-all(bf16[32,4,128]{2,1,0:T(4,128)(2,1)S(1)} %get-tuple-element.35), channel_id=1, replica_groups=mesh['ens'=2,'lat'=4,'lon'=4] {'ens','lat','lon'}, dimensions={0} | all-to-all | bytes 65536 | tf_op jit(solution)/shard_map/all_to_all | solution.py:625
  34.7 0.0 collective-permute-done.4.other_ref
  34.7 1.3 %analysis.1 = bf16[24,64,128]{2,1,0:T(8,128)(2,1)} custom-call(bf16[32,4,128]{2,1,0:T(4,128)(2,1)S(1)} %all_to_all.5.told_ref, bf16[1536,128]{1,0:T(8,128)(2,1)S(1)} %get-tuple-element.36.mine_ref, bf16[1536,128]{1,0:T(8,128)(2,1)S(1)} %collective-permute-done.4.other_ref), custom_call_target="tpu_custom_call" | custom-call | tf_op jit(solution)/shard_map/analysis/pallas_call | solution.py:521
Async XLA Ops:
  1.0 9.3 %collective-permute-start = (bf16[48,128]{1,0:T(8,128)(2,1)S(1)}, bf16[48,128]{1,0:T(8,128)(2,1)S(1)}, u32[]{:S(2)}, u32[]{:S(2)}) collective-permute-start(bf16[48,128]{1,0:T(8,128)(2,1)S(1)} %get-tuple-element.24), channel_id=1, source_target_pairs={{0,4},{4,8},{8,12},{1,5},{5,9},{9,13},{2,6},{6,10},{10,14},{3,7},{... | collective-permute-start | bytes 36872 | tf_op jit(solution)/shard_map/ppermute | solution.py:594
  6.0 5.6 %collective-permute-start.1 = (bf16[48,128]{1,0:T(8,128)(2,1)S(1)}, bf16[48,128]{1,0:T(8,128)(2,1)S(1)}, u32[]{:S(2)}, u32[]{:S(2)}) collective-permute-start(bf16[48,128]{1,0:T(8,128)(2,1)S(1)} %get-tuple-element.25), channel_id=1, source_target_pairs={{4,0},{8,4},{12,8},{5,1},{9,5},{13,9},{6,2},{10,6},{14,10},{7,3},{... | collective-permute-start | bytes 36872 | tf_op jit(solution)/shard_map/ppermute | solution.py:595
  11.6 3.3 %collective-permute-start.2 = (bf16[48,128]{1,0:T(8,128)(2,1)S(1)}, bf16[48,128]{1,0:T(8,128)(2,1)S(1)}, u32[]{:S(2)}, u32[]{:S(2)}) collective-permute-start(bf16[48,128]{1,0:T(8,128)(2,1)S(1)} %get-tuple-element.29), channel_id=1, source_target_pairs={{1,2},{3,0},{2,1},{0,3},{5,6},{7,4},{6,5},{4,7},{9,10},{11,8},{10,... | collective-permute-start | bytes 36872 | tf_op jit(solution)/shard_map/ppermute | solution.py:608
  11.7 3.2 %collective-permute-start.3 = (bf16[48,128]{1,0:T(8,128)(2,1)S(1)}, bf16[48,128]{1,0:T(8,128)(2,1)S(1)}, u32[]{:S(2)}, u32[]{:S(2)}) collective-permute-start(bf16[48,128]{1,0:T(8,128)(2,1)S(1)} %get-tuple-element.30), channel_id=1, source_target_pairs={{0,1},{2,3},{1,0},{3,2},{4,5},{6,7},{5,4},{7,6},{8,9},{10,11},{9,8... | collective-permute-start | bytes 36872 | tf_op jit(solution)/shard_map/ppermute | solution.py:609
  21.5 13.3 %collective-permute-start.4 = (bf16[1536,128]{1,0:T(8,128)(2,1)S(1)}, bf16[1536,128]{1,0:T(8,128)(2,1)S(1)}, u32[]{:S(2)}, u32[]{:S(2)}) collective-permute-start(bf16[1536,128]{1,0:T(8,128)(2,1)S(1)} %get-tuple-element.36.mine_ref), channel_id=1, source_target_pairs={{0,16},{16,0},{1,17},{17,1},{2,18},{18,2},{3,19},{19,3},{4,20},{20... | collective-permute-start | bytes 1179656 | tf_op jit(solution)/shard_map/ppermute | solution.py:627

commit v9 on v8

--- a/solution.py
+++ b/solution.py
@@ -30,16 +30,20 @@
     nvar, rows, cols = x.shape
     tile = 16
 
-    def kernel(x_ref, up_ref, down_ref, part, stage, sems):
+    def kernel(x_ref, near_ref, far_ref, part, stage, sems):
         copies = []
         for i, first in enumerate((0, rows - tile)):
             copies.append(pltpu.make_async_copy(x_ref.at[:, first : first + tile, :], part.at[i], sems.at[i]))
             copies[i].start()
-        for i, (out, first) in enumerate(((up_ref, 0), (down_ref, tile - 2))):
+        ends = []
+        for i, first in enumerate((0, tile - 2)):
             copies[i].wait()
             stage[...] = part[i].reshape(nvar * tile, cols).astype(F32)
             both = [stage[pl.ds(first + j, nvar, stride=tile), :] for j in range(2)]
-            out[...] = jnp.concatenate(both, axis=0).astype(BF16)
+            ends.append(jnp.concatenate(both, axis=0))
+        even = lax.axis_index("lat") % 2 == 0
+        near_ref[...] = jnp.where(even, ends[1], ends[0]).astype(BF16)
+        far_ref[...] = jnp.where(even, ends[0], ends[1]).astype(BF16)
 
     out = jax.ShapeDtypeStruct((2 * nvar, cols), BF16)
     return pl.pallas_call(
@@ -204,16 +208,22 @@
     )(*placed)
 
 
-def edge_columns(own, north, south, rows):
+def bands(near_ref, far_ref):
+    even = lax.axis_index("lat") % 2 == 0
+    near, far = near_ref[...].astype(F32), far_ref[...].astype(F32)
+    return jnp.where(even, far, near), jnp.where(even, near, far)
+
+
+def edge_columns(own, near, far, rows):
     nvar, cols = own.shape[0] // 4, own.shape[1]
     wanted = (0, 1, cols - 2, cols - 1)
 
-    def kernel(own_ref, north_ref, south_ref, left_ref, right_ref, between_ref, within_ref):
+    def kernel(own_ref, near_ref, far_ref, left_ref, right_ref, between_ref, within_ref):
         lane = lanes_of((nvar, cols))
         halo = []
-        for ref, first in ((north_ref, 0), (south_ref, rows + 2)):
+        for band, first in zip(bands(near_ref, far_ref), (0, rows + 2)):
             for i in range(2):
-                halo.append((first + i, ref[i * nvar : (i + 1) * nvar, :].astype(F32)))
+                halo.append((first + i, band[i * nvar : (i + 1) * nvar, :]))
         outs = []
         for i, c in enumerate(wanted):
             column = own_ref[i * nvar : (i + 1) * nvar, :]
@@ -234,7 +244,7 @@
         out_shape=(out,) * 4,
         compiler_params=pltpu.CompilerParams(vmem_limit_bytes=SMALL),
         name="edge_columns",
-    )(own, north, south)
+    )(own, near, far)
 
 
 def gelu2(pre):
@@ -250,8 +260,8 @@
     spot_refs = refs[:fold]
     (
     taps_ref,
-    north_ref,
-    south_ref,
+    near_ref,
+    far_ref,
     own_left_ref,
     own_right_ref,
     between_ref,
@@ -270,7 +280,7 @@
     conv,
     out_w,
     ) = refs[fold:]
-    nvar, cols = north_ref.shape[0] // 2, north_ref.shape[1]
+    nvar, cols = near_ref.shape[0] // 2, near_ref.shape[1]
     block = 3 * nvar + PAD
     rows = taps_ref.shape[0] // block
     deep = 3 * block
@@ -304,9 +314,9 @@
     east, far_east = from_right[:nvar], from_right[nvar:]
     inner_west, inner_east = own_left[:nvar], own_right[nvar:]
 
-    for ref, start in ((north_ref, 0), (south_ref, rows + 2)):
+    for band, start in zip(bands(near_ref, far_ref), (0, rows + 2)):
         for i in range(2):
-            row = ref[i * nvar : (i + 1) * nvar, :].astype(F32)
+            row = band[i * nvar : (i + 1) * nvar, :]
             first[(start + i) * block : (start + i + 1) * block, :] = tap_rows(row, west, east, start + i)
 
     group = lax.broadcasted_iota(jnp.int32, (block, cols), 0)
@@ -408,8 +418,8 @@
         notes_ref[d] = note
 
 
-def run_forecast(spot, taps, north, south, own_left, own_right, between, within, conv, out_w, chosen, extra, devices):
-    nvar, cols = north.shape[0] // 2, north.shape[1]
+def run_forecast(spot, taps, near, far, own_left, own_right, between, within, conv, out_w, chosen, extra, devices):
+    nvar, cols = near.shape[0] // 2, near.shape[1]
     slots = len(spot) * cols
     block = 3 * nvar + PAD
     rows = taps.shape[0] // block
@@ -434,7 +444,7 @@
         ],
         compiler_params=pltpu.CompilerParams(vmem_limit_bytes=24 << 20),
         name="forecast",
-    )(*spot, taps, north, south, own_left, own_right, between, within, conv, out_w, chosen, extra)
+    )(*spot, taps, near, far, own_left, own_right, between, within, conv, out_w, chosen, extra)
 
 
 def pair_weights(gram, proj):
@@ -584,15 +594,15 @@
     x = sample_quantities[0]
     _, rows, cols = x.shape
     n_ens, n_lat, n_lon = (lax.axis_size(axis) for axis in ("ens", "lat", "lon"))
-    down_lat = [(i, i + 1) for i in range(n_lat - 1)]
-    up_lat = [(j, i) for i, j in down_lat]
     assert n_lon % 2 == 0
+    first_bands = [(i, i + 1) for i in range(0, n_lat - 1, 2)]
+    second_bands = [(i, i + 1) for i in range(1, n_lat - 1, 2)]
     odd_pairs = [(i, (i + 1) % n_lon) for i in range(1, n_lon, 2)]
     even_pairs = [(i, i + 1) for i in range(0, n_lon, 2)]
 
-    first_rows, last_rows = edge_rows(x)
-    north = lax.ppermute(last_rows, "lat", down_lat)
-    south = lax.ppermute(first_rows, "lat", up_lat)
+    near_rows, far_rows = edge_rows(x)
+    near = lax.ppermute(near_rows, "lat", first_bands + [(j, i) for i, j in first_bands])
+    far = lax.ppermute(far_rows, "lat", second_bands + [(j, i) for i, j in second_bands])
     fold = (obs_index.size // cols, cols)
     taps, own, conv, out_w, extra, chosen, *spot = spread(
         x,
@@ -604,14 +614,14 @@
         obs_value.reshape(fold),
         obs_weight.reshape(fold),
     )
-    own_left, own_right, outer, inner = edge_columns(own, north, south, rows)
+    own_left, own_right, outer, inner = edge_columns(own, near, far, rows)
     between = lax.ppermute(outer, "lon", odd_pairs + [(j, i) for i, j in odd_pairs])
     within = lax.ppermute(inner, "lon", even_pairs + [(j, i) for i, j in even_pairs])
     forecast, notes = run_forecast(
         spot,
         taps,
-        north,
-        south,
+        near,
+        far,
         own_left,
         own_right,
         between,

time: 36.3 us -> 33.5 us (0.923)
  starting transfers between devices: 9.5 us -> 7.02 us
  waiting for transfers between devices: 2.83 us -> 1.61 us
  blocking collectives: 11.7 us -> 12.7 us
    ppermute x2, starting transfers between devices: 6.25 us -> 3.77 us  [the longest x1 3.12 us: per_device(): lax.ppermute(near_rows, 'lat', first_bands + [(j, i) for i, j in first_ba...]
    ppermute x2, waiting for transfers between devices: 1.23 us -> 0.01 us  [the longest x1 0.01 us: per_device(): lax.ppermute(near_rows, 'lat', first_bands + [(j, i) for i, j in first_ba...]
    all_to_all x1, blocking collectives: 11.7 us -> 12.7 us  [per_device(): told = lax.all_to_all(notes, ('ens', 'lat', 'lon'), 0, 0, tiled=True)]
    ppermute x1, starting transfers between devices: 0.07 us -> 0.72 us  [per_device(): lax.ppermute(outer, 'lon', odd_pairs + [(j, i) for i, j in odd_pairs])]
    ppermute x1, starting transfers between devices: 1.59 us -> 0.96 us  [per_device(): lax.ppermute(inner, 'lon', even_pairs + [(j, i) for i, j in even_pairs])]
  transfers between devices with their start and end apart: 5 -> 5, of which waited for: 2 -> 1; matrix products, arithmetic and copies ran while one was open for 0% -> 0% of each run, Pallas kernels for 7% -> 7%
where the time goes in v9:
time: 33.5 us; the launch traced here: 33.3 us
  blocking collectives  12.7 us (38%)
  Pallas kernels  11.3 us (34%)
  starting transfers between devices  7.02 us (21%)
  waiting for transfers between devices  1.61 us (5%)
  between operations  0.71 us (2%)
    all_to_all x1, blocking collectives, per_device(): told = lax.all_to_all(notes, ('ens', 'lat', 'lon'), 0, 0, tiled=True)  12.7 us
    pallas_call x1, Pallas kernels, run_forecast(): pl.pallas_call(functools.partial(forecast_kernel, len(spot)), out_shape=(...  6.53 us
    ppermute x1, starting transfers between devices, per_device(): lax.ppermute(near_rows, 'lat', first_bands + [(j, i) for i, j in first_ba...  3.12 us
    pallas_call x1, Pallas kernels, spread(): pl.pallas_call(spread_kernel, out_shape=(shape((rows * block, cols), BF16...  2.39 us
    ppermute x1, waiting for transfers between devices, per_device(): lax.ppermute(outer, 'lon', odd_pairs + [(j, i) for i, j in odd_pairs])  1.6 us
    ppermute x1, starting transfers between devices, per_device(): other = lax.ppermute(forecast, 'ens', [(0, 1), (1, 0)])  1.58 us
    pallas_call x1, Pallas kernels, run_analysis(): pl.pallas_call(analysis_kernel, out_shape=jax.ShapeDtypeStruct(shape, BF1...  1.3 us
    pallas_call x1, Pallas kernels, edge_rows(): pl.pallas_call(kernel, out_shape=(out, out), in_specs=[pl.BlockSpec(memor...  0.98 us
  transfers between devices with their start and end apart: 5, of which 1 were waited for; matrix products, arithmetic and copies ran while one was open for 0% of the time, Pallas kernels for 7%

profile of v9, /device:TPU:0, one launch (start us, length us, event | category | flops | bytes accessed | tf_op | source)
XLA Modules:
  0.0 33.3 jit_solution(18369081269151809172)
XLA Ops:
  0.0 1.0 %edge_rows.1 = (bf16[48,128]{1,0:T(8,128)(2,1)S(1)}, bf16[48,128]{1,0:T(8,128)(2,1)S(1)}) custom-call(bf16[24,64,128]{2,1,0:T(8,128)(2,1)} %bitcast.7), custom_call_target="tpu_custom_call" | custom-call | tf_op jit(solution)/shard_map/edge_rows/pallas_call | solution.py:49
  1.0 3.1 %collective-permute-start = (bf16[48,128]{1,0:T(8,128)(2,1)S(1)}, bf16[48,128]{1,0:T(8,128)(2,1)S(1)}, u32[]{:S(2)}, u32[]{:S(2)}) collective-permute-start(bf16[48,128]{1,0:T(8,128)(2,1)S(1)} %get-tuple-element.24), channel_id=1, source_target_pairs={{0,4},{8,12},{4,0},{12,8},{1,5},{9,13},{5,1},{13,9},{2,6},{10,14},... | collective-permute-start | bytes 36872 | tf_op jit(solution)/shard_map/ppermute | solution.py:604
  4.1 0.7 %collective-permute-start.1 = (bf16[48,128]{1,0:T(8,128)(2,1)S(1)}, bf16[48,128]{1,0:T(8,128)(2,1)S(1)}, u32[]{:S(2)}, u32[]{:S(2)}) collective-permute-start(bf16[48,128]{1,0:T(8,128)(2,1)S(1)} %get-tuple-element.25), channel_id=1, source_target_pairs={{4,8},{8,4},{5,9},{9,5},{6,10},{10,6},{7,11},{11,7},{20,24},{24,20... | collective-permute-start | bytes 36872 | tf_op jit(solution)/shard_map/ppermute | solution.py:605
  5.4 2.4 %spread.1 = (bf16[5120,128]{1,0:T(8,128)(2,1)S(1)}, f32[96,128]{1,0:T(8,128)S(1)}, bf16[256,240]{1,0:T(8,128)(2,1)S(1)}, bf16[24,256]{1,0:T(8,128)(2,1)S(1)}, f3...) custom-call(bf16[24,64,128]{2,1,0:T(8,128)(2,1)} %bitcast.8, ...), custom_call_target="tpu_custom_call" | custom-call | flops 100000000 | bytes 4000000 | tf_op jit(solution)/shard_map/spread/pallas_call | solution.py:187
  7.8 0.0 collective-permute-done.near_ref.refs_3_
  7.8 0.0 collective-permute-done.1.far_ref.refs_4_
  7.8 0.1 edge_columns.1
  8.0 0.7 %collective-permute-start.2 = (bf16[48,128]{1,0:T(8,128)(2,1)S(1)}, bf16[48,128]{1,0:T(8,128)(2,1)S(1)}, u32[]{:S(2)}, u32[]{:S(2)}) collective-permute-start(bf16[48,128]{1,0:T(8,128)(2,1)S(1)} %get-tuple-element.29), channel_id=1, source_target_pairs={{1,2},{3,0},{2,1},{0,3},{5,6},{7,4},{6,5},{4,7},{9,10},{11,8},{10,... | collective-permute-start | bytes 36872 | tf_op jit(solution)/shard_map/ppermute | solution.py:618
  8.7 1.0 %collective-permute-start.3 = (bf16[48,128]{1,0:T(8,128)(2,1)S(1)}, bf16[48,128]{1,0:T(8,128)(2,1)S(1)}, u32[]{:S(2)}, u32[]{:S(2)}) collective-permute-start(bf16[48,128]{1,0:T(8,128)(2,1)S(1)} %get-tuple-element.30), channel_id=1, source_target_pairs={{0,1},{2,3},{1,0},{3,2},{4,5},{6,7},{5,4},{7,6},{8,9},{10,11},{9,8... | collective-permute-start | bytes 36872 | tf_op jit(solution)/shard_map/ppermute | solution.py:619
  9.6 1.6 %collective-permute-done.2.refs_7_ = bf16[48,128]{1,0:T(8,128)(2,1)S(1)} collective-permute-done((bf16[48,128]{1,0:T(8,128)(2,1)S(1)}, bf16[48,128]{1,0:T(8,128)(2,1)S(1)}, u32[]{:S(2)}, u32[]{:S(2)}) %collective-permute-start.2) | collective-permute-done | bytes 12320 | tf_op jit(solution)/shard_map/ppermute | solution.py:618
  11.2 0.0 collective-permute-done.3.refs_8_
  11.2 6.5 %forecast.1 = (bf16[1536,128]{1,0:T(8,128)(2,1)S(1)}, bf16[32,4,128]{2,1,0:T(4,128)(2,1)S(1)}) custom-call(s32[1,128]{1,0:T(1,128)S(1)} %get-tuple-element.21.refs_0_, s32[1,128]{1,0:T(1,128)S(1)} %get-tuple-element.22.refs_1_, bf16[5120,128]{1,0:T(8,128)(2,1)S(1)} %get-tuple-element.23.refs_2_, bf16[48,128]{1,0:T(8,128)(2,1)S(1)} %collective-permute-done.near_ref.refs_3_, ...), custom_call_target="tpu_custom_call" | custom-call | tf_op jit(solution)/shard_map/forecast/pallas_call | solution.py:428
  17.8 1.6 %collective-permute-start.4 = (bf16[1536,128]{1,0:T(8,128)(2,1)S(1)}, bf16[1536,128]{1,0:T(8,128)(2,1)S(1)}, u32[]{:S(2)}, u32[]{:S(2)}) collective-permute-start(bf16[1536,128]{1,0:T(8,128)(2,1)S(1)} %get-tuple-element.36.mine_ref), channel_id=1, source_target_pairs={{0,16},{16,0},{1,17},{17,1},{2,18},{18,2},{3,19},{19,3},{4,20},{20... | collective-permute-start | bytes 1179656 | tf_op jit(solution)/shard_map/ppermute | solution.py:637
  19.4 12.7 %all_to_all.5.told_ref = bf16[32,4,128]{2,1,0:T(4,128)(2,1)S(1)} all-to-all(bf16[32,4,128]{2,1,0:T(4,128)(2,1)S(1)} %get-tuple-element.35), channel_id=1, replica_groups=mesh['ens'=2,'lat'=4,'lon'=4] {'ens','lat','lon'}, dimensions={0} | all-to-all | bytes 65536 | tf_op jit(solution)/shard_map/all_to_all | solution.py:635
  32.0 0.0 collective-permute-done.4.other_ref
  32.0 1.3 %analysis.1 = bf16[24,64,128]{2,1,0:T(8,128)(2,1)} custom-call(bf16[32,4,128]{2,1,0:T(4,128)(2,1)S(1)} %all_to_all.5.told_ref, bf16[1536,128]{1,0:T(8,128)(2,1)S(1)} %get-tuple-element.36.mine_ref, bf16[1536,128]{1,0:T(8,128)(2,1)S(1)} %collective-permute-done.4.other_ref), custom_call_target="tpu_custom_call" | custom-call | tf_op jit(solution)/shard_map/analysis/pallas_call | solution.py:531
Async XLA Ops:
  1.0 6.8 %collective-permute-start = (bf16[48,128]{1,0:T(8,128)(2,1)S(1)}, bf16[48,128]{1,0:T(8,128)(2,1)S(1)}, u32[]{:S(2)}, u32[]{:S(2)}) collective-permute-start(bf16[48,128]{1,0:T(8,128)(2,1)S(1)} %get-tuple-element.24), channel_id=1, source_target_pairs={{0,4},{8,12},{4,0},{12,8},{1,5},{9,13},{5,1},{13,9},{2,6},{10,14},... | collective-permute-start | bytes 36872 | tf_op jit(solution)/shard_map/ppermute | solution.py:604
  4.1 3.7 %collective-permute-start.1 = (bf16[48,128]{1,0:T(8,128)(2,1)S(1)}, bf16[48,128]{1,0:T(8,128)(2,1)S(1)}, u32[]{:S(2)}, u32[]{:S(2)}) collective-permute-start(bf16[48,128]{1,0:T(8,128)(2,1)S(1)} %get-tuple-element.25), channel_id=1, source_target_pairs={{4,8},{8,4},{5,9},{9,5},{6,10},{10,6},{7,11},{11,7},{20,24},{24,20... | collective-permute-start | bytes 36872 | tf_op jit(solution)/shard_map/ppermute | solution.py:605
  8.0 3.3 %collective-permute-start.2 = (bf16[48,128]{1,0:T(8,128)(2,1)S(1)}, bf16[48,128]{1,0:T(8,128)(2,1)S(1)}, u32[]{:S(2)}, u32[]{:S(2)}) collective-permute-start(bf16[48,128]{1,0:T(8,128)(2,1)S(1)} %get-tuple-element.29), channel_id=1, source_target_pairs={{1,2},{3,0},{2,1},{0,3},{5,6},{7,4},{6,5},{4,7},{9,10},{11,8},{10,... | collective-permute-start | bytes 36872 | tf_op jit(solution)/shard_map/ppermute | solution.py:618
  8.7 2.6 %collective-permute-start.3 = (bf16[48,128]{1,0:T(8,128)(2,1)S(1)}, bf16[48,128]{1,0:T(8,128)(2,1)S(1)}, u32[]{:S(2)}, u32[]{:S(2)}) collective-permute-start(bf16[48,128]{1,0:T(8,128)(2,1)S(1)} %get-tuple-element.30), channel_id=1, source_target_pairs={{0,1},{2,3},{1,0},{3,2},{4,5},{6,7},{5,4},{7,6},{8,9},{10,11},{9,8... | collective-permute-start | bytes 36872 | tf_op jit(solution)/shard_map/ppermute | solution.py:619
  17.8 14.3 %collective-permute-start.4 = (bf16[1536,128]{1,0:T(8,128)(2,1)S(1)}, bf16[1536,128]{1,0:T(8,128)(2,1)S(1)}, u32[]{:S(2)}, u32[]{:S(2)}) collective-permute-start(bf16[1536,128]{1,0:T(8,128)(2,1)S(1)} %get-tuple-element.36.mine_ref), channel_id=1, source_target_pairs={{0,16},{16,0},{1,17},{17,1},{2,18},{18,2},{3,19},{19,3},{4,20},{20... | collective-permute-start | bytes 1179656 | tf_op jit(solution)/shard_map/ppermute | solution.py:637
